TPU v7x, 128 devices: a whole 4x4x4 slice. The times are simulated.
128 devices in a mesh: seq: 32 (over y, z, x_lo), rep: 2 (over x_hi), own: 2 (over core).
Axes of the slice: x: 4 (x_hi: 2, x_lo: 2; x = x_hi * 2 + x_lo), y: 4, z: 4, core: 2. Of those that a mesh axis runs over, the one named last changes fastest.
Arguments:
- latent: bfloat16 [4096, 8, 1280], P('seq', ('rep', 'own')), may hold values from -40 to 40
- cotangent: bfloat16 [4096, 8, 1280], P('seq', ('rep', 'own')), may hold values from -16 to 16
- norm_gain: float32 [1280], replicated, may hold values from 0.1 to 1.9
- norm_shift: float32 [1280], replicated, may hold values from -3 to 3
- proj_qkv: bfloat16 [1280, 3072], P('own'), may hold values from -1 to 1
- proj_out: bfloat16 [1024, 1280], P('own'), may hold values from -0.1875 to 0.1875
Outputs:
- mixed: bfloat16 [4096, 8, 1280], P('seq', ('rep', 'own'))
- grad_latent: bfloat16 [4096, 8, 1280], P('seq', ('rep', 'own'))
- grad_proj_qkv: float32 [1280, 3072], P(('seq', 'rep', 'own'))
- grad_proj_out: float32 [1024, 1280], P(('seq', 'rep', 'own'))
All inputs are finite; a program needn't handle non-finite values.
Results may differ from a plain program's by a relative error of at most 0.0055.
The roundings to bfloat16 on the way count: a program that leaves them out, or rounds other values in their place, can miss the bound.
Values may be sent and summed in bfloat16 or wider, within the bound.
A program may use at most 192 MiB of HBM per device.

v0:
```python
import jax
import jax.numpy as jnp
from jax import lax
from jax.sharding import PartitionSpec as P

HEADS = 16
HEAD = 64
GROUPS = 32


def joined_along(blocks, dim):
    blocks = jnp.moveaxis(blocks, 0, dim)
    lengths = blocks.shape
    return blocks.reshape(*lengths[:dim], lengths[dim] * lengths[dim + 1], *lengths[dim + 2 :])


def gather_together(arrays, axis, dims):
    line = jnp.concatenate([a.reshape(-1) for a in arrays])
    lines, at, done = (lax.all_gather(line, axis), 0, [])
    for a, dim in zip(arrays, dims):
        blocks = lines[:, at : at + a.size].reshape(-1, *a.shape)
        done.append(joined_along(blocks, dim))
        at += a.size
    return tuple(done)


def in_blocks(value, dim, count):
    lengths = value.shape
    blocks = value.reshape(*lengths[:dim], count, lengths[dim] // count, *lengths[dim + 1 :])
    return jnp.moveaxis(blocks, dim, 0)


def scatter_lines(value, axis, dim):
    count = lax.axis_size(axis)
    blocks = in_blocks(value, dim, count)
    lines = blocks.reshape(count, -1)
    extent = max(16, -(-lines.shape[1] // 1024) * 8)
    lines = jnp.pad(lines, ((0, 0), (0, extent * 128 - lines.shape[1]))).reshape(-1, 128)
    own = lax.psum_scatter(lines, axis, scatter_dimension=0, tiled=True)
    return own.reshape(-1)[: blocks[0].size].reshape(blocks.shape[1:])


def sent_to_all(value, axis):
    count = lax.axis_size(axis)
    return lax.all_to_all(
        jnp.broadcast_to(value[None], (count, *value.shape)), axis, 0, 0, tiled=True
    )


def taken_together(value, axis):
    return sent_to_all(value, axis).sum(axis=0)


def packed_total(arrays, axis):
    ends = [0]
    for a in arrays:
        ends.append(ends[-1] + a.size)
    total = taken_together(jnp.concatenate([a.ravel() for a in arrays]), axis)
    return tuple((total[b:e].reshape(a.shape) for a, b, e in zip(arrays, ends, ends[1:])))


def shards(latent, cotangent, norm_gain, norm_shift, proj_qkv, proj_out):
    local_len, images, channels = latent.shape
    seq_count = lax.axis_size("seq")
    per_group = channels // GROUPS
    inner_width = HEADS * HEAD
    score_scale = HEAD ** (-0.5)
    total_count = local_len * seq_count * per_group
    full_qkv, full_out = (
        lax.all_gather(proj_qkv, "own", axis=0, tiled=True),
        lax.all_gather(proj_out, "own", axis=0, tiled=True),
    )
    values = latent.astype(jnp.float32)
    grouped = values.reshape(local_len, images, GROUPS, per_group)
    first_sum, second_sum = lax.psum(
        (jnp.sum(grouped, axis=(0, 3)), jnp.sum(grouped * grouped, axis=(0, 3))), "seq"
    )
    group_mean = first_sum / total_count
    inv_std = lax.rsqrt(second_sum / total_count - group_mean * group_mean + 1e-06)
    centred = (grouped - group_mean[None, :, :, None]) * inv_std[None, :, :, None]
    normed = (centred.reshape(local_len, images, channels) * norm_gain + norm_shift).astype(
        jnp.bfloat16
    )
    normed_rows = normed.reshape(local_len * images, channels)
    projected = jnp.dot(normed_rows, full_qkv, preferred_element_type=jnp.float32).astype(
        jnp.bfloat16
    )
    projected = projected.reshape(local_len, images, 3, inner_width)
    query_tok = projected[:, :, 0].reshape(local_len, images * inner_width)
    key_tok = projected[:, :, 1].reshape(local_len, images * inner_width)
    value_tok = projected[:, :, 2].reshape(local_len, images * inner_width)
    query_heads, key_heads, value_heads = (
        lax.all_to_all(query_tok, "seq", split_axis=1, concat_axis=0, tiled=True),
        lax.all_to_all(key_tok, "seq", split_axis=1, concat_axis=0, tiled=True),
        lax.all_to_all(value_tok, "seq", split_axis=1, concat_axis=0, tiled=True),
    )
    full_len, head_cols = query_heads.shape
    pair_count = head_cols // HEAD
    query_heads = query_heads.reshape(full_len, pair_count, HEAD)
    key_heads = key_heads.reshape(full_len, pair_count, HEAD)
    value_heads = value_heads.reshape(full_len, pair_count, HEAD)
    block_len = min(512, full_len)
    block_count = full_len // block_len

    def probabilities(query_block):
        scores = (
            jnp.einsum("qhd,khd->hqk", query_block, key_heads, preferred_element_type=jnp.float32)
            * score_scale
        )
        row_max = jnp.max(scores, axis=-1, keepdims=True)
        weights = jnp.exp(scores - row_max)
        return weights / jnp.sum(weights, axis=-1, keepdims=True)

    def attend_block(query_block):
        probs_low = probabilities(query_block).astype(jnp.bfloat16)
        return jnp.einsum(
            "hqk,khd->qhd", probs_low, value_heads, preferred_element_type=jnp.float32
        ).astype(jnp.bfloat16)

    query_blocks = query_heads.reshape(block_count, block_len, pair_count, HEAD)
    attended_heads = lax.map(attend_block, query_blocks).reshape(full_len, head_cols)
    attended_tok = lax.all_to_all(attended_heads, "seq", split_axis=0, concat_axis=1, tiled=True)
    attended_rows = attended_tok.reshape(local_len * images, inner_width)
    mixed_out = (
        values
        + jnp.dot(attended_rows, full_out, preferred_element_type=jnp.float32).reshape(
            local_len, images, channels
        )
    ).astype(jnp.bfloat16)
    back_qkv, back_out = gather_together((proj_qkv, proj_out), "own", (0, 0))
    grad_rows = cotangent.reshape(local_len * images, channels)
    grad_attended = lax.dot_general(
        grad_rows, back_out, (((1,), (1,)), ((), ())), preferred_element_type=jnp.float32
    ).astype(jnp.bfloat16)
    grad_heads = lax.all_to_all(
        grad_attended.reshape(local_len, images * inner_width),
        "seq",
        split_axis=1,
        concat_axis=0,
        tiled=True,
    )
    grad_blocks = grad_heads.reshape(block_count, block_len, pair_count, HEAD)

    def backward_block(totals, operands):
        query_block, grad_block = operands
        probs_high = probabilities(query_block)
        probs_low = probs_high.astype(jnp.bfloat16)
        dprobs = jnp.einsum(
            "qhd,khd->hqk", grad_block, value_heads, preferred_element_type=jnp.float32
        )
        row_delta = jnp.sum(probs_high * dprobs, axis=-1, keepdims=True)
        dscores = (probs_high * (dprobs - row_delta) * score_scale).astype(jnp.bfloat16)
        grad_query = jnp.einsum(
            "hqk,khd->qhd", dscores, key_heads, preferred_element_type=jnp.float32
        ).astype(jnp.bfloat16)
        key_total = totals[0] + jnp.einsum(
            "hqk,qhd->khd", dscores, query_block, preferred_element_type=jnp.float32
        )
        value_total = totals[1] + jnp.einsum(
            "hqk,qhd->khd", probs_low, grad_block, preferred_element_type=jnp.float32
        )
        return ((key_total, value_total), grad_query)

    zeros_heads = jnp.zeros((full_len, pair_count, HEAD), jnp.float32)
    (key_total, value_total), grad_query = lax.scan(
        backward_block, (zeros_heads, zeros_heads), (query_blocks, grad_blocks)
    )
    grad_query = grad_query.reshape(full_len, head_cols)
    grad_key = key_total.astype(jnp.bfloat16).reshape(full_len, head_cols)
    grad_value = value_total.astype(jnp.bfloat16).reshape(full_len, head_cols)
    query_back, key_back, value_back = (
        lax.all_to_all(grad_query, "seq", split_axis=0, concat_axis=1, tiled=True),
        lax.all_to_all(grad_key, "seq", split_axis=0, concat_axis=1, tiled=True),
        lax.all_to_all(grad_value, "seq", split_axis=0, concat_axis=1, tiled=True),
    )
    grad_projected = jnp.stack(
        [
            query_back.reshape(local_len, images, inner_width),
            key_back.reshape(local_len, images, inner_width),
            value_back.reshape(local_len, images, inner_width),
        ],
        axis=2,
    )
    grad_projected = grad_projected.reshape(local_len * images, 3 * inner_width)
    grad_normed = lax.dot_general(
        grad_projected, back_qkv, (((1,), (1,)), ((), ())), preferred_element_type=jnp.float32
    )
    row_piece = normed_rows
    qkv_summed = lax.psum_scatter(
        lax.dot_general(
            row_piece, grad_projected, (((0,), (0,)), ((), ())), preferred_element_type=jnp.float32
        ),
        ("seq", "rep", "own"),
        scatter_dimension=0,
        tiled=True,
    )
    grad_centred = (grad_normed.reshape(local_len, images, channels) * norm_gain).reshape(
        local_len, images, GROUPS, per_group
    )
    sum_one, sum_two = packed_total(
        (jnp.sum(grad_centred, axis=(0, 3)), jnp.sum(grad_centred * centred, axis=(0, 3))), "seq"
    )
    mean_one = sum_one / total_count
    mean_two = sum_two / total_count
    grad_values = inv_std[None, :, :, None] * (
        grad_centred - mean_one[None, :, :, None] - centred * mean_two[None, :, :, None]
    )
    grad_latent = (
        cotangent.astype(jnp.float32) + grad_values.reshape(local_len, images, channels)
    ).astype(jnp.bfloat16)
    row_piece = attended_rows
    out_summed = scatter_lines(
        lax.dot_general(
            row_piece, grad_rows, (((0,), (0,)), ((), ())), preferred_element_type=jnp.float32
        ),
        ("seq", "rep", "own"),
        0,
    )
    return (mixed_out, grad_latent, qkv_summed, out_summed)


def solution(mesh):
    placed = (
        P("seq", ("rep", "own"), None),
        P("seq", ("rep", "own"), None),
        P(),
        P(),
        P("own", None),
        P("own", None),
    )
    return jax.shard_map(
        shards,
        mesh=mesh,
        in_specs=placed,
        out_specs=(
            P("seq", ("rep", "own"), None),
            P("seq", ("rep", "own"), None),
            P(("seq", "rep", "own"), None),
            P(("seq", "rep", "own"), None),
        ),
        check_vma=False,
    )
```

profile of v0, /device:TPU:1, one launch (start us, length us, event | category | flops | bytes accessed | tf_op | source)
XLA Modules:
  0.0 1123.2 jit_solution(13517986084234501598)
XLA Ops:
  14.2 18.7 %pad_maximum_fusion = bf16[2621440]{0:T(1024)(128)(2,1)} fusion(bf16[655360]{0:T(1024)(128)(2,1)S(1)} %reshape.249, bf16[1966080]{0:T(1024)(128)(2,1)S(1)} %bitcast.178), kind=kLoop, calls=%fused_computation.46 | loop fusion | flops 10485760 | bytes 10485760 | tf_op jit(solution)/shard_map/concatenate | solution.py:18
  34.5 71.6 %all-reduce.1 = (f32[2,32]{1,0:T(2,128)S(1)}, f32[2,32]{1,0:T(2,128)S(1)}) all-reduce(f32[2,32]{1,0:T(2,128)S(1)} %reduce_sum.105, f32[2,32]{1,0:T(2,128)S(1)} %reduce_sum.86), channel_id=1, replica_groups=mesh['seq'=32,'rep'=2,'own'=2] {'seq'}, use_global_device_ids=true, to_apply=%region_5.0 | all-reduce | flops 128 | bytes 1024 | tf_op jit(solution)/shard_map/psum | solution.py:75
  109.5 6.6 convolution_convert_fusion.1
  116.1 4.6 reshape.245
  134.8 6.3 all-to-all-done.2
  146.9 9.1 all-to-all-done.1
  161.8 8.0 all-to-all-done
  170.7 41.4 %while.25 = (s32[]{:T(128)}, bf16[8,512,1,64]{1,3,2,0:T(8,128)(2,1)S(1)}, bf16[8,512,1,64]{1,3,2,0:T(8,128)(2,1)S(1)}, bf16[4096,1,64]{0,2,1:T(8,128)(2,1)S(1)}, bf16[4096,1,64]{0,2,1:T(8,128)(2,1)S(1)}, /*index=5*/s32[]{:T(128)}) while((s32[]{:T(128)}, bf16[8,512,1,64]{1,3,2,0:T(8,128)(2,1)S(1)}, bf16[8,512,1,64]{1,3,2,0:T(8,128)(2,1)S(1)}, ...), condition=%wide.region_9.10_spmd, body=%wide.region_6.9_spmd.sunk | while | flops 555777024 | bytes 26355796 | solution.py:121
  214.5 5.1 all-to-all-start.3
  220.7 12.2 %reshape.257 = bf16[2,2621440]{1,0:T(2,128)(2,1)} reshape(bf16[5242880]{0:T(1024)(128)(2,1)} %all-gather.9.cloned.1.call-done) | data formatting | bytes 20971520 | tf_op jit(solution)/shard_map/all_gather | solution.py:19
  243.4 8.0 all-to-all-start.4
  254.6 4.4 fusion.57
  259.0 6.6 reshape.256
  268.4 136.2 %while.26 = (s32[]{:T(128)}, f32[4096,1,64]{0,2,1:T(8,128)S(1)}, f32[4096,1,64]{0,2,1:T(8,128)}, bf16[8,512,1,64]{1,3,2,0:T(8,128)(2,1)S(1)}, bf16[8,512,1,64]{1...) while((s32[]{:T(128)}, f32[4096,1,64]{0,2,1:T(8,128)S(1)}, ...), condition=%wide.region_14.15_spmd.clone, body=%wide.region_10.14_spmd.clone.sunk | while | flops 1387297280 | bytes 85809352 | solution.py:165
  406.3 7.6 all-to-all-start.5
  416.4 7.9 all-to-all-done.5
  428.6 9.4 all-to-all-done.7
  438.0 13.2 %all_to_all.134 = bf16[32,128,64]{1,2,0:T(8,128)(2,1)S(1)} all-to-all(bf16[32,128,64]{1,2,0:T(8,128)(2,1)S(1)} %copy.145), channel_id=1, replica_groups=mesh['seq'=32,'rep'=2,'own'=2] {'seq'}, dimensions={0} | all-to-all | bytes 1048576 | tf_op jit(solution)/shard_map/all_to_all | solution.py:173
  456.7 7.7 fusion.56
  464.5 7.9 slice.48
  472.4 14.1 %reshape.263 = bf16[1280,3072,1]{1,0,2:T(8,128)(2,1)} reshape(bf16[2,1966080]{1,0:T(2,128)(2,1)} %slice.48) | data formatting | bytes 15728640 | tf_op jit(solution)/shard_map/reshape;reshape | solution.py:14
  486.6 5.8 fusion.54
  507.8 424.2 %reduce-scatter.2.cloned.1.call-done = f32[80,128]{1,0:T(8,128)} async-done(((f32[10240,128]{1,0:T(8,128)}), f32[80,128]{1,0:T(8,128)}) %reduce-scatter.2.cloned.1.call-update) | async-done | bytes 40976 | tf_op jit(solution)/shard_map/reduce_scatter | solution.py:39
  933.4 181.1 %all-reduce.4.cloned.1.call-done = f32[1280,3072]{1,0:T(8,128)} async-done(((f32[1280,3072]{1,0:T(8,128)}), f32[1280,3072]{1,0:T(8,128)}) %all-reduce.4.cloned.1.call-update) | async-done | bytes 15728656
  (243 shorter events, 267.4 us)
Async XLA Ops:
  7.2 101.6 %all-gather.5.cloned.1.call-start = ((), (), s32[]{:S(2)}) async-start(), calls=%async_computation.10 | async-start | bytes 11796480 | tf_op jit(solution)/shard_map/all_gather | solution.py:70
  7.9 212.8 %all-gather.9.cloned.1.call-start = ((), (), s32[]{:S(2)}) async-start(), calls=%async_computation.13 | async-start | bytes 15728640 | tf_op jit(solution)/shard_map/all_gather | solution.py:19
  32.9 74.6 %copy-start.15 = (f32[1280]{0:T(1024)S(1)}, f32[1280]{0:T(1024)}, u32[]{:S(2)}) copy-start(f32[1280]{0:T(1024)} %param.13) | copy-start | bytes 15364
  32.9 74.6 %copy-start.16 = (f32[1280]{0:T(1024)S(1)}, f32[1280]{0:T(1024)}, u32[]{:S(2)}) copy-start(f32[1280]{0:T(1024)} %param.12) | copy-start | bytes 15364
  127.5 13.6 %all-to-all-start.2 = ((bf16[128,32,64]{0,2,1:T(8,128)(2,1)}), bf16[128,32,64]{0,2,1:T(8,128)(2,1)S(1)}, u32[]{:S(2)}, u32[]{:S(2)}) async-start(bf16[128,32,64]{0,2,1:T(8,128)(2,1)} %bitcast.11), calls=%async_computation.2 | async-start | bytes 1048576 | tf_op jit(solution)/shard_map/all_to_all | solution.py:95
  141.1 14.9 %all-to-all-start.1 = ((bf16[128,32,64]{0,2,1:T(8,128)(2,1)}), bf16[128,32,64]{0,2,1:T(8,128)(2,1)S(1)}, u32[]{:S(2)}, u32[]{:S(2)}) async-start(bf16[128,32,64]{0,2,1:T(8,128)(2,1)} %bitcast.9), calls=%async_computation.1 | async-start | bytes 1048576 | tf_op jit(solution)/shard_map/all_to_all | solution.py:94
  156.0 13.8 %all-to-all-start = ((bf16[128,32,64]{0,2,1:T(8,128)(2,1)}), bf16[128,32,64]{0,2,1:T(8,128)(2,1)S(1)}, u32[]{:S(2)}, u32[]{:S(2)}) async-start(bf16[128,32,64]{0,2,1:T(8,128)(2,1)} %bitcast.7), calls=%async_computation | async-start | bytes 1048576 | tf_op jit(solution)/shard_map/all_to_all | solution.py:93
  159.9 338.0 %all-gather.7.cloned.1.call-start = ((), (), s32[]{:S(2)}) async-start(), calls=%async_computation.11 | async-start | bytes 3932160 | tf_op jit(solution)/shard_map/all_gather | solution.py:71
  170.7 49.0 %copy-start.5 = (bf16[128,2,1280]{2,1,0:T(2,128)(2,1)S(1)}, bf16[128,2,1280]{2,1,0:T(2,128)(2,1)}, u32[]{:S(2)}) copy-start(bf16[128,2,1280]{2,1,0:T(2,128)(2,1)} %param.11) | copy-start | bytes 1966084
  212.9 7.8 copy-start.2
  214.5 28.8 %all-to-all-start.3 = ((bf16[32,128,64]{1,2,0:T(8,128)(2,1)}), bf16[32,128,64]{1,2,0:T(8,128)(2,1)}, u32[]{:S(2)}, u32[]{:S(2)}) async-start(bf16[32,128,64]{1,2,0:T(8,128)(2,1)} %copy.135), calls=%async_computation.3 | async-start | bytes 1048576 | tf_op jit(solution)/shard_map/all_to_all | solution.py:122
  243.4 22.3 %all-to-all-start.4 = ((bf16[128,32,64]{0,2,1:T(8,128)(2,1)}), bf16[128,32,64]{0,2,1:T(8,128)(2,1)}, u32[]{:S(2)}, u32[]{:S(2)}) async-start(bf16[128,32,64]{0,2,1:T(8,128)(2,1)} %copy.139), calls=%async_computation.4 | async-start | bytes 1048576 | tf_op jit(solution)/shard_map/all_to_all | solution.py:135
  251.4 680.7 %reduce-scatter.2.cloned.1.call-start = ((), (), s32[]{:S(2)}) async-start(), calls=%async_computation.12 | async-start | bytes 5283840 | tf_op jit(solution)/shard_map/reduce_scatter | solution.py:39
  275.1 3.4 copy-start.8
  292.1 3.4 copy-start.8
  406.3 18.0 %all-to-all-start.5 = ((bf16[32,128,64]{1,2,0:T(8,128)(2,1)}), bf16[32,128,64]{1,2,0:T(8,128)(2,1)S(1)}, u32[]{:S(2)}, u32[]{:S(2)}) async-start(bf16[32,128,64]{1,2,0:T(8,128)(2,1)} %copy.144), calls=%async_computation.5 | async-start | bytes 1048576 | tf_op jit(solution)/shard_map/all_to_all | solution.py:172
  424.3 13.7 %all-to-all-start.7 = ((bf16[32,128,64]{1,2,0:T(8,128)(2,1)}), bf16[32,128,64]{1,2,0:T(8,128)(2,1)S(1)}, u32[]{:S(2)}, u32[]{:S(2)}) async-start(bf16[32,128,64]{1,2,0:T(8,128)(2,1)} %copy.146), calls=%async_computation.7 | async-start | bytes 1048576 | tf_op jit(solution)/shard_map/all_to_all | solution.py:174
  428.2 686.3 %all-reduce.4.cloned.1.call-start = ((), (), s32[]{:S(2)}) async-start(), calls=%async_computation.14 | async-start | bytes 31457280
  451.2 5.5 copy-start.4
  472.4 14.2 %copy-start.1 = (bf16[128,2,1280]{2,1,0:T(2,128)(2,1)S(1)}, bf16[128,2,1280]{2,1,0:T(2,128)(2,1)}, u32[]{:S(2)}) copy-start(bf16[128,2,1280]{2,1,0:T(2,128)(2,1)} %param.10) | copy-start | bytes 1966084
  472.4 14.2 %copy-start.12 = (f32[2,1280]{1,0:T(2,128)S(1)}, f32[2,1280]{1,0:T(2,128)}, u32[]{:S(2)}) copy-start(f32[2,1280]{1,0:T(2,128)} %copy-done.11) | copy-start | bytes 30724
  492.5 13.4 %copy-start.6 = (bf16[128,2,1280]{2,1,0:T(2,128)(2,1)S(1)}, bf16[128,2,1280]{2,1,0:T(2,128)(2,1)}, u32[]{:S(2)}) copy-start(bf16[128,2,1280]{2,1,0:T(2,128)(2,1)} %param.11) | copy-start | bytes 1966084
  492.5 13.4 %copy-start.14 = (f32[2,1280]{1,0:T(2,128)S(1)}, f32[2,1280]{1,0:T(2,128)}, u32[]{:S(2)}) copy-start(f32[2,1280]{1,0:T(2,128)} %copy-done.13) | copy-start | bytes 30724
  493.7 11.5 %all-to-all-start.8 = ((f32[32,1,128]{2,1,0:T(1,128)}), f32[32,1,128]{2,1,0:T(1,128)S(1)}, u32[]{:S(2)}, u32[]{:S(2)}) async-start(f32[32,1,128]{2,1,0:T(1,128)} %broadcast_in_dim.17), calls=%async_computation.8 | async-start | bytes 32768 | tf_op jit(solution)/shard_map/all_to_all | solution.py:45
  (21 other events, 40.9 us)
Sparse Core Ops, SparseCore 0:
  9.6 25.3 all-gather.4
  36.7 26.6 all-gather.8
  162.3 31.8 all-gather.6
  265.8 666.2 reduce-scatter.1
  936.9 177.6 all-reduce.3
where the time goes:
time: 1130 us; the launch traced here: 1120 us
  waiting for transfers between devices  650 us (58%)
  matrix products  153 us (14%)
  local copies, waits for them, and re-layouts  103 us (9%)
  blocking collectives  84.8 us (8%)
  other arithmetic  75.1 us (7%)
  starting transfers between devices  40.8 us (4%)
  between operations  14.8 us (1%)
    reduce_scatter x1, waiting for transfers between devices, scatter_lines(): own = lax.psum_scatter(lines, axis, scatter_dimension=0, tiled=True)  424 us
    unnamed x6, waiting for transfers between devices  182 us
    psum x1, blocking collectives, shards(): lax.psum((jnp.sum(grouped, axis=(0, 3)), jnp.sum(grouped * grouped, axis=...  71.6 us
    convert_element_type x8, other arithmetic, backward_block(): (probs_high * (dprobs - row_delta) * score_scale).astype(jnp.bfloat16)  29.5 us
    dot_general x16, matrix products, probabilities(): jnp.einsum('qhd,khd->hqk', query_block, key_heads, preferred_element_type...  28.6 us
    dot_general x8, matrix products, backward_block(): jnp.einsum('qhd,khd->hqk', grad_block, value_heads, preferred_element_typ...  27 us
    reduce_sum x16, other arithmetic, probabilities(): return weights / jnp.sum(weights, axis=-1, keepdims=True)  24 us
    dot_general x8, matrix products, backward_block(): jnp.einsum('hqk,qhd->khd', probs_low, grad_block, preferred_element_type=...  23.5 us
  transfers between devices with their start and end apart: 13, of which 8 were waited for; matrix products, arithmetic and copies ran while one was open for 29% of the time, Pallas kernels for 0%

commit v1 on v0

v1 whole, which is shorter than its diff:
```python
import functools

import jax
import jax.numpy as jnp
from jax import lax
from jax.experimental import pallas as pl
from jax.experimental.pallas import tpu as pltpu
from jax.sharding import Mesh
from jax.sharding import PartitionSpec as P

HEADS = 16
HEAD = 64
GROUPS = 32
SCALE = HEAD ** (-0.5)
SEQ = ("y", "z", "xl")
LINE = ("y", "z", "xl", "rep")
ALL = ("y", "z", "xl", "rep", "own")
F32, BF16 = jnp.float32, jnp.bfloat16
VMEM = 60 << 20


def members(channels):
    channel = lax.broadcasted_iota(jnp.int32, (channels, 128), 0)
    group = lax.broadcasted_iota(jnp.int32, (channels, 128), 1)
    first = group * (channels // GROUPS)
    return ((channel >= first) & (channel < first + channels // GROUPS)).astype(F32)


def by_group(rows, table):
    return lax.dot_general(
        rows, table, (((1,), (0,)), ((), ())),
        precision=lax.Precision.HIGHEST, preferred_element_type=F32,
    )


def by_channel(rows, table):
    return lax.dot_general(
        rows, table, (((1,), (1,)), ((), ())),
        precision=lax.Precision.HIGHEST, preferred_element_type=F32,
    )


def four_rows(rows):
    width = rows[0].shape[1]
    return jnp.concatenate([*rows, jnp.zeros((4, width), F32)], axis=0)


def stats_kernel(lat_ref, out_ref):
    rows = []
    values = [lat_ref[i].astype(F32) for i in range(2)]
    rows = [jnp.sum(v, axis=0, keepdims=True) for v in values]
    rows += [jnp.sum(v * v, axis=0, keepdims=True) for v in values]
    out_ref[...] = by_group(four_rows(rows), members(lat_ref.shape[2]))


def stats(lat):
    return pl.pallas_call(
        stats_kernel,
        out_shape=jax.ShapeDtypeStruct((8, 128), F32),
        compiler_params=pltpu.CompilerParams(vmem_limit_bytes=VMEM),
        cost_estimate=pl.CostEstimate(flops=1 << 20, bytes_accessed=lat.size * 2, transcendentals=0),
    )(lat)


def moments(sums, count):
    means = sums / count
    var = means[2:4] - means[0:2] * means[0:2]
    return jnp.concatenate([means[0:2], lax.rsqrt(var + 1e-06), jnp.zeros((4, 128), F32)], axis=0)


def project_kernel(count, own_ref, lat_ref, sums_ref, gain_ref, shift_ref, *refs):
    mine, other = refs[0:3], refs[3:6]
    out_ref, chan_ref, normed_ref = refs[6:]
    own = own_ref[0]
    half = mine[0].shape[0]

    @pl.when(pl.program_id(0) == 0)
    def _():
        table = members(lat_ref.shape[2])
        chan = by_channel(moments(jnp.sum(sums_ref[...], axis=0), count), table)
        chan_ref[...] = chan
        for i in range(2):
            centred = (lat_ref[i].astype(F32) - chan[i : i + 1]) * chan[2 + i : 3 + i]
            normed_ref[i * 128 : (i + 1) * 128] = (centred * gain_ref[...] + shift_ref[...]).astype(BF16)

    near = normed_ref[:, pl.ds(pl.multiple_of(own * half, 128), half)]
    far = normed_ref[:, pl.ds(pl.multiple_of((1 - own) * half, 128), half)]
    query, key, value = [
        jnp.dot(near, a[...], preferred_element_type=F32) + jnp.dot(far, b[...], preferred_element_type=F32)
        for a, b in zip(mine, other)
    ]
    low = lax.broadcasted_iota(jnp.int32, (128, 128), 1) < HEAD
    for h in range(0, query.shape[1] // HEAD, 2):
        for i in range(2):
            rows, lanes = slice(i * 128, (i + 1) * 128), slice(h * HEAD, (h + 2) * HEAD)
            q, k, v = query[rows, lanes], key[rows, lanes], value[rows, lanes]
            k_roll, v_roll = pltpu.roll(k, HEAD, 1), pltpu.roll(v, HEAD, 1)
            out_ref[h, i, :128] = jnp.where(low, k, v_roll).astype(BF16)
            out_ref[h + 1, i, :128] = jnp.where(low, k_roll, v).astype(BF16)
            first, second = q[:64], q[64:]
            out_ref[h, i, 128:] = jnp.where(low[:64], first, pltpu.roll(second, HEAD, 1)).astype(BF16)
            out_ref[h + 1, i, 128:] = jnp.where(low[:64], pltpu.roll(first, HEAD, 1), second).astype(BF16)


def project(own, lat, sums, gain, shift, mine, other, count):
    channels = lat.shape[2]
    cols, half = HEADS * HEAD // 256, mine.shape[0]

    def weight(part):
        return pl.BlockSpec((half, 256), lambda s, own: (0, part * cols + s))

    def whole(*shape):
        return pl.BlockSpec(shape, lambda s, own: (0,) * len(shape))

    return pl.pallas_call(
        functools.partial(project_kernel, count),
        grid_spec=pltpu.PrefetchScalarGridSpec(
            num_scalar_prefetch=1,
            grid=(cols,),
            in_specs=[whole(*lat.shape), whole(*sums.shape), whole(1, channels), whole(1, channels)]
            + [weight(p) for p in range(3)] * 2,
            out_specs=[pl.BlockSpec((4, 2, 192, 128), lambda s, own: (s, 0, 0, 0)), whole(8, channels)],
            scratch_shapes=[pltpu.VMEM((256, channels), BF16)],
        ),
        out_shape=[
            jax.ShapeDtypeStruct((HEADS, 2, 192, 128), BF16),
            jax.ShapeDtypeStruct((8, channels), F32),
        ],
        compiler_params=pltpu.CompilerParams(vmem_limit_bytes=VMEM),
        cost_estimate=pl.CostEstimate(flops=2 * 256 * 1280 * 3072, bytes_accessed=12 << 20, transcendentals=0),
    )(own, lat, sums, gain, shift, mine, mine, mine, other, other, other)


def attended_grad_kernel(own_ref, cot_ref, w_ref, out_ref):
    rows = cot_ref[...].reshape(256, cot_ref.shape[2])
    grad = lax.dot_general(rows, w_ref[...], (((1,), (1,)), ((), ())), preferred_element_type=F32)
    low = lax.broadcasted_iota(jnp.int32, (64, 128), 1) < HEAD
    for h in range(0, grad.shape[1] // HEAD, 2):
        for i in range(2):
            first = grad[i * 128 : i * 128 + 64, h * HEAD : (h + 2) * HEAD]
            second = grad[i * 128 + 64 : (i + 1) * 128, h * HEAD : (h + 2) * HEAD]
            out_ref[h, i] = jnp.where(low, first, pltpu.roll(second, HEAD, 1)).astype(BF16)
            out_ref[h + 1, i] = jnp.where(low, pltpu.roll(first, HEAD, 1), second).astype(BF16)


def attended_grad(own, cot, halves):
    channels = cot.shape[2]
    per = halves.shape[1] // 256

    return pl.pallas_call(
        attended_grad_kernel,
        grid_spec=pltpu.PrefetchScalarGridSpec(
            num_scalar_prefetch=1,
            grid=(2 * per,),
            in_specs=[
                pl.BlockSpec(cot.shape, lambda s, own: (0, 0, 0)),
                pl.BlockSpec((None, 256, channels), lambda s, own: (s // per, s % per, 0)),
            ],
            out_specs=pl.BlockSpec(
                (4, 2, 64, 128),
                lambda s, own: ((s // per + own[0] - 2 * own[0] * (s // per)) * per + s % per, 0, 0, 0),
            ),
        ),
        out_shape=jax.ShapeDtypeStruct((HEADS, 2, 64, 128), BF16),
        compiler_params=pltpu.CompilerParams(vmem_limit_bytes=VMEM),
        cost_estimate=pl.CostEstimate(flops=2 * 256 * 1280 * 1024, bytes_accessed=4 << 20, transcendentals=0),
    )(own, cot, halves)


def attention_kernel(ck, kvq_ref, g_ref, dqo_ref, dkv_ref, s_ref, x_ref, y_ref, acc_ref):
    step, last = pl.program_id(0), pl.num_programs(0) - 1
    sources, _, width = kvq_ref.shape
    keys = sources * 128
    here = dqo_ref.shape[0]
    rows = here * 128
    half = rows // 2

    @pl.when(step == 0)
    def _():
        acc_ref[...] = jnp.zeros_like(acc_ref)

    low = lax.broadcasted_iota(jnp.int32, (half, width), 1) < HEAD
    xq = kvq_ref[pl.ds(step * here, here), 128:192, :].reshape(half, width).astype(F32) * SCALE
    xg = g_ref[pl.ds(step * here, here), :, :].reshape(half, width).astype(F32)
    zero = jnp.zeros_like(xq)
    y_ref[0 * half : 1 * half] = jnp.where(low, xq, zero).astype(BF16)
    y_ref[1 * half : 2 * half] = jnp.where(low, pltpu.roll(xq, HEAD, 1), zero).astype(BF16)
    y_ref[2 * half : 3 * half] = jnp.where(low, zero, pltpu.roll(xg, HEAD, 1)).astype(BF16)
    y_ref[3 * half : 4 * half] = jnp.where(low, zero, xg).astype(BF16)
    y = y_ref[...]
    spans = [(c, c + ck) for c in range(0, keys, ck)]

    def kv_chunk(a, b):
        return kvq_ref[a // 128 : b // 128, :128, :].reshape(b - a, width)

    top = None
    for a, b in spans:
        both = lax.dot_general(y, kv_chunk(a, b), (((1,), (1,)), ((), ())), preferred_element_type=F32)
        s_ref[:, a:b] = both
        for t in range(0, ck, 128):
            piece = both[:rows, t : t + 128]
            top = piece if top is None else jnp.maximum(top, piece)
    top = jnp.max(top, axis=1, keepdims=True)
    total = jnp.zeros((rows, 128), F32)
    delta = jnp.zeros((rows, 128), F32)
    for a, b in spans:
        weights = jnp.exp(s_ref[:rows, a:b] - top)
        s_ref[:rows, a:b] = weights
        fold = weights * s_ref[rows:, a:b]
        for t in range(0, ck, 128):
            total = total + weights[:, t : t + 128]
            delta = delta + fold[:, t : t + 128]
    inverse = 1.0 / jnp.sum(total, axis=1, keepdims=True)
    delta = jnp.sum(delta, axis=1, keepdims=True) * inverse
    out = jnp.zeros((2 * rows, width), F32)
    for a, b in spans:
        probs = s_ref[:rows, a:b] * inverse
        x_ref[rows:, a:b] = probs.astype(BF16)
        x_ref[:rows, a:b] = (probs * (s_ref[rows:, a:b] - delta)).astype(BF16)
        x = x_ref[:, a:b]
        out = out + jnp.dot(x, kv_chunk(a, b), preferred_element_type=F32)
        acc_ref[a:b, :] += lax.dot_general(x, y, (((0,), (0,)), ((), ())), preferred_element_type=F32)
    lows = lax.broadcasted_iota(jnp.int32, (rows, width), 1) < HEAD
    res = jnp.where(lows, out[:rows] * SCALE, out[rows:]).astype(BF16)
    for h in range(2):
        for a in range(here):
            at = h * half + a * 64
            dqo_ref[a, h * 64 : (h + 1) * 64, :] = res[at : at + 64]

    @pl.when(step == last)
    def _():
        dkv_ref[...] = acc_ref[...].reshape(sources, 128, width).astype(BF16)


def attention(kvq, g, here=2, ck=1024):
    sources = kvq.shape[0]
    keys, rows = sources * 128, here * 128
    return pl.pallas_call(
        functools.partial(attention_kernel, ck),
        grid=(sources // here,),
        in_specs=[
            pl.BlockSpec((sources, 192, 128), lambda i: (0, 0, 0), pipeline_mode=pl.Buffered(1)),
            pl.BlockSpec((sources, 64, 128), lambda i: (0, 0, 0), pipeline_mode=pl.Buffered(1)),
        ],
        out_specs=[
            pl.BlockSpec((here, 128, 128), lambda i: (i, 0, 0)),
            pl.BlockSpec((sources, 128, 128), lambda i: (0, 0, 0)),
        ],
        out_shape=[
            jax.ShapeDtypeStruct((sources, 128, 128), BF16),
            jax.ShapeDtypeStruct((sources, 128, 128), BF16),
        ],
        scratch_shapes=[
            pltpu.VMEM((2 * rows, keys), F32),
            pltpu.VMEM((2 * rows, keys), BF16),
            pltpu.VMEM((2 * rows, 128), BF16),
            pltpu.VMEM((keys, 128), F32),
        ],
        compiler_params=pltpu.CompilerParams(vmem_limit_bytes=VMEM),
        cost_estimate=pl.CostEstimate(flops=48 * keys * keys * HEAD, bytes_accessed=4 << 20, transcendentals=keys * keys),
    )(kvq, g)


def in_weight_kernel(lat_ref, chan_ref, gain_ref, shift_ref, dqo_ref, dkv_ref, out_ref, acc_ref, turned_ref):
    step, last = pl.program_id(0), pl.num_programs(0) - 1
    sources, _, channels = lat_ref.shape
    rows = sources * 128

    @pl.when(step == 0)
    def _():
        acc_ref[...] = jnp.zeros_like(acc_ref)

    lat = lat_ref[...].reshape(rows, channels).astype(F32)
    centred = (lat - chan_ref[0:1]) * chan_ref[1:2]
    normed = (centred * gain_ref[...] + shift_ref[...]).astype(BF16)
    grads = jnp.concatenate(
        [dqo_ref[...].reshape(rows, 128), dkv_ref[...].reshape(rows, 128)], axis=1
    )
    acc_ref[...] += lax.dot_general(grads, normed, (((0,), (0,)), ((), ())), preferred_element_type=F32)

    @pl.when(step == last)
    def _():
        turned_ref[...] = acc_ref[...].T
        low = lax.broadcasted_iota(jnp.int32, (5, 128), 1) < HEAD
        for d in range(channels // 10):
            at = d * 10
            out_ref[d, 0:10] = turned_ref[at : at + 10, 128:256]
            first, second = turned_ref[at : at + 5, 0:128], turned_ref[at + 5 : at + 10, 0:128]
            out_ref[d, 10:15] = jnp.where(low, first, pltpu.roll(second, HEAD, 1))
            out_ref[d, 15:16] = jnp.zeros((1, 128), F32)


def in_weight(lat, chan, gain, shift, dqo, dkv, here=4):
    sources, _, channels = lat.shape
    return pl.pallas_call(
        in_weight_kernel,
        grid=(sources // here,),
        in_specs=[
            pl.BlockSpec((here, 128, channels), lambda i: (i, 0, 0)),
            pl.BlockSpec((2, channels), lambda i: (0, 0)),
            pl.BlockSpec((1, channels), lambda i: (0, 0)),
            pl.BlockSpec((1, channels), lambda i: (0, 0)),
            pl.BlockSpec((here, 128, 128), lambda i: (i, 0, 0)),
            pl.BlockSpec((here, 128, 128), lambda i: (i, 0, 0)),
        ],
        out_specs=pl.BlockSpec((channels // 10, 16, 128), lambda i: (0, 0, 0)),
        out_shape=jax.ShapeDtypeStruct((channels // 10, 16, 128), F32),
        scratch_shapes=[pltpu.VMEM((256, channels), F32), pltpu.VMEM((channels, 256), F32)],
        compiler_params=pltpu.CompilerParams(vmem_limit_bytes=VMEM),
        cost_estimate=pl.CostEstimate(flops=2 * 4096 * 1280 * 256, bytes_accessed=14 << 20, transcendentals=0),
    )(lat, chan, gain, shift, dqo, dkv)


def paired(first, second, low, upper):
    if upper:
        return jnp.where(low, pltpu.roll(first.astype(F32), HEAD, 1), second.astype(F32)).astype(BF16)
    return jnp.where(low, first.astype(F32), pltpu.roll(second.astype(F32), HEAD, 1)).astype(BF16)


def mixed_kernel(own_ref, dqo_ref, lat_ref, w_ref, mixed_ref, att_ref):
    half = w_ref.shape[1]
    low = lax.broadcasted_iota(jnp.int32, (128, 128), 1) < HEAD
    for h in range(0, HEADS, 2):
        for i in range(2):
            att_ref[i, :, h * HEAD : (h + 2) * HEAD] = paired(dqo_ref[h, i], dqo_ref[h + 1, i], low, True)
    own = own_ref[0]
    for i in range(2):
        near = att_ref[i, :, pl.ds(pl.multiple_of(own * half, 128), half)]
        far = att_ref[i, :, pl.ds(pl.multiple_of((1 - own) * half, 128), half)]
        total = jnp.dot(near, w_ref[0], preferred_element_type=F32)
        total = total + jnp.dot(far, w_ref[1], preferred_element_type=F32)
        mixed_ref[i] = (lat_ref[i].astype(F32) + total).astype(BF16)


def mix(own, dqo, lat, halves):
    channels = lat.shape[2]

    def whole(*shape):
        return pl.BlockSpec(shape, lambda s, own: (0,) * len(shape))

    return pl.pallas_call(
        mixed_kernel,
        grid_spec=pltpu.PrefetchScalarGridSpec(
            num_scalar_prefetch=1,
            grid=(1,),
            in_specs=[whole(*dqo.shape), whole(*lat.shape), whole(*halves.shape)],
            out_specs=[whole(*lat.shape), whole(2, 128, HEADS * HEAD)],
        ),
        out_shape=[
            jax.ShapeDtypeStruct(lat.shape, BF16),
            jax.ShapeDtypeStruct((2, 128, HEADS * HEAD), BF16),
        ],
        compiler_params=pltpu.CompilerParams(vmem_limit_bytes=VMEM),
        cost_estimate=pl.CostEstimate(flops=2 * 256 * 1280 * 1024, bytes_accessed=6 << 20, transcendentals=0),
    )(own, dqo, lat, halves)


def out_weight_kernel(own_ref, att_ref, att_far_ref, cot_ref, cot_far_ref, out_ref):
    channels = cot_ref.shape[2]
    wide = att_ref.shape[2]
    att = jnp.concatenate([att_ref[...].reshape(256, wide), att_far_ref[...].reshape(256, wide)], axis=0)
    cot = jnp.concatenate([cot_ref[...].reshape(256, channels), cot_far_ref[...].reshape(256, channels)], axis=0)
    total = lax.dot_general(att, cot, (((0,), (0,)), ((), ())), preferred_element_type=F32)
    blocks = total.reshape(wide // 16, 2, 8, channels)
    own = own_ref[0]
    out_ref[...] = jnp.where(own == 0, blocks[:, 0], blocks[:, 1])


def out_weight(own, att, att_far, cot, cot_far):
    channels, wide = cot.shape[2], att.shape[2]
    tile = 256
    side = pl.BlockSpec((2, 128, tile), lambda s, own: (0, 0, s))
    full = pl.BlockSpec(cot.shape, lambda s, own: (0, 0, 0))
    return pl.pallas_call(
        out_weight_kernel,
        grid_spec=pltpu.PrefetchScalarGridSpec(
            num_scalar_prefetch=1,
            grid=(wide // tile,),
            in_specs=[side, side, full, full],
            out_specs=pl.BlockSpec((tile // 16, 8, channels), lambda s, own: (s, 0, 0)),
        ),
        out_shape=jax.ShapeDtypeStruct((wide // 16, 8, channels), F32),
        compiler_params=pltpu.CompilerParams(vmem_limit_bytes=VMEM),
        cost_estimate=pl.CostEstimate(flops=4 * 256 * 1280 * 1024, bytes_accessed=6 << 20, transcendentals=0),
    )(own, att, att_far, cot, cot_far)


def back_kernel(own_ref, dqo_ref, dkv_ref, mine_ref, other_ref, lat_ref, chan_ref, gain_ref, grad_ref, sums_ref, rows_ref):
    own = own_ref[0]
    inner, half = HEADS * HEAD, mine_ref.shape[0]
    low = lax.broadcasted_iota(jnp.int32, (128, 128), 1) < HEAD
    for h in range(0, HEADS, 2):
        for i in range(2):
            rows, at = slice(i * 128, (i + 1) * 128), h * HEAD
            dq, dk = (dqo_ref[h, i], dqo_ref[h + 1, i]), (dkv_ref[h, i], dkv_ref[h + 1, i])
            rows_ref[rows, at : at + 128] = paired(*dq, low, False)
            rows_ref[rows, inner + at : inner + at + 128] = paired(*dk, low, False)
            rows_ref[rows, 2 * inner + at : 2 * inner + at + 128] = paired(*dk, low, True)
    grads = rows_ref[...]
    for side, w_ref in ((own, mine_ref), (1 - own, other_ref)):
        part = lax.dot_general(grads, w_ref[...], (((1,), (1,)), ((), ())), preferred_element_type=F32)
        lanes = pl.ds(pl.multiple_of(side * half, 128), half)
        for i in range(2):
            grad_ref[i, :, lanes] = part[i * 128 : (i + 1) * 128]
    ones, twos = [], []
    for i in range(2):
        grad = grad_ref[i] * gain_ref[...]
        grad_ref[i] = grad
        centred = (lat_ref[i].astype(F32) - chan_ref[i : i + 1]) * chan_ref[2 + i : 3 + i]
        ones.append(jnp.sum(grad, axis=0, keepdims=True))
        twos.append(jnp.sum(grad * centred, axis=0, keepdims=True))
    sums_ref[...] = by_group(four_rows(ones + twos), members(lat_ref.shape[2]))


def back(own, dqo, dkv, mine, other, lat, chan, gain):
    def whole(shape):
        return pl.BlockSpec(shape, lambda s, own: (0,) * len(shape), pipeline_mode=pl.Buffered(1))

    operands = (dqo, dkv, mine, other, lat, chan, gain)
    return pl.pallas_call(
        back_kernel,
        grid_spec=pltpu.PrefetchScalarGridSpec(
            num_scalar_prefetch=1,
            grid=(1,),
            in_specs=[whole(a.shape) for a in operands],
            out_specs=[whole(lat.shape), whole((8, 128))],
            scratch_shapes=[pltpu.VMEM((256, 3 * HEADS * HEAD), BF16)],
        ),
        out_shape=[jax.ShapeDtypeStruct(lat.shape, F32), jax.ShapeDtypeStruct((8, 128), F32)],
        compiler_params=pltpu.CompilerParams(vmem_limit_bytes=VMEM),
        cost_estimate=pl.CostEstimate(flops=2 * 256 * 1280 * 3072, bytes_accessed=14 << 20, transcendentals=0),
    )(own, *operands)


def final_kernel(count, grad_ref, sums_ref, lat_ref, cot_ref, chan_ref, out_ref):
    table = members(lat_ref.shape[2])
    means = by_channel(jnp.sum(sums_ref[...], axis=0) / count, table)
    for i in range(2):
        inv = chan_ref[2 + i : 3 + i]
        centred = (lat_ref[i].astype(F32) - chan_ref[i : i + 1]) * inv
        grad = inv * (grad_ref[i] - means[i : i + 1] - centred * means[2 + i : 3 + i])
        out_ref[i] = (cot_ref[i].astype(F32) + grad).astype(BF16)


def final(grad, sums, lat, cot, chan, count):
    return pl.pallas_call(
        functools.partial(final_kernel, count),
        out_shape=jax.ShapeDtypeStruct(lat.shape, BF16),
        compiler_params=pltpu.CompilerParams(vmem_limit_bytes=VMEM),
        cost_estimate=pl.CostEstimate(flops=4 << 20, bytes_accessed=4 << 20, transcendentals=0),
    )(grad, sums, lat, cot, chan)


def swapped(value, axis):
    return lax.ppermute(value, axis, [(0, 1), (1, 0)])


def exchanged(value, axes):
    return lax.all_to_all(value, axes, 0, 0, tiled=True)


def shared(value, axes):
    return exchanged(jnp.broadcast_to(value[None], (lax.axis_size(axes), *value.shape)), axes)


def shards(latent, cotangent, norm_gain, norm_shift, proj_qkv, proj_out):
    local_len, images, channels = latent.shape
    seq_count = lax.axis_size(SEQ)
    count = local_len * seq_count * (channels // GROUPS)
    own = lax.axis_index("own").reshape(1)
    gain, shift = norm_gain.reshape(1, channels), norm_shift.reshape(1, channels)

    other_out = swapped(proj_out, "own")
    other_qkv = swapped(proj_qkv, "own")
    lat, cot = latent.transpose(1, 0, 2), cotangent.transpose(1, 0, 2)
    image_lat = lax.all_gather(exchanged(lat, "xl"), ("y", "z"), tiled=True)
    sums = shared(stats(lat), SEQ)
    halves_out = jnp.stack([proj_out, other_out])
    cot_far = swapped(cot, "own")
    g_send = attended_grad(own, cot, halves_out)
    g = exchanged(g_send.reshape(seq_count, 64, 128), SEQ)
    kvq_send, chan = project(own, lat, sums, gain, shift, proj_qkv, other_qkv, count)
    kvq = exchanged(kvq_send.reshape(seq_count, 192, 128), SEQ)

    dqo, dkv = attention(kvq, g)

    dqo_tok = exchanged(dqo, SEQ).reshape(HEADS, images, 128, 128)
    dkv_tok = exchanged(dkv, SEQ).reshape(HEADS, images, 128, 128)
    image = lax.axis_index("xl")
    chan_image = lax.dynamic_slice_in_dim(chan[:4].reshape(2, 2, channels), image, 1, 1).reshape(2, channels)
    in_part = in_weight(image_lat, chan_image, gain, shift, dqo, dkv)
    mixed, att = mix(own, dqo_tok, lat, halves_out)
    out_part = out_weight(own, att, swapped(att, "own"), cot, cot_far)
    out_blocks = exchanged(out_part, LINE)
    in_blocks = exchanged(in_part, ALL)
    grad, back_sums = back(own, dqo_tok, dkv_tok, proj_qkv, other_qkv, lat, chan, gain)
    grad_latent = final(grad, shared(back_sums, SEQ), lat, cot, chan, count)

    grad_out = jnp.sum(out_blocks, axis=0)
    summed = jnp.sum(in_blocks.reshape(HEADS, 8, 16, 128), axis=1)
    dq = summed[:, 10:15].reshape(HEADS, 5, 2, HEAD).transpose(2, 1, 0, 3).reshape(10, HEADS * HEAD)
    dk = summed[:, :10, :HEAD].transpose(1, 0, 2).reshape(10, HEADS * HEAD)
    dv = summed[:, :10, HEAD:].transpose(1, 0, 2).reshape(10, HEADS * HEAD)
    grad_qkv = jnp.concatenate([dq, dk, dv], axis=1)
    return (mixed.transpose(1, 0, 2), grad_latent.transpose(1, 0, 2), grad_qkv, grad_out)


def solution(mesh):
    fine = Mesh(mesh.devices.reshape(4, 4, 2, 2, 2), ALL)
    tokens = P(SEQ, ("rep", "own"), None)
    return jax.shard_map(
        shards,
        mesh=fine,
        in_specs=(tokens, tokens, P(), P(), P("own", None), P("own", None)),
        out_specs=(tokens, tokens, P(ALL, None), P(ALL, None)),
        check_vma=False,
    )
```

time: 1130 us -> 325 us (0.29)
  waiting for transfers between devices: 650 us -> 41.1 us
  matrix products: 153 us -> 0 us
  Pallas kernels: 0 us -> 131 us
  local copies, waits for them, and re-layouts: 103 us -> 15.7 us
  other arithmetic: 75.1 us -> 4.46 us
  blocking collectives: 84.8 us -> 69.7 us
    reduce_scatter x1 -> x0, waiting for transfers between devices: 424 us -> none  [scatter_lines(): own = lax.psum_scatter(lines, axis, scatter_dimension=0, tiled=True)]
    unnamed x6 -> x1, waiting for transfers between devices: 182 us -> 0.02 us
    dot_general x62 -> x0, matrix products: 153 us -> none  [the longest x16 28.6 us: probabilities(): jnp.einsum('qhd,khd->hqk', query_block, key_heads, preferred_element_type...]
    pallas_call x0 -> x9, Pallas kernels: none -> 131 us  [the longest x1 83 us: attention(): pl.pallas_call(functools.partial(attention_kernel, ck), grid=(sources //...]
    psum x1 -> x0, blocking collectives: 71.6 us -> none  [shards(): lax.psum((jnp.sum(grouped, axis=(0, 3)), jnp.sum(grouped * grouped, axis=...]
    all_to_all x1 -> x3, blocking collectives: 13.2 us -> 69.7 us  [exchanged(): return lax.all_to_all(value, axes, 0, 0, tiled=True)]
    convert_element_type x10 -> x0, other arithmetic: 30.1 us -> none  [the longest x8 29.5 us: backward_block(): (probs_high * (dprobs - row_delta) * score_scale).astype(jnp.bfloat16)]
    reduce_sum x22 -> x2, other arithmetic: 24.6 us -> 2.08 us  [the longest x1 1.31 us: shards(): summed = jnp.sum(in_blocks.reshape(HEADS, 8, 16, 128), axis=1)]
  transfers between devices with their start and end apart: 13 -> 11, of which waited for: 8 -> 5; matrix products, arithmetic and copies ran while one was open for 29% -> 4% of each run, Pallas kernels for 0% -> 41%
where the time goes in v1:
time: 325 us; the launch traced here: 323 us
  Pallas kernels  131 us (40%)
  blocking collectives  69.7 us (21%)
  starting transfers between devices  47.1 us (14%)
  waiting for transfers between devices  41.1 us (13%)
  local copies, waits for them, and re-layouts  15.7 us (5%)
  between operations  14.3 us (4%)
  other arithmetic  4.46 us (1%)
    pallas_call x1, Pallas kernels, attention(): pl.pallas_call(functools.partial(attention_kernel, ck), grid=(sources //...  83 us
    all_to_all x3, blocking collectives, exchanged(): return lax.all_to_all(value, axes, 0, 0, tiled=True)  69.7 us
    all_to_all x6, starting transfers between devices, exchanged(): return lax.all_to_all(value, axes, 0, 0, tiled=True)  42.2 us
    all_to_all x6, waiting for transfers between devices, exchanged(): return lax.all_to_all(value, axes, 0, 0, tiled=True)  41.1 us
    pallas_call x1, Pallas kernels, in_weight(): pl.pallas_call(in_weight_kernel, grid=(sources // here,), in_specs=[pl.Bl...  11.6 us
    unnamed x31, local copies, waits for them, and re-layouts  11.3 us
    pallas_call x1, Pallas kernels, back(): pl.pallas_call(back_kernel, grid_spec=pltpu.PrefetchScalarGridSpec(num_sc...  8.34 us
    pallas_call x1, Pallas kernels, project(): pl.pallas_call(functools.partial(project_kernel, count), grid_spec=pltpu....  8.1 us
  transfers between devices with their start and end apart: 11, of which 5 were waited for; matrix products, arithmetic and copies ran while one was open for 4% of the time, Pallas kernels for 41%

profile of v1, /device:TPU:1, one launch (start us, length us, event | category | flops | bytes accessed | tf_op | source)
XLA Modules:
  0.0 323.4 jit_solution(7013523490956146476)
XLA Ops:
  8.5 12.4 %all_to_all.45 = bf16[2,128,1280]{2,1,0:T(8,128)(2,1)} all-to-all(bf16[2,128,1280]{2,1,0:T(8,128)(2,1)S(1)} %bitcast.29), channel_id=1, replica_groups=mesh['y'=4,'z'=4,'xl'=2,'rep'=2,'own'=2] {'xl'}, dimensions={0} | all-to-all | bytes 1310720 | tf_op jit(solution)/shard_map/all_to_all | solution.py:459
  22.8 2.3 shard_map.93
  26.4 8.3 %all-to-all-start = ((f32[32,8,128]{2,1,0:T(8,128)}), f32[32,8,128]{2,1,0:T(8,128)S(1)}, u32[]{:S(2)}, u32[]{:S(2)}) async-start(f32[32,8,128]{2,1,0:T(8,128)} %broadcast_in_dim.4), calls=%async_computation | async-start | bytes 262144 | tf_op jit(solution)/shard_map/all_to_all | solution.py:459
  34.7 2.1 copy.43
  38.4 4.7 %shard_map.95 = bf16[16,2,64,128]{3,2,1,0:T(8,128)(2,1)} custom-call(s32[1]{0:T(128)} %bitcast.own_ref, bf16[2,128,1280]{2,1,0:T(8,128)(2,1)} %bitcast.35, bf16[2,512,1280]{2,1,0:T(8,128)(2,1)} %pad_maximum_fusion.w_ref), custom_call_target="tpu_custom_call" | custom-call | flops 671088640 | bytes 4194304 | tf_op jit(solution)/shard_map/pallas_call | solution.py:150
  43.1 7.7 %all-to-all-start.2 = ((bf16[32,64,128]{2,1,0:T(8,128)(2,1)}), bf16[32,64,128]{2,1,0:T(8,128)(2,1)S(1)}, u32[]{:S(2)}, u32[]{:S(2)}) async-start(bf16[32,64,128]{2,1,0:T(8,128)(2,1)} %bitcast.43), calls=%async_computation.2 | async-start | bytes 1048576 | tf_op jit(solution)/shard_map/all_to_all | solution.py:459
  52.1 8.1 %shard_map.94 = (bf16[16,2,192,128]{3,2,1,0:T(8,128)(2,1)}, f32[8,1280]{1,0:T(8,128)}) custom-call(s32[1]{0:T(128)} %bitcast.own_ref, bf16[2,128,1280]{2,1,0:T(8,128)(2,1)} %bitcast.31, f32[32,8,128]{2,1,0:T(8,128)} %copy-done.9, f32[1,1280]{1,0:T(1,128)} %reshape.53.gain_ref, f32[1,1280]{1,0:T(1,128)} %reshape.54.shift_ref, bf16[640,3072]{1,0:T(8,128)(2,1)} %mine_ref.1, ...), custom_call_target="tpu_custom_call" | custom-call | flops 2013265920 | bytes 12582912 | tf_op jit(solution)/shard_map/pallas_call | solution.py:115
  61.7 35.7 %all_to_all.46.kvq_ref = bf16[32,192,128]{2,1,0:T(8,128)(2,1)} all-to-all(bf16[32,192,128]{2,1,0:T(8,128)(2,1)} %bitcast.44), channel_id=1, replica_groups=mesh['y'=4,'z'=4,'xl'=2,'rep'=2,'own'=2] {'y','z','xl'}, dimensions={0} | all-to-all | bytes 3145728 | tf_op jit(solution)/shard_map/all_to_all | solution.py:459
  97.5 83.0 %shard_map.96 = (bf16[32,128,128]{2,1,0:T(8,128)(2,1)}, bf16[32,128,128]{2,1,0:T(8,128)(2,1)}) custom-call(bf16[32,192,128]{2,1,0:T(8,128)(2,1)} %all_to_all.46.kvq_ref, bf16[32,64,128]{2,1,0:T(8,128)(2,1)} %copy-done.7), custom_call_target="tpu_custom_call" | custom-call | flops 51539607552 | bytes 4194304 | tf_op jit(solution)/shard_map/pallas_call | solution.py:238
  180.5 21.6 %all_to_all.47 = bf16[32,128,128]{2,1,0:T(8,128)(2,1)} all-to-all(bf16[32,128,128]{2,1,0:T(8,128)(2,1)} %get-tuple-element.13.dqo_ref), channel_id=1, replica_groups=mesh['y'=4,'z'=4,'xl'=2,'rep'=2,'own'=2] {'y','z','xl'}, dimensions={0} | all-to-all | bytes 2097152 | tf_op jit(solution)/shard_map/all_to_all | solution.py:459
  202.1 3.9 %all-to-all-start.4 = ((bf16[32,128,128]{2,1,0:T(8,128)(2,1)}), bf16[32,128,128]{2,1,0:T(8,128)(2,1)S(1)}, u32[]{:S(2)}, u32[]{:S(2)}) async-start(bf16[32,128,128]{2,1,0:T(8,128)(2,1)} %get-tuple-element.15.dkv_ref), calls=%async_computation.4 | async-start | bytes 2097152 | tf_op jit(solution)/shard_map/all_to_all | solution.py:459
  206.0 3.1 collective-permute-start.3
  209.1 4.2 %shard_map.97 = (bf16[2,128,1280]{2,1,0:T(8,128)(2,1)}, bf16[2,128,1024]{2,1,0:T(8,128)(2,1)}) custom-call(s32[1]{0:T(128)} %bitcast.own_ref, bf16[16,2,128,128]{3,2,1,0:T(8,128)(2,1)} %bitcast.39, bf16[2,128,1280]{2,1,0:T(8,128)(2,1)} %bitcast.32, bf16[2,512,1280]{2,1,0:T(8,128)(2,1)} %pad_maximum_fusion.w_ref), custom_call_target="tpu_custom_call" | custom-call | flops 671088640 | bytes 6291456 | tf_op jit(solution)/shard_map/pallas_call | solution.py:341
  213.3 8.4 %all-to-all-done.4 = bf16[32,128,128]{2,1,0:T(8,128)(2,1)S(1)} async-done(((bf16[32,128,128]{2,1,0:T(8,128)(2,1)}), bf16[32,128,128]{2,1,0:T(8,128)(2,1)S(1)}, u32[]{:S(2)}, u32[]{:S(2)}) %all-to-all-start.4) | async-done | bytes 1048608 | tf_op jit(solution)/shard_map/all_to_all | solution.py:459
  222.7 8.3 %shard_map.98 = (f32[2,128,1280]{2,1,0:T(8,128)}, f32[8,128]{1,0:T(8,128)}) custom-call(s32[1]{0:T(128)} %bitcast.own_ref, bf16[16,2,128,128]{3,2,1,0:T(8,128)(2,1)} %bitcast.40, bf16[16,2,128,128]{3,2,1,0:T(8,128)(2,1)} %bitcast.41, bf16[640,3072]{1,0:T(8,128)(2,1)} %mine_ref.1, bf16[640,3072]{1,0:T(8,128)(2,1)} %collective-permute-done.refs_3_.refs_4_.refs_5_.other_ref, ...), custom_call_target="tpu_custom_call" | custom-call | flops 2013265920 | bytes 14680064 | tf_op jit(solution)/shard_map/pallas_call | solution.py:420
  232.4 3.9 %all-to-all-start.5 = ((f32[32,8,128]{2,1,0:T(8,128)}), f32[32,8,128]{2,1,0:T(8,128)S(1)}, u32[]{:S(2)}, u32[]{:S(2)}) async-start(f32[32,8,128]{2,1,0:T(8,128)} %broadcast_in_dim.5), calls=%async_computation.5 | async-start | bytes 262144 | tf_op jit(solution)/shard_map/all_to_all | solution.py:459
  237.9 5.3 %shard_map.101 = f32[64,8,1280]{2,1,0:T(8,128)} custom-call(s32[1]{0:T(128)} %bitcast.own_ref, bf16[2,128,1024]{2,1,0:T(8,128)(2,1)} %get-tuple-element.19.att_ref, bf16[2,128,1024]{2,1,0:T(8,128)(2,1)} %copy-done.6, bf16[2,128,1280]{2,1,0:T(8,128)(2,1)} %bitcast.36, bf16[2,128,1280]{2,1,0:T(8,128)(2,1)} %copy-done.4), custom_call_target="tpu_custom_call" | custom-call | flops 1342177280 | bytes 6291456 | tf_op jit(solution)/shard_map/pallas_call | solution.py:374
  244.5 9.3 %all-to-all-start.8 = ((f32[64,8,1280]{2,1,0:T(8,128)}), f32[64,8,1280]{2,1,0:T(8,128)S(1)}, u32[]{:S(2)}, u32[]{:S(2)}) async-start(f32[64,8,1280]{2,1,0:T(8,128)} %shard_map.101), calls=%async_computation.8 | async-start | bytes 5242880 | tf_op jit(solution)/shard_map/all_to_all | solution.py:459
  254.5 11.6 %shard_map.100 = f32[128,16,128]{2,1,0:T(8,128)} custom-call(bf16[32,128,1280]{2,1,0:T(8,128)(2,1)} %all-gather.2.cloned.1.call-done.lat_ref, f32[2,1280]{1,0:T(2,128)} %bitcast.49, f32[1,1280]{1,0:T(1,128)} %reshape.53.gain_ref, f32[1,1280]{1,0:T(1,128)} %reshape.54.shift_ref, bf16[32,128,128]{2,1,0:T(8,128)(2,1)} %get-tuple-element.13.dqo_ref, ...), custom_call_target="tpu_custom_call" | custom-call | flops 2684354560 | bytes 14680064 | tf_op jit(solution)/shard_map/pallas_call | solution.py:295
  266.1 20.0 %all-to-all-done.8 = f32[64,8,1280]{2,1,0:T(8,128)S(1)} async-done(((f32[64,8,1280]{2,1,0:T(8,128)}), f32[64,8,1280]{2,1,0:T(8,128)S(1)}, u32[]{:S(2)}, u32[]{:S(2)}) %all-to-all-start.8) | async-done | bytes 2621472 | tf_op jit(solution)/shard_map/all_to_all | solution.py:459
  286.1 9.0 %all-to-all-start.7 = ((f32[128,16,128]{2,1,0:T(8,128)}), f32[128,16,128]{2,1,0:T(8,128)}, u32[]{:S(2)}, u32[]{:S(2)}) async-start(f32[128,16,128]{2,1,0:T(8,128)} %shard_map.100), calls=%async_computation.7 | async-start | bytes 2097152 | tf_op jit(solution)/shard_map/all_to_all | solution.py:459
  296.6 3.6 %shard_map.99 = bf16[2,128,1280]{2,1,0:T(8,128)(2,1)} custom-call(f32[2,128,1280]{2,1,0:T(8,128)} %get-tuple-element.17.grad_ref, f32[32,8,128]{2,1,0:T(8,128)} %copy-done.8, bf16[2,128,1280]{2,1,0:T(8,128)(2,1)} %bitcast.34, bf16[2,128,1280]{2,1,0:T(8,128)(2,1)} %bitcast.37, f32[8,1280]{1,0:T(8,128)} %get-tuple-element.16.chan_ref), custom_call_target="tpu_custom_call" | custom-call | flops 4194304 | bytes 4194304 | tf_op jit(solution)/shard_map/pallas_call | solution.py:446
  300.2 2.6 copy.38
  303.6 10.4 %all-to-all-done.7 = f32[128,16,128]{2,1,0:T(8,128)} async-done(((f32[128,16,128]{2,1,0:T(8,128)}), f32[128,16,128]{2,1,0:T(8,128)}, u32[]{:S(2)}, u32[]{:S(2)}) %all-to-all-start.7) | async-done | bytes 1048608 | tf_op jit(solution)/shard_map/all_to_all | solution.py:459
  (63 shorter events, 19.7 us)
Async XLA Ops:
  7.2 15.5 %copy-start.3 = (bf16[512,1280]{1,0:T(8,128)(2,1)S(1)}, bf16[512,1280]{1,0:T(8,128)(2,1)}, u32[]{:S(2)}) copy-start(bf16[512,1280]{1,0:T(8,128)(2,1)} %param.11) | copy-start | bytes 3932164
  7.2 247.4 %all-gather.2.cloned.1.call-start = ((), (), s32[]{:S(2)}) async-start(), calls=%async_computation.9 | async-start | bytes 11141120 | tf_op jit(solution)/shard_map/all_gather | solution.py:476
  8.5 14.3 %copy-start = (bf16[128,2,1280]{2,0,1:T(8,128)(2,1)}, bf16[128,2,1280]{2,0,1:T(8,128)(2,1)S(1)}, u32[]{:S(2)}) copy-start(bf16[128,2,1280]{2,0,1:T(8,128)(2,1)S(1)} %copy.44) | copy-start | bytes 1966084
  20.9 31.1 %collective-permute-start = (bf16[640,3072]{1,0:T(8,128)(2,1)}, bf16[640,3072]{1,0:T(8,128)(2,1)}, u32[]{:S(2)}, u32[]{:S(2)}) collective-permute-start(bf16[640,3072]{1,0:T(8,128)(2,1)} %mine_ref.1), channel_id=1, source_target_pairs={{0,1},{1,0},{2,3},{3,2},{4,5},{5,4},{6,7},{7,6},{8,9},{9,8},{10,11... | collective-permute-start | bytes 11796488 | tf_op jit(solution)/shard_map/ppermute | solution.py:455
  22.7 14.1 %collective-permute-start.1 = (bf16[512,1280]{1,0:T(8,128)(2,1)S(1)}, bf16[512,1280]{1,0:T(8,128)(2,1)S(1)}, u32[]{:S(2)}, u32[]{:S(2)}) collective-permute-start(bf16[512,1280]{1,0:T(8,128)(2,1)S(1)} %copy-done.3), channel_id=1, source_target_pairs={{0,1},{1,0},{2,3},{3,2},{4,5},{5,4},{6,7},{7,6},{8,9},{9,8},{10,11... | collective-permute-start | bytes 3932168 | tf_op jit(solution)/shard_map/ppermute | solution.py:455
  26.4 16.7 %all-to-all-start = ((f32[32,8,128]{2,1,0:T(8,128)}), f32[32,8,128]{2,1,0:T(8,128)S(1)}, u32[]{:S(2)}, u32[]{:S(2)}) async-start(f32[32,8,128]{2,1,0:T(8,128)} %broadcast_in_dim.4), calls=%async_computation | async-start | bytes 262144 | tf_op jit(solution)/shard_map/all_to_all | solution.py:459
  38.4 12.4 %copy-start.11 = (f32[1280]{0:T(1024)S(1)}, f32[1280]{0:T(1024)}, u32[]{:S(2)}) copy-start(f32[1280]{0:T(1024)} %param.8) | copy-start | bytes 15364
  38.4 13.0 %copy-start.12 = (f32[1280]{0:T(1024)S(1)}, f32[1280]{0:T(1024)}, u32[]{:S(2)}) copy-start(f32[1280]{0:T(1024)} %param.9) | copy-start | bytes 15364
  43.1 9.0 %copy-start.9 = (f32[32,8,128]{2,1,0:T(8,128)}, f32[32,8,128]{2,1,0:T(8,128)S(1)}, u32[]{:S(2)}) copy-start(f32[32,8,128]{2,1,0:T(8,128)S(1)} %all-to-all-done.sums_ref) | copy-start | bytes 393220
  43.1 18.6 %all-to-all-start.2 = ((bf16[32,64,128]{2,1,0:T(8,128)(2,1)}), bf16[32,64,128]{2,1,0:T(8,128)(2,1)S(1)}, u32[]{:S(2)}, u32[]{:S(2)}) async-start(bf16[32,64,128]{2,1,0:T(8,128)(2,1)} %bitcast.43), calls=%async_computation.2 | async-start | bytes 1048576 | tf_op jit(solution)/shard_map/all_to_all | solution.py:459
  61.7 35.7 %copy-start.7 = (bf16[32,64,128]{2,1,0:T(8,128)(2,1)}, bf16[32,64,128]{2,1,0:T(8,128)(2,1)S(1)}, u32[]{:S(2)}) copy-start(bf16[32,64,128]{2,1,0:T(8,128)(2,1)S(1)} %all-to-all-done.2.g_ref) | copy-start | bytes 1572868
  180.5 25.5 %copy-start.1 = (bf16[128,2,1280]{2,0,1:T(8,128)(2,1)S(1)}, bf16[128,2,1280]{2,0,1:T(8,128)(2,1)}, u32[]{:S(2)}) copy-start(bf16[128,2,1280]{2,0,1:T(8,128)(2,1)} %copy.43) | copy-start | bytes 1966084
  202.1 19.7 %all-to-all-start.4 = ((bf16[32,128,128]{2,1,0:T(8,128)(2,1)}), bf16[32,128,128]{2,1,0:T(8,128)(2,1)S(1)}, u32[]{:S(2)}, u32[]{:S(2)}) async-start(bf16[32,128,128]{2,1,0:T(8,128)(2,1)} %get-tuple-element.15.dkv_ref), calls=%async_computation.4 | async-start | bytes 2097152 | tf_op jit(solution)/shard_map/all_to_all | solution.py:459
  206.0 30.2 %collective-permute-start.3 = (bf16[2,128,1280]{2,1,0:T(8,128)(2,1)S(1)}, bf16[2,128,1280]{2,1,0:T(8,128)(2,1)S(1)}, u32[]{:S(2)}, u32[]{:S(2)}) collective-permute-start(bf16[2,128,1280]{2,1,0:T(8,128)(2,1)S(1)} %bitcast.38), channel_id=1, source_target_pairs={{0,1},{1,0},{2,3},{3,2},{4,5},{5,4},{6,7},{7,6},{8,9},{9,8},{10,11... | collective-permute-start | bytes 1966088 | tf_op jit(solution)/shard_map/ppermute | solution.py:455
  213.3 23.0 %collective-permute-start.2 = (bf16[2,128,1024]{2,1,0:T(8,128)(2,1)}, bf16[2,128,1024]{2,1,0:T(8,128)(2,1)S(1)}, u32[]{:S(2)}, u32[]{:S(2)}) collective-permute-start(bf16[2,128,1024]{2,1,0:T(8,128)(2,1)} %get-tuple-element.19.att_ref), channel_id=1, source_target_pairs={{0,1},{1,0},{2,3},{3,2},{4,5},{5,4},{6,7},{7,6},{8,9},{9,8},{10,11... | collective-permute-start | bytes 1572872 | tf_op jit(solution)/shard_map/ppermute | solution.py:455
  221.7 1.0 copy-start.2
  232.4 11.5 %all-to-all-start.5 = ((f32[32,8,128]{2,1,0:T(8,128)}), f32[32,8,128]{2,1,0:T(8,128)S(1)}, u32[]{:S(2)}, u32[]{:S(2)}) async-start(f32[32,8,128]{2,1,0:T(8,128)} %broadcast_in_dim.5), calls=%async_computation.5 | async-start | bytes 262144 | tf_op jit(solution)/shard_map/all_to_all | solution.py:459
  236.3 0.8 copy-start.4
  237.1 0.8 copy-start.6
  243.2 10.7 %copy-start.10 = (f32[8,1280]{1,0:T(8,128)S(1)}, f32[8,1280]{1,0:T(8,128)}, u32[]{:S(2)}) copy-start(f32[8,1280]{1,0:T(8,128)} %get-tuple-element.16.chan_ref) | copy-start | bytes 122884
  243.9 0.7 copy-start.8
  244.5 41.5 %all-to-all-start.8 = ((f32[64,8,1280]{2,1,0:T(8,128)}), f32[64,8,1280]{2,1,0:T(8,128)S(1)}, u32[]{:S(2)}, u32[]{:S(2)}) async-start(f32[64,8,1280]{2,1,0:T(8,128)} %shard_map.101), calls=%async_computation.8 | async-start | bytes 5242880 | tf_op jit(solution)/shard_map/all_to_all | solution.py:459
  254.5 40.6 %copy-start.5 = (bf16[2,128,1280]{2,1,0:T(8,128)(2,1)S(1)}, bf16[2,128,1280]{2,1,0:T(8,128)(2,1)}, u32[]{:S(2)}) copy-start(bf16[2,128,1280]{2,1,0:T(8,128)(2,1)} %get-tuple-element.14) | copy-start | bytes 1966084
  286.1 27.9 %all-to-all-start.7 = ((f32[128,16,128]{2,1,0:T(8,128)}), f32[128,16,128]{2,1,0:T(8,128)}, u32[]{:S(2)}, u32[]{:S(2)}) async-start(f32[128,16,128]{2,1,0:T(8,128)} %shard_map.100), calls=%async_computation.7 | async-start | bytes 2097152 | tf_op jit(solution)/shard_map/all_to_all | solution.py:459
Sparse Core Ops, SparseCore 0:
  21.1 101.7 all-gather.1

commit v2 on v1

--- a/solution.py
+++ b/solution.py
@@ -46,17 +46,16 @@
 
 
 def stats_kernel(lat_ref, out_ref):
-    rows = []
     values = [lat_ref[i].astype(F32) for i in range(2)]
     rows = [jnp.sum(v, axis=0, keepdims=True) for v in values]
     rows += [jnp.sum(v * v, axis=0, keepdims=True) for v in values]
-    out_ref[...] = by_group(four_rows(rows), members(lat_ref.shape[2]))
-
-
-def stats(lat):
+    out_ref[...] = jnp.broadcast_to(by_group(four_rows(rows), members(lat_ref.shape[2]))[None], out_ref.shape)
+
+
+def stats(lat, copies):
     return pl.pallas_call(
         stats_kernel,
-        out_shape=jax.ShapeDtypeStruct((8, 128), F32),
+        out_shape=jax.ShapeDtypeStruct((copies, 8, 128), F32),
         compiler_params=pltpu.CompilerParams(vmem_limit_bytes=VMEM),
         cost_estimate=pl.CostEstimate(flops=1 << 20, bytes_accessed=lat.size * 2, transcendentals=0),
     )(lat)
@@ -68,7 +67,7 @@
     return jnp.concatenate([means[0:2], lax.rsqrt(var + 1e-06), jnp.zeros((4, 128), F32)], axis=0)
 
 
-def project_kernel(count, own_ref, lat_ref, sums_ref, gain_ref, shift_ref, *refs):
+def project_kernel(count, own_ref, lat_ref, sums_ref, gain_ref, shift_ref, g_ref, *refs):
     mine, other = refs[0:3], refs[3:6]
     out_ref, chan_ref, normed_ref = refs[6:]
     own = own_ref[0]
@@ -83,6 +82,7 @@
             centred = (lat_ref[i].astype(F32) - chan[i : i + 1]) * chan[2 + i : 3 + i]
             normed_ref[i * 128 : (i + 1) * 128] = (centred * gain_ref[...] + shift_ref[...]).astype(BF16)
 
+    out_ref[:, :, 192:256] = g_ref[...]
     near = normed_ref[:, pl.ds(pl.multiple_of(own * half, 128), half)]
     far = normed_ref[:, pl.ds(pl.multiple_of((1 - own) * half, 128), half)]
     query, key, value = [
@@ -98,11 +98,11 @@
             out_ref[h, i, :128] = jnp.where(low, k, v_roll).astype(BF16)
             out_ref[h + 1, i, :128] = jnp.where(low, k_roll, v).astype(BF16)
             first, second = q[:64], q[64:]
-            out_ref[h, i, 128:] = jnp.where(low[:64], first, pltpu.roll(second, HEAD, 1)).astype(BF16)
-            out_ref[h + 1, i, 128:] = jnp.where(low[:64], pltpu.roll(first, HEAD, 1), second).astype(BF16)
-
-
-def project(own, lat, sums, gain, shift, mine, other, count):
+            out_ref[h, i, 128:192] = jnp.where(low[:64], first, pltpu.roll(second, HEAD, 1)).astype(BF16)
+            out_ref[h + 1, i, 128:192] = jnp.where(low[:64], pltpu.roll(first, HEAD, 1), second).astype(BF16)
+
+
+def project(own, lat, sums, gain, shift, g, mine, other, count):
     channels = lat.shape[2]
     cols, half = HEADS * HEAD // 256, mine.shape[0]
 
@@ -118,17 +118,18 @@
             num_scalar_prefetch=1,
             grid=(cols,),
             in_specs=[whole(*lat.shape), whole(*sums.shape), whole(1, channels), whole(1, channels)]
+            + [pl.BlockSpec((4, 2, 64, 128), lambda s, own: (s, 0, 0, 0))]
             + [weight(p) for p in range(3)] * 2,
-            out_specs=[pl.BlockSpec((4, 2, 192, 128), lambda s, own: (s, 0, 0, 0)), whole(8, channels)],
+            out_specs=[pl.BlockSpec((4, 2, 256, 128), lambda s, own: (s, 0, 0, 0)), whole(8, channels)],
             scratch_shapes=[pltpu.VMEM((256, channels), BF16)],
         ),
         out_shape=[
-            jax.ShapeDtypeStruct((HEADS, 2, 192, 128), BF16),
+            jax.ShapeDtypeStruct((HEADS, 2, 256, 128), BF16),
             jax.ShapeDtypeStruct((8, channels), F32),
         ],
         compiler_params=pltpu.CompilerParams(vmem_limit_bytes=VMEM),
         cost_estimate=pl.CostEstimate(flops=2 * 256 * 1280 * 3072, bytes_accessed=12 << 20, transcendentals=0),
-    )(own, lat, sums, gain, shift, mine, mine, mine, other, other, other)
+    )(own, lat, sums, gain, shift, g, mine, mine, mine, other, other, other)
 
 
 def attended_grad_kernel(own_ref, cot_ref, w_ref, out_ref):
@@ -167,7 +168,7 @@
     )(own, cot, halves)
 
 
-def attention_kernel(ck, kvq_ref, g_ref, dqo_ref, dkv_ref, s_ref, x_ref, y_ref, acc_ref):
+def attention_kernel(ck, kvq_ref, dqo_ref, dkv_ref, s_ref, x_ref, y_ref, acc_ref):
     step, last = pl.program_id(0), pl.num_programs(0) - 1
     sources, _, width = kvq_ref.shape
     keys = sources * 128
@@ -181,7 +182,7 @@
 
     low = lax.broadcasted_iota(jnp.int32, (half, width), 1) < HEAD
     xq = kvq_ref[pl.ds(step * here, here), 128:192, :].reshape(half, width).astype(F32) * SCALE
-    xg = g_ref[pl.ds(step * here, here), :, :].reshape(half, width).astype(F32)
+    xg = kvq_ref[pl.ds(step * here, here), 192:256, :].reshape(half, width).astype(F32)
     zero = jnp.zeros_like(xq)
     y_ref[0 * half : 1 * half] = jnp.where(low, xq, zero).astype(BF16)
     y_ref[1 * half : 2 * half] = jnp.where(low, pltpu.roll(xq, HEAD, 1), zero).astype(BF16)
@@ -232,15 +233,14 @@
         dkv_ref[...] = acc_ref[...].reshape(sources, 128, width).astype(BF16)
 
 
-def attention(kvq, g, here=2, ck=1024):
+def attention(kvq, here=2, ck=1024):
     sources = kvq.shape[0]
     keys, rows = sources * 128, here * 128
     return pl.pallas_call(
         functools.partial(attention_kernel, ck),
         grid=(sources // here,),
         in_specs=[
-            pl.BlockSpec((sources, 192, 128), lambda i: (0, 0, 0), pipeline_mode=pl.Buffered(1)),
-            pl.BlockSpec((sources, 64, 128), lambda i: (0, 0, 0), pipeline_mode=pl.Buffered(1)),
+            pl.BlockSpec((sources, 256, 128), lambda i: (0, 0, 0), pipeline_mode=pl.Buffered(1)),
         ],
         out_specs=[
             pl.BlockSpec((here, 128, 128), lambda i: (i, 0, 0)),
@@ -258,7 +258,7 @@
         ],
         compiler_params=pltpu.CompilerParams(vmem_limit_bytes=VMEM),
         cost_estimate=pl.CostEstimate(flops=48 * keys * keys * HEAD, bytes_accessed=4 << 20, transcendentals=keys * keys),
-    )(kvq, g)
+    )(kvq)
 
 
 def in_weight_kernel(lat_ref, chan_ref, gain_ref, shift_ref, dqo_ref, dkv_ref, out_ref, acc_ref, turned_ref):
@@ -409,10 +409,10 @@
         centred = (lat_ref[i].astype(F32) - chan_ref[i : i + 1]) * chan_ref[2 + i : 3 + i]
         ones.append(jnp.sum(grad, axis=0, keepdims=True))
         twos.append(jnp.sum(grad * centred, axis=0, keepdims=True))
-    sums_ref[...] = by_group(four_rows(ones + twos), members(lat_ref.shape[2]))
-
-
-def back(own, dqo, dkv, mine, other, lat, chan, gain):
+    sums_ref[...] = jnp.broadcast_to(by_group(four_rows(ones + twos), members(lat_ref.shape[2]))[None], sums_ref.shape)
+
+
+def back(own, dqo, dkv, mine, other, lat, chan, gain, copies):
     def whole(shape):
         return pl.BlockSpec(shape, lambda s, own: (0,) * len(shape), pipeline_mode=pl.Buffered(1))
 
@@ -423,10 +423,10 @@
             num_scalar_prefetch=1,
             grid=(1,),
             in_specs=[whole(a.shape) for a in operands],
-            out_specs=[whole(lat.shape), whole((8, 128))],
+            out_specs=[whole(lat.shape), whole((copies, 8, 128))],
             scratch_shapes=[pltpu.VMEM((256, 3 * HEADS * HEAD), BF16)],
         ),
-        out_shape=[jax.ShapeDtypeStruct(lat.shape, F32), jax.ShapeDtypeStruct((8, 128), F32)],
+        out_shape=[jax.ShapeDtypeStruct(lat.shape, F32), jax.ShapeDtypeStruct((copies, 8, 128), F32)],
         compiler_params=pltpu.CompilerParams(vmem_limit_bytes=VMEM),
         cost_estimate=pl.CostEstimate(flops=2 * 256 * 1280 * 3072, bytes_accessed=14 << 20, transcendentals=0),
     )(own, *operands)
@@ -459,10 +459,6 @@
     return lax.all_to_all(value, axes, 0, 0, tiled=True)
 
 
-def shared(value, axes):
-    return exchanged(jnp.broadcast_to(value[None], (lax.axis_size(axes), *value.shape)), axes)
-
-
 def shards(latent, cotangent, norm_gain, norm_shift, proj_qkv, proj_out):
     local_len, images, channels = latent.shape
     seq_count = lax.axis_size(SEQ)
@@ -472,29 +468,39 @@
 
     other_out = swapped(proj_out, "own")
     other_qkv = swapped(proj_qkv, "own")
-    lat, cot = latent.transpose(1, 0, 2), cotangent.transpose(1, 0, 2)
-    image_lat = lax.all_gather(exchanged(lat, "xl"), ("y", "z"), tiled=True)
-    sums = shared(stats(lat), SEQ)
+    lat = latent.transpose(1, 0, 2)
+    sums = exchanged(stats(lat, seq_count), SEQ)
+    cot = cotangent.transpose(1, 0, 2)
+    image = lax.axis_index("xl")
+    near = jnp.where(image == 0, lat[0], lat[1])
+    far = swapped(jnp.where(image == 0, lat[1], lat[0]), "xl")
+    pair_lat = jnp.where(image == 0, jnp.stack([near, far]), jnp.stack([far, near]))
     halves_out = jnp.stack([proj_out, other_out])
     cot_far = swapped(cot, "own")
-    g_send = attended_grad(own, cot, halves_out)
-    g = exchanged(g_send.reshape(seq_count, 64, 128), SEQ)
-    kvq_send, chan = project(own, lat, sums, gain, shift, proj_qkv, other_qkv, count)
-    kvq = exchanged(kvq_send.reshape(seq_count, 192, 128), SEQ)
-
-    dqo, dkv = attention(kvq, g)
-
-    dqo_tok = exchanged(dqo, SEQ).reshape(HEADS, images, 128, 128)
-    dkv_tok = exchanged(dkv, SEQ).reshape(HEADS, images, 128, 128)
-    image = lax.axis_index("xl")
-    chan_image = lax.dynamic_slice_in_dim(chan[:4].reshape(2, 2, channels), image, 1, 1).reshape(2, channels)
+    g = attended_grad(own, cot, halves_out)
+    kvqg_send, chan = project(own, lat, sums, gain, shift, g, proj_qkv, other_qkv, count)
+    kvqg = exchanged(kvqg_send.reshape(seq_count, 256, 128), SEQ)
+    pair_lat, kvqg = lax.optimization_barrier((pair_lat, kvqg))
+    image_lat = lax.all_gather(pair_lat, ("y", "z"), tiled=True)
+
+    dqo, dkv = attention(kvqg)
+
+    dqo_tok = exchanged(dqo, SEQ)
+    chan_image = jnp.where(image == 0, chan[0:4:2], chan[1:4:2])
     in_part = in_weight(image_lat, chan_image, gain, shift, dqo, dkv)
+    dqo_tok, dkv, in_part = lax.optimization_barrier((dqo_tok, dkv, in_part))
+    dkv_tok = exchanged(dkv, SEQ)
+    dqo_tok = dqo_tok.reshape(HEADS, images, 128, 128)
     mixed, att = mix(own, dqo_tok, lat, halves_out)
     out_part = out_weight(own, att, swapped(att, "own"), cot, cot_far)
+    dkv_tok, out_part = lax.optimization_barrier((dkv_tok, out_part))
     out_blocks = exchanged(out_part, LINE)
+    dkv_tok = dkv_tok.reshape(HEADS, images, 128, 128)
+    grad, back_sums = back(own, dqo_tok, dkv_tok, proj_qkv, other_qkv, lat, chan, gain, seq_count)
+    out_blocks, back_sums = lax.optimization_barrier((out_blocks, back_sums))
+    back_sums, in_part = lax.optimization_barrier((exchanged(back_sums, SEQ), in_part))
     in_blocks = exchanged(in_part, ALL)
-    grad, back_sums = back(own, dqo_tok, dkv_tok, proj_qkv, other_qkv, lat, chan, gain)
-    grad_latent = final(grad, shared(back_sums, SEQ), lat, cot, chan, count)
+    grad_latent = final(grad, back_sums, lat, cot, chan, count)
 
     grad_out = jnp.sum(out_blocks, axis=0)
     summed = jnp.sum(in_blocks.reshape(HEADS, 8, 16, 128), axis=1)

time: 325 us -> 304 us (0.935)
  blocking collectives: 69.7 us -> 12.1 us
  waiting for transfers between devices: 41.1 us -> 73.3 us
  starting transfers between devices: 47.1 us -> 53.2 us
    all_to_all x3 -> x1, blocking collectives: 69.7 us -> 12.1 us  [exchanged(): return lax.all_to_all(value, axes, 0, 0, tiled=True)]
    ppermute x4 -> x5, waiting for transfers between devices: 0.01 us -> 31.8 us  [swapped(): return lax.ppermute(value, axis, [(0, 1), (1, 0)])]
    all_to_all x6, starting transfers between devices: 42.2 us -> 47.3 us  [exchanged(): return lax.all_to_all(value, axes, 0, 0, tiled=True)]
    unnamed x31 -> x32, local copies, waits for them, and re-layouts: 11.3 us -> 10.8 us
  transfers between devices with their start and end apart: 11 -> 12, of which waited for: 5 -> 6; matrix products, arithmetic and copies ran while one was open for 4% -> 4% of each run, Pallas kernels for 41% -> 41%
where the time goes in v2:
time: 304 us; the launch traced here: 303 us
  Pallas kernels  131 us (43%)
  waiting for transfers between devices  73.3 us (24%)
  starting transfers between devices  53.2 us (18%)
  between operations  14.3 us (5%)
  local copies, waits for them, and re-layouts  12.6 us (4%)
  blocking collectives  12.1 us (4%)
  other arithmetic  6.04 us (2%)
    pallas_call x1, Pallas kernels, attention(): pl.pallas_call(functools.partial(attention_kernel, ck), grid=(sources //...  83 us
    all_to_all x6, starting transfers between devices, exchanged(): return lax.all_to_all(value, axes, 0, 0, tiled=True)  47.3 us
    all_to_all x6, waiting for transfers between devices, exchanged(): return lax.all_to_all(value, axes, 0, 0, tiled=True)  41.5 us
    ppermute x5, waiting for transfers between devices, swapped(): return lax.ppermute(value, axis, [(0, 1), (1, 0)])  31.8 us
    all_to_all x1, blocking collectives, exchanged(): return lax.all_to_all(value, axes, 0, 0, tiled=True)  12.1 us
    pallas_call x1, Pallas kernels, in_weight(): pl.pallas_call(in_weight_kernel, grid=(sources // here,), in_specs=[pl.Bl...  11.6 us
    unnamed x32, local copies, waits for them, and re-layouts  10.8 us
    pallas_call x1, Pallas kernels, project(): pl.pallas_call(functools.partial(project_kernel, count), grid_spec=pltpu....  8.38 us
  transfers between devices with their start and end apart: 12, of which 6 were waited for; matrix products, arithmetic and copies ran while one was open for 4% of the time, Pallas kernels for 41%

profile of v2, /device:TPU:1, one launch (start us, length us, event | category | flops | bytes accessed | tf_op | source)
XLA Modules:
  0.0 302.7 jit_solution(10597568424997736167)
XLA Ops:
  8.8 2.0 copy.38
  10.8 2.3 shard_map.93
  13.1 9.1 %all-to-all-start = ((f32[32,8,128]{2,1,0:T(8,128)}), f32[32,8,128]{2,1,0:T(8,128)S(1)}, u32[]{:S(2)}, u32[]{:S(2)}) async-start(f32[32,8,128]{2,1,0:T(8,128)} %shard_map.93), calls=%async_computation | async-start | bytes 262144 | tf_op jit(solution)/shard_map/all_to_all | solution.py:459
  26.0 4.6 %shard_map.94.g_ref = bf16[16,2,64,128]{3,2,1,0:T(8,128)(2,1)} custom-call(s32[1]{0:T(128)} %bitcast.own_ref, bf16[2,128,1280]{2,1,0:T(8,128)(2,1)} %bitcast.34, bf16[2,512,1280]{2,1,0:T(8,128)(2,1)} %pad_maximum_fusion.w_ref), custom_call_target="tpu_custom_call" | custom-call | flops 671088640 | bytes 4194304 | tf_op jit(solution)/shard_map/pallas_call | solution.py:151
  31.3 8.4 %shard_map.95 = (bf16[16,2,256,128]{3,2,1,0:T(8,128)(2,1)}, f32[8,1280]{1,0:T(8,128)}) custom-call(s32[1]{0:T(128)} %bitcast.own_ref, bf16[2,128,1280]{2,1,0:T(8,128)(2,1)} %bitcast.29, f32[32,8,128]{2,1,0:T(8,128)} %copy-done.9, f32[1,1280]{1,0:T(1,128)} %reshape.44.gain_ref, f32[1,1280]{1,0:T(1,128)} %reshape.45.shift_ref, ...), custom_call_target="tpu_custom_call" | custom-call | flops 2013265920 | bytes 12582912 | tf_op jit(solution)/shard_map/pallas_call | solution.py:115
  39.7 7.9 %all-to-all-start.1 = ((bf16[32,256,128]{2,1,0:T(8,128)(2,1)}), bf16[32,256,128]{2,1,0:T(8,128)(2,1)S(1)}, u32[]{:S(2)}, u32[]{:S(2)}) async-start(bf16[32,256,128]{2,1,0:T(8,128)(2,1)} %bitcast.42), calls=%async_computation.1 | async-start | bytes 4194304 | tf_op jit(solution)/shard_map/all_to_all | solution.py:459
  49.0 29.7 %collective-permute-done = bf16[128,1280]{1,0:T(8,128)(2,1)S(1)} collective-permute-done((bf16[128,1280]{1,0:T(8,128)(2,1)S(1)}, bf16[128,1280]{1,0:T(8,128)(2,1)S(1)}, u32[]{:S(2)}, u32[]{:S(2)}) %collective-permute-start) | collective-permute-done | bytes 327712 | tf_op jit(solution)/shard_map/ppermute | solution.py:455
  80.9 83.0 %shard_map.96 = (bf16[32,128,128]{2,1,0:T(8,128)(2,1)}, bf16[32,128,128]{2,1,0:T(8,128)(2,1)}) custom-call(bf16[32,256,128]{2,1,0:T(8,128)(2,1)} %copy-done.4), custom_call_target="tpu_custom_call" | custom-call | flops 51539607552 | bytes 4194304 | tf_op jit(solution)/shard_map/pallas_call | solution.py:239
  163.9 9.4 %all-to-all-start.2 = ((bf16[32,128,128]{2,1,0:T(8,128)(2,1)}), bf16[32,128,128]{2,1,0:T(8,128)(2,1)S(1)}, u32[]{:S(2)}, u32[]{:S(2)}) async-start(bf16[32,128,128]{2,1,0:T(8,128)(2,1)} %get-tuple-element.25.dqo_ref), calls=%async_computation.2 | async-start | bytes 2097152 | tf_op jit(solution)/shard_map/all_to_all | solution.py:459
  174.0 11.6 %shard_map.97 = f32[128,16,128]{2,1,0:T(8,128)} custom-call(bf16[32,128,1280]{2,1,0:T(8,128)(2,1)} %all-gather.2.cloned.1.call-done.lat_ref, f32[2,1280]{1,0:T(2,128)} %broadcast_select_fusion.1.chan_ref, f32[1,1280]{1,0:T(1,128)} %reshape.44.gain_ref, f32[1,1280]{1,0:T(1,128)} %reshape.45.shift_ref, bf16[32,128,128]{2,1,0:T(8,128)(2,1)} %get-tuple-element.25.dqo_ref, ...), custom_call_target="tpu_custom_call" | custom-call | flops 2684354560 | bytes 14680064 | tf_op jit(solution)/shard_map/pallas_call | solution.py:295
  185.6 3.2 %all-to-all-done.2 = bf16[32,128,128]{2,1,0:T(8,128)(2,1)S(1)} async-done(((bf16[32,128,128]{2,1,0:T(8,128)(2,1)}), bf16[32,128,128]{2,1,0:T(8,128)(2,1)S(1)}, u32[]{:S(2)}, u32[]{:S(2)}) %all-to-all-start.2) | async-done | bytes 1048608 | tf_op jit(solution)/shard_map/all_to_all | solution.py:459
  188.8 4.3 %all-to-all-start.3 = ((bf16[32,128,128]{2,1,0:T(8,128)(2,1)}), bf16[32,128,128]{2,1,0:T(8,128)(2,1)S(1)}, u32[]{:S(2)}, u32[]{:S(2)}) async-start(bf16[32,128,128]{2,1,0:T(8,128)(2,1)} %get-tuple-element.31.dkv_ref), calls=%async_computation.3 | async-start | bytes 2097152 | tf_op jit(solution)/shard_map/all_to_all | solution.py:459
  193.2 3.0 collective-permute-start.4
  196.2 4.2 %shard_map.98 = (bf16[2,128,1280]{2,1,0:T(8,128)(2,1)}, bf16[2,128,1024]{2,1,0:T(8,128)(2,1)}) custom-call(s32[1]{0:T(128)} %bitcast.own_ref, bf16[16,2,128,128]{3,2,1,0:T(8,128)(2,1)} %bitcast.38, bf16[2,128,1280]{2,1,0:T(8,128)(2,1)} %bitcast.30, bf16[2,512,1280]{2,1,0:T(8,128)(2,1)} %pad_maximum_fusion.w_ref), custom_call_target="tpu_custom_call" | custom-call | flops 671088640 | bytes 6291456 | tf_op jit(solution)/shard_map/pallas_call | solution.py:341
  200.4 2.1 collective-permute-done.3.att_far_ref
  203.3 5.2 %shard_map.99 = f32[64,8,1280]{2,1,0:T(8,128)} custom-call(s32[1]{0:T(128)} %bitcast.own_ref, bf16[2,128,1024]{2,1,0:T(8,128)(2,1)} %get-tuple-element.32.att_ref, bf16[2,128,1024]{2,1,0:T(8,128)(2,1)} %copy-done.10, bf16[2,128,1280]{2,1,0:T(8,128)(2,1)} %bitcast.35, bf16[2,128,1280]{2,1,0:T(8,128)(2,1)} %copy-done.6), custom_call_target="tpu_custom_call" | custom-call | flops 1342177280 | bytes 6291456 | tf_op jit(solution)/shard_map/pallas_call | solution.py:374
  210.0 9.3 %all-to-all-start.4 = ((f32[64,8,1280]{2,1,0:T(8,128)}), f32[64,8,1280]{2,1,0:T(8,128)S(1)}, u32[]{:S(2)}, u32[]{:S(2)}) async-start(f32[64,8,1280]{2,1,0:T(8,128)} %shard_map.99), calls=%async_computation.4 | async-start | bytes 5242880 | tf_op jit(solution)/shard_map/all_to_all | solution.py:459
  219.4 8.3 %shard_map.100 = (f32[2,128,1280]{2,1,0:T(8,128)}, f32[32,8,128]{2,1,0:T(8,128)}) custom-call(s32[1]{0:T(128)} %bitcast.own_ref, bf16[16,2,128,128]{3,2,1,0:T(8,128)(2,1)} %bitcast.39, bf16[16,2,128,128]{3,2,1,0:T(8,128)(2,1)} %bitcast.40, bf16[640,3072]{1,0:T(8,128)(2,1)} %mine_ref.1, ...), custom_call_target="tpu_custom_call" | custom-call | flops 2013265920 | bytes 14680064 | tf_op jit(solution)/shard_map/pallas_call | solution.py:420
  227.7 27.3 %all-to-all-done.4 = f32[64,8,1280]{2,1,0:T(8,128)S(1)} async-done(((f32[64,8,1280]{2,1,0:T(8,128)}), f32[64,8,1280]{2,1,0:T(8,128)S(1)}, u32[]{:S(2)}, u32[]{:S(2)}) %all-to-all-start.4) | async-done | bytes 2621472 | tf_op jit(solution)/shard_map/all_to_all | solution.py:459
  255.0 12.1 %all_to_all.35.sums_ref = f32[32,8,128]{2,1,0:T(8,128)} all-to-all(f32[32,8,128]{2,1,0:T(8,128)} %get-tuple-element.37), channel_id=1, replica_groups=mesh['y'=4,'z'=4,'xl'=2,'rep'=2,'own'=2] {'y','z','xl'}, dimensions={0} | all-to-all | bytes 262144 | tf_op jit(solution)/shard_map/all_to_all | solution.py:459
  267.1 7.3 %all-to-all-start.6 = ((f32[128,16,128]{2,1,0:T(8,128)}), f32[128,16,128]{2,1,0:T(8,128)}, u32[]{:S(2)}, u32[]{:S(2)}) async-start(f32[128,16,128]{2,1,0:T(8,128)} %shard_map.97), calls=%async_computation.6 | async-start | bytes 2097152 | tf_op jit(solution)/shard_map/all_to_all | solution.py:459
  276.7 3.6 %shard_map.101 = bf16[2,128,1280]{2,1,0:T(8,128)(2,1)} custom-call(f32[2,128,1280]{2,1,0:T(8,128)} %get-tuple-element.34.grad_ref, f32[32,8,128]{2,1,0:T(8,128)} %all_to_all.35.sums_ref, bf16[2,128,1280]{2,1,0:T(8,128)(2,1)} %bitcast.32, bf16[2,128,1280]{2,1,0:T(8,128)(2,1)} %bitcast.36, f32[8,1280]{1,0:T(8,128)} %get-tuple-element.28.chan_ref), custom_call_target="tpu_custom_call" | custom-call | flops 4194304 | bytes 4194304 | tf_op jit(solution)/shard_map/pallas_call | solution.py:446
  280.3 2.6 copy.34
  282.9 10.4 %all-to-all-done.6 = f32[128,16,128]{2,1,0:T(8,128)} async-done(((f32[128,16,128]{2,1,0:T(8,128)}), f32[128,16,128]{2,1,0:T(8,128)}, u32[]{:S(2)}, u32[]{:S(2)}) %all-to-all-start.6) | async-done | bytes 1048608 | tf_op jit(solution)/shard_map/all_to_all | solution.py:459
  (64 shorter events, 17.6 us)
Async XLA Ops:
  7.2 17.2 %copy-start.5 = (bf16[512,1280]{1,0:T(8,128)(2,1)S(1)}, bf16[512,1280]{1,0:T(8,128)(2,1)}, u32[]{:S(2)}) copy-start(bf16[512,1280]{1,0:T(8,128)(2,1)} %param.11) | copy-start | bytes 3932164
  7.2 15.0 %copy-start.7 = (bf16[128,2,1280]{2,1,0:T(2,128)(2,1)S(1)}, bf16[128,2,1280]{2,1,0:T(2,128)(2,1)}, u32[]{:S(2)}) copy-start(bf16[128,2,1280]{2,1,0:T(2,128)(2,1)} %param.7) | copy-start | bytes 1966084
  7.2 16.0 %copy-start.12 = (f32[1280]{0:T(1024)S(1)}, f32[1280]{0:T(1024)}, u32[]{:S(2)}) copy-start(f32[1280]{0:T(1024)} %param.8) | copy-start | bytes 15364
  7.2 16.5 %copy-start.13 = (f32[1280]{0:T(1024)S(1)}, f32[1280]{0:T(1024)}, u32[]{:S(2)}) copy-start(f32[1280]{0:T(1024)} %param.9) | copy-start | bytes 15364
  7.2 23.4 %collective-permute-start.2 = (bf16[640,3072]{1,0:T(8,128)(2,1)}, bf16[640,3072]{1,0:T(8,128)(2,1)}, u32[]{:S(2)}, u32[]{:S(2)}) collective-permute-start(bf16[640,3072]{1,0:T(8,128)(2,1)} %mine_ref.1), channel_id=1, source_target_pairs={{0,1},{1,0},{2,3},{3,2},{4,5},{5,4},{6,7},{7,6},{8,9},{9,8},{10,11... | collective-permute-start | bytes 11796488 | tf_op jit(solution)/shard_map/ppermute | solution.py:455
  8.7 15.7 %collective-permute-start.1 = (bf16[512,1280]{1,0:T(8,128)(2,1)}, bf16[512,1280]{1,0:T(8,128)(2,1)S(1)}, u32[]{:S(2)}, u32[]{:S(2)}) collective-permute-start(bf16[512,1280]{1,0:T(8,128)(2,1)} %param.11), channel_id=1, source_target_pairs={{0,1},{1,0},{2,3},{3,2},{4,5},{5,4},{6,7},{7,6},{8,9},{9,8},{10,11... | collective-permute-start | bytes 3932168 | tf_op jit(solution)/shard_map/ppermute | solution.py:455
  13.1 17.5 %all-to-all-start = ((f32[32,8,128]{2,1,0:T(8,128)}), f32[32,8,128]{2,1,0:T(8,128)S(1)}, u32[]{:S(2)}, u32[]{:S(2)}) async-start(f32[32,8,128]{2,1,0:T(8,128)} %shard_map.93), calls=%async_computation | async-start | bytes 262144 | tf_op jit(solution)/shard_map/all_to_all | solution.py:459
  39.7 7.9 %copy-start = (bf16[128,2,1280]{2,0,1:T(8,128)(2,1)S(1)}, bf16[128,2,1280]{2,0,1:T(8,128)(2,1)}, u32[]{:S(2)}) copy-start(bf16[128,2,1280]{2,0,1:T(8,128)(2,1)} %copy.38) | copy-start | bytes 1966084
  39.7 39.9 %all-to-all-start.1 = ((bf16[32,256,128]{2,1,0:T(8,128)(2,1)}), bf16[32,256,128]{2,1,0:T(8,128)(2,1)S(1)}, u32[]{:S(2)}, u32[]{:S(2)}) async-start(bf16[32,256,128]{2,1,0:T(8,128)(2,1)} %bitcast.42), calls=%async_computation.1 | async-start | bytes 4194304 | tf_op jit(solution)/shard_map/all_to_all | solution.py:459
  47.6 126.4 %all-gather.2.cloned.1.call-start = ((), (), s32[]{:S(2)}) async-start(), calls=%async_computation.7 | async-start | bytes 11141120 | tf_op jit(solution)/shard_map/all_gather | solution.py:484
  47.7 31.0 %collective-permute-start = (bf16[128,1280]{1,0:T(8,128)(2,1)S(1)}, bf16[128,1280]{1,0:T(8,128)(2,1)S(1)}, u32[]{:S(2)}, u32[]{:S(2)}) collective-permute-start(bf16[128,1280]{1,0:T(8,128)(2,1)S(1)} %get-tuple-element.59), channel_id=1, source_target_pairs={{0,4},{4,0},{1,5},{5,1},{2,6},{6,2},{3,7},{7,3},{8,12},{12,8},{9,1... | collective-permute-start | bytes 983048 | tf_op jit(solution)/shard_map/ppermute | solution.py:455
  79.6 1.3 copy-start.4
  80.9 92.4 %copy-start.11 = (f32[8,1280]{1,0:T(8,128)S(1)}, f32[8,1280]{1,0:T(8,128)}, u32[]{:S(2)}) copy-start(f32[8,1280]{1,0:T(8,128)} %get-tuple-element.28.chan_ref) | copy-start | bytes 122884
  163.9 24.9 %all-to-all-start.2 = ((bf16[32,128,128]{2,1,0:T(8,128)(2,1)}), bf16[32,128,128]{2,1,0:T(8,128)(2,1)S(1)}, u32[]{:S(2)}, u32[]{:S(2)}) async-start(bf16[32,128,128]{2,1,0:T(8,128)(2,1)} %get-tuple-element.25.dqo_ref), calls=%async_computation.2 | async-start | bytes 2097152 | tf_op jit(solution)/shard_map/all_to_all | solution.py:459
  174.0 19.2 %copy-start.1 = (bf16[128,2,1280]{2,0,1:T(8,128)(2,1)S(1)}, bf16[128,2,1280]{2,0,1:T(8,128)(2,1)}, u32[]{:S(2)}) copy-start(bf16[128,2,1280]{2,0,1:T(8,128)(2,1)} %copy.37) | copy-start | bytes 1966084
  188.8 7.4 %copy-start.2 = (bf16[32,128,128]{2,1,0:T(8,128)(2,1)}, bf16[32,128,128]{2,1,0:T(8,128)(2,1)S(1)}, u32[]{:S(2)}) copy-start(bf16[32,128,128]{2,1,0:T(8,128)(2,1)S(1)} %all-to-all-done.2) | copy-start | bytes 3145732
  188.8 20.3 %all-to-all-start.3 = ((bf16[32,128,128]{2,1,0:T(8,128)(2,1)}), bf16[32,128,128]{2,1,0:T(8,128)(2,1)S(1)}, u32[]{:S(2)}, u32[]{:S(2)}) async-start(bf16[32,128,128]{2,1,0:T(8,128)(2,1)} %get-tuple-element.31.dkv_ref), calls=%async_computation.3 | async-start | bytes 2097152 | tf_op jit(solution)/shard_map/all_to_all | solution.py:459
  193.2 7.2 %collective-permute-start.4 = (bf16[2,128,1280]{2,1,0:T(8,128)(2,1)S(1)}, bf16[2,128,1280]{2,1,0:T(8,128)(2,1)S(1)}, u32[]{:S(2)}, u32[]{:S(2)}) collective-permute-start(bf16[2,128,1280]{2,1,0:T(8,128)(2,1)S(1)} %bitcast.37), channel_id=1, source_target_pairs={{0,1},{1,0},{2,3},{3,2},{4,5},{5,4},{6,7},{7,6},{8,9},{9,8},{10,11... | collective-permute-start | bytes 1966088 | tf_op jit(solution)/shard_map/ppermute | solution.py:455
  200.3 2.1 collective-permute-start.3
  200.4 2.1 copy-start.6
  209.1 1.0 copy-start.3
  210.0 45.0 %all-to-all-start.4 = ((f32[64,8,1280]{2,1,0:T(8,128)}), f32[64,8,1280]{2,1,0:T(8,128)S(1)}, u32[]{:S(2)}, u32[]{:S(2)}) async-start(f32[64,8,1280]{2,1,0:T(8,128)} %shard_map.99), calls=%async_computation.4 | async-start | bytes 5242880 | tf_op jit(solution)/shard_map/all_to_all | solution.py:459
  227.7 46.7 %copy-start.8 = (bf16[2,128,1280]{2,1,0:T(8,128)(2,1)S(1)}, bf16[2,128,1280]{2,1,0:T(8,128)(2,1)}, u32[]{:S(2)}) copy-start(bf16[2,128,1280]{2,1,0:T(8,128)(2,1)} %get-tuple-element.30) | copy-start | bytes 1966084
  267.1 26.1 %all-to-all-start.6 = ((f32[128,16,128]{2,1,0:T(8,128)}), f32[128,16,128]{2,1,0:T(8,128)}, u32[]{:S(2)}, u32[]{:S(2)}) async-start(f32[128,16,128]{2,1,0:T(8,128)} %shard_map.97), calls=%async_computation.6 | async-start | bytes 2097152 | tf_op jit(solution)/shard_map/all_to_all | solution.py:459
  (2 other events, 1.5 us)
Sparse Core Ops, SparseCore 0:
  79.7 84.9 all-gather.1

commit v3 on v2

--- a/solution.py
+++ b/solution.py
@@ -385,8 +385,74 @@
     )(own, att, att_far, cot, cot_far)
 
 
-def back_kernel(own_ref, dqo_ref, dkv_ref, mine_ref, other_ref, lat_ref, chan_ref, gain_ref, grad_ref, sums_ref, rows_ref):
-    own = own_ref[0]
+def place():
+    return tuple(lax.axis_index(axis) for axis in ALL)
+
+
+def shifted(here, k, sign):
+    dy, dz, dx, dr = k // 16, (k // 4) % 4, (k // 2) % 2, k % 2
+    y = (here[0] + (dy if sign > 0 else 4 - dy)) % 4
+    z = (here[1] + (dz if sign > 0 else 4 - dz)) % 4
+    x = (here[2] + dx) % 2
+    r = (here[3] + dr) % 2
+    return {"y": y, "z": z, "xl": x, "rep": r}, ((y * 4 + z) * 2 + x) * 2 + r
+
+
+def tail_kernel(
+    count, part_ref, dqo_ref, dkv_ref, mine_ref, other_ref, lat_ref, cot_ref, chan_ref, gain_ref,
+    out_ref, weight_ref, rows_ref, grad_ref, near_ref, far_ref, got_ref,
+    part_send, part_recv, sums_send, sums_recv,
+):
+    here = place()
+    own = here[4]
+    lines, seqs = part_ref.shape[0], far_ref.shape[0]
+    block = ((here[0] * 4 + here[1]) * 2 + here[2]) * 2 + here[3]
+    line = block // 2
+
+    barrier = pltpu.get_barrier_semaphore()
+
+    @pl.loop(1, lines)
+    def _(k):
+        pl.semaphore_signal(barrier, inc=1, device_id=shifted(here, k, 1)[0], device_id_type=pl.DeviceIdType.MESH)
+
+    pl.semaphore_wait(barrier, lines - 1)
+
+    def part_copy(k):
+        target, there = shifted(here, k, 1)
+        return pltpu.make_async_remote_copy(
+            src_ref=part_ref.at[there], dst_ref=got_ref.at[block],
+            send_sem=part_send.at[k], recv_sem=part_recv.at[k],
+            device_id=target, device_id_type=pl.DeviceIdType.MESH,
+        )
+
+    def part_arrival(k):
+        source, there = shifted(here, k, -1)
+        return pltpu.make_async_remote_copy(
+            src_ref=part_ref.at[there], dst_ref=got_ref.at[there],
+            send_sem=part_send.at[k], recv_sem=part_recv.at[k],
+            device_id=source, device_id_type=pl.DeviceIdType.MESH,
+        )
+
+    def sums_copy(k):
+        target, _ = shifted(here, 2 * k, 1)
+        return pltpu.make_async_remote_copy(
+            src_ref=near_ref, dst_ref=far_ref.at[line],
+            send_sem=sums_send.at[k], recv_sem=sums_recv.at[k],
+            device_id=target, device_id_type=pl.DeviceIdType.MESH,
+        )
+
+    def sums_arrival(k):
+        source, there = shifted(here, 2 * k, -1)
+        return pltpu.make_async_remote_copy(
+            src_ref=near_ref, dst_ref=far_ref.at[there // 2],
+            send_sem=sums_send.at[k], recv_sem=sums_recv.at[k],
+            device_id=source, device_id_type=pl.DeviceIdType.MESH,
+        )
+
+    @pl.loop(1, lines)
+    def _(k):
+        part_copy(k).start()
+
     inner, half = HEADS * HEAD, mine_ref.shape[0]
     low = lax.broadcasted_iota(jnp.int32, (128, 128), 1) < HEAD
     for h in range(0, HEADS, 2):
@@ -409,46 +475,60 @@
         centred = (lat_ref[i].astype(F32) - chan_ref[i : i + 1]) * chan_ref[2 + i : 3 + i]
         ones.append(jnp.sum(grad, axis=0, keepdims=True))
         twos.append(jnp.sum(grad * centred, axis=0, keepdims=True))
-    sums_ref[...] = jnp.broadcast_to(by_group(four_rows(ones + twos), members(lat_ref.shape[2]))[None], sums_ref.shape)
-
-
-def back(own, dqo, dkv, mine, other, lat, chan, gain, copies):
-    def whole(shape):
-        return pl.BlockSpec(shape, lambda s, own: (0,) * len(shape), pipeline_mode=pl.Buffered(1))
-
-    operands = (dqo, dkv, mine, other, lat, chan, gain)
-    return pl.pallas_call(
-        back_kernel,
-        grid_spec=pltpu.PrefetchScalarGridSpec(
-            num_scalar_prefetch=1,
-            grid=(1,),
-            in_specs=[whole(a.shape) for a in operands],
-            out_specs=[whole(lat.shape), whole((copies, 8, 128))],
-            scratch_shapes=[pltpu.VMEM((256, 3 * HEADS * HEAD), BF16)],
-        ),
-        out_shape=[jax.ShapeDtypeStruct(lat.shape, F32), jax.ShapeDtypeStruct((copies, 8, 128), F32)],
-        compiler_params=pltpu.CompilerParams(vmem_limit_bytes=VMEM),
-        cost_estimate=pl.CostEstimate(flops=2 * 256 * 1280 * 3072, bytes_accessed=14 << 20, transcendentals=0),
-    )(own, *operands)
-
-
-def final_kernel(count, grad_ref, sums_ref, lat_ref, cot_ref, chan_ref, out_ref):
     table = members(lat_ref.shape[2])
-    means = by_channel(jnp.sum(sums_ref[...], axis=0) / count, table)
+    sums = by_group(four_rows(ones + twos), table)
+    near_ref[...] = sums
+    far_ref[line] = sums
+
+    @pl.loop(1, seqs)
+    def _(k):
+        sums_copy(k).start()
+
+    got_ref[block] = part_ref[block]
+
+    @pl.loop(1, seqs)
+    def _(k):
+        sums_arrival(k).wait_recv()
+
+    means = by_channel(jnp.sum(far_ref[...], axis=0) / count, table)
     for i in range(2):
         inv = chan_ref[2 + i : 3 + i]
         centred = (lat_ref[i].astype(F32) - chan_ref[i : i + 1]) * inv
         grad = inv * (grad_ref[i] - means[i : i + 1] - centred * means[2 + i : 3 + i])
         out_ref[i] = (cot_ref[i].astype(F32) + grad).astype(BF16)
 
-
-def final(grad, sums, lat, cot, chan, count):
-    return pl.pallas_call(
-        functools.partial(final_kernel, count),
-        out_shape=jax.ShapeDtypeStruct(lat.shape, BF16),
-        compiler_params=pltpu.CompilerParams(vmem_limit_bytes=VMEM),
-        cost_estimate=pl.CostEstimate(flops=4 << 20, bytes_accessed=4 << 20, transcendentals=0),
-    )(grad, sums, lat, cot, chan)
+    @pl.loop(1, lines)
+    def _(k):
+        part_arrival(k).wait_recv()
+
+    weight_ref[...] = jnp.sum(got_ref[...], axis=0)
+
+    @pl.loop(1, lines)
+    def _(k):
+        part_copy(k).wait_send()
+
+    @pl.loop(1, seqs)
+    def _(k):
+        sums_copy(k).wait_send()
+
+
+def tail(part, dqo, dkv, mine, other, lat, cot, chan, gain, count):
+    lines, channels = part.shape[0], part.shape[2]
+    dma = pltpu.SemaphoreType.DMA
+    return pl.pallas_call(
+        functools.partial(tail_kernel, count),
+        out_shape=[jax.ShapeDtypeStruct(lat.shape, BF16), jax.ShapeDtypeStruct((8, channels), F32)],
+        scratch_shapes=[
+            pltpu.VMEM((256, 3 * HEADS * HEAD), BF16),
+            pltpu.VMEM(lat.shape, F32),
+            pltpu.VMEM((8, 128), F32),
+            pltpu.VMEM((lines // 2, 8, 128), F32),
+            pltpu.VMEM(part.shape, F32),
+            dma((lines,)), dma((lines,)), dma((lines // 2,)), dma((lines // 2,)),
+        ],
+        compiler_params=pltpu.CompilerParams(vmem_limit_bytes=VMEM, collective_id=1, has_side_effects=True),
+        cost_estimate=pl.CostEstimate(flops=2 << 34, bytes_accessed=16 << 20, transcendentals=0),
+    )(part, dqo, dkv, mine, other, lat, cot, chan, gain)
 
 
 def swapped(value, axis):
@@ -493,16 +573,13 @@
     dqo_tok = dqo_tok.reshape(HEADS, images, 128, 128)
     mixed, att = mix(own, dqo_tok, lat, halves_out)
     out_part = out_weight(own, att, swapped(att, "own"), cot, cot_far)
-    dkv_tok, out_part = lax.optimization_barrier((dkv_tok, out_part))
-    out_blocks = exchanged(out_part, LINE)
+    dkv_tok, out_part, in_part = lax.optimization_barrier((dkv_tok, out_part, in_part))
+    in_blocks = exchanged(in_part, ALL)
     dkv_tok = dkv_tok.reshape(HEADS, images, 128, 128)
-    grad, back_sums = back(own, dqo_tok, dkv_tok, proj_qkv, other_qkv, lat, chan, gain, seq_count)
-    out_blocks, back_sums = lax.optimization_barrier((out_blocks, back_sums))
-    back_sums, in_part = lax.optimization_barrier((exchanged(back_sums, SEQ), in_part))
-    in_blocks = exchanged(in_part, ALL)
-    grad_latent = final(grad, back_sums, lat, cot, chan, count)
-
-    grad_out = jnp.sum(out_blocks, axis=0)
+    grad_latent, grad_out = tail(
+        out_part, dqo_tok, dkv_tok, proj_qkv, other_qkv, lat, cot, chan, gain, count
+    )
+
     summed = jnp.sum(in_blocks.reshape(HEADS, 8, 16, 128), axis=1)
     dq = summed[:, 10:15].reshape(HEADS, 5, 2, HEAD).transpose(2, 1, 0, 3).reshape(10, HEADS * HEAD)
     dk = summed[:, :10, :HEAD].transpose(1, 0, 2).reshape(10, HEADS * HEAD)

time: 304 us -> 293 us (0.964)
  Pallas kernels: 131 us -> 178 us
  waiting for transfers between devices: 73.3 us -> 32.9 us
  blocking collectives: 12.1 us -> 0 us
  starting transfers between devices: 53.2 us -> 45.9 us
    pallas_call x2 -> x1, Pallas kernels: 11.9 us -> 58.4 us  [tail(): pl.pallas_call(functools.partial(tail_kernel, count), out_shape=[jax.Shap...]
    all_to_all x6 -> x5, waiting for transfers between devices: 41.5 us -> 3.24 us  [exchanged(): return lax.all_to_all(value, axes, 0, 0, tiled=True)]
    all_to_all x1 -> x0, blocking collectives: 12.1 us -> none  [exchanged(): return lax.all_to_all(value, axes, 0, 0, tiled=True)]
    all_to_all x6 -> x5, starting transfers between devices: 47.3 us -> 39.9 us  [exchanged(): return lax.all_to_all(value, axes, 0, 0, tiled=True)]
    unnamed x32 -> x33, local copies, waits for them, and re-layouts: 10.8 us -> 12.3 us
  transfers between devices with their start and end apart: 12 -> 11, of which waited for: 6 -> 2; matrix products, arithmetic and copies ran while one was open for 4% -> 4% of each run, Pallas kernels for 41% -> 59%
where the time goes in v3:
time: 293 us; the launch traced here: 289 us
  Pallas kernels  178 us (61%)
  starting transfers between devices  45.9 us (16%)
  waiting for transfers between devices  32.9 us (11%)
  between operations  14.3 us (5%)
  local copies, waits for them, and re-layouts  14.1 us (5%)
  other arithmetic  4.03 us (1%)
    pallas_call x1, Pallas kernels, attention(): pl.pallas_call(functools.partial(attention_kernel, ck), grid=(sources //...  83 us
    pallas_call x1, Pallas kernels, tail(): pl.pallas_call(functools.partial(tail_kernel, count), out_shape=[jax.Shap...  58.4 us
    all_to_all x5, starting transfers between devices, exchanged(): return lax.all_to_all(value, axes, 0, 0, tiled=True)  39.9 us
    ppermute x5, waiting for transfers between devices, swapped(): return lax.ppermute(value, axis, [(0, 1), (1, 0)])  29.7 us
    unnamed x33, local copies, waits for them, and re-layouts  12.3 us
    pallas_call x1, Pallas kernels, in_weight(): pl.pallas_call(in_weight_kernel, grid=(sources // here,), in_specs=[pl.Bl...  11.6 us
    pallas_call x1, Pallas kernels, project(): pl.pallas_call(functools.partial(project_kernel, count), grid_spec=pltpu....  8.39 us
    ppermute x5, starting transfers between devices, swapped(): return lax.ppermute(value, axis, [(0, 1), (1, 0)])  5.87 us
  transfers between devices with their start and end apart: 11, of which 2 were waited for; matrix products, arithmetic and copies ran while one was open for 4% of the time, Pallas kernels for 59%

profile of v3, /device:TPU:1, one launch (start us, length us, event | category | flops | bytes accessed | tf_op | source)
XLA Modules:
  0.0 288.9 jit_solution(5056973410173879938)
XLA Ops:
  7.2 1.5 collective-permute-start.2
  8.8 2.0 copy.38
  10.8 2.3 shard_map.93
  13.1 9.1 %all-to-all-start = ((f32[32,8,128]{2,1,0:T(8,128)}), f32[32,8,128]{2,1,0:T(8,128)S(1)}, u32[]{:S(2)}, u32[]{:S(2)}) async-start(f32[32,8,128]{2,1,0:T(8,128)} %shard_map.93), calls=%async_computation | async-start | bytes 262144 | tf_op jit(solution)/shard_map/all_to_all | solution.py:539
  24.3 1.7 pad_maximum_fusion.w_ref
  26.0 4.6 %shard_map.94.g_ref = bf16[16,2,64,128]{3,2,1,0:T(8,128)(2,1)} custom-call(s32[1]{0:T(128)} %bitcast.own_ref, bf16[2,128,1280]{2,1,0:T(8,128)(2,1)} %bitcast.33, bf16[2,512,1280]{2,1,0:T(8,128)(2,1)} %pad_maximum_fusion.w_ref), custom_call_target="tpu_custom_call" | custom-call | flops 671088640 | bytes 4194304 | tf_op jit(solution)/shard_map/pallas_call | solution.py:151
  31.3 8.4 %shard_map.95 = (bf16[16,2,256,128]{3,2,1,0:T(8,128)(2,1)}, f32[8,1280]{1,0:T(8,128)}) custom-call(s32[1]{0:T(128)} %bitcast.own_ref, bf16[2,128,1280]{2,1,0:T(8,128)(2,1)} %bitcast.29, f32[32,8,128]{2,1,0:T(8,128)} %copy-done.8, f32[1,1280]{1,0:T(1,128)} %reshape.44.gain_ref, f32[1,1280]{1,0:T(1,128)} %reshape.45.shift_ref, ...), custom_call_target="tpu_custom_call" | custom-call | flops 2013265920 | bytes 12582912 | tf_op jit(solution)/shard_map/pallas_call | solution.py:115
  39.7 7.9 %all-to-all-start.1 = ((bf16[32,256,128]{2,1,0:T(8,128)(2,1)}), bf16[32,256,128]{2,1,0:T(8,128)(2,1)S(1)}, u32[]{:S(2)}, u32[]{:S(2)}) async-start(bf16[32,256,128]{2,1,0:T(8,128)(2,1)} %bitcast.39), calls=%async_computation.1 | async-start | bytes 4194304 | tf_op jit(solution)/shard_map/all_to_all | solution.py:539
  47.7 1.3 collective-permute-start
  49.0 29.7 %collective-permute-done = bf16[128,1280]{1,0:T(8,128)(2,1)S(1)} collective-permute-done((bf16[128,1280]{1,0:T(8,128)(2,1)S(1)}, bf16[128,1280]{1,0:T(8,128)(2,1)S(1)}, u32[]{:S(2)}, u32[]{:S(2)}) %collective-permute-start) | collective-permute-done | bytes 327712 | tf_op jit(solution)/shard_map/ppermute | solution.py:535
  78.7 0.9 maximum_select_fusion
  79.6 1.3 copy-done.3
  80.9 83.0 %shard_map.96 = (bf16[32,128,128]{2,1,0:T(8,128)(2,1)}, bf16[32,128,128]{2,1,0:T(8,128)(2,1)}) custom-call(bf16[32,256,128]{2,1,0:T(8,128)(2,1)} %copy-done.3), custom_call_target="tpu_custom_call" | custom-call | flops 51539607552 | bytes 4194304 | tf_op jit(solution)/shard_map/pallas_call | solution.py:239
  163.9 9.4 %all-to-all-start.2 = ((bf16[32,128,128]{2,1,0:T(8,128)(2,1)}), bf16[32,128,128]{2,1,0:T(8,128)(2,1)S(1)}, u32[]{:S(2)}, u32[]{:S(2)}) async-start(bf16[32,128,128]{2,1,0:T(8,128)(2,1)} %get-tuple-element.22.dqo_ref), calls=%async_computation.2 | async-start | bytes 2097152 | tf_op jit(solution)/shard_map/all_to_all | solution.py:539
  174.0 11.6 %shard_map.97 = f32[128,16,128]{2,1,0:T(8,128)} custom-call(bf16[32,128,1280]{2,1,0:T(8,128)(2,1)} %all-gather.2.cloned.1.call-done.lat_ref, f32[2,1280]{1,0:T(2,128)} %broadcast_select_fusion.1.chan_ref, f32[1,1280]{1,0:T(1,128)} %reshape.44.gain_ref, f32[1,1280]{1,0:T(1,128)} %reshape.45.shift_ref, bf16[32,128,128]{2,1,0:T(8,128)(2,1)} %get-tuple-element.22.dqo_ref, ...), custom_call_target="tpu_custom_call" | custom-call | flops 2684354560 | bytes 14680064 | tf_op jit(solution)/shard_map/pallas_call | solution.py:295
  185.6 3.2 %all-to-all-done.2 = bf16[32,128,128]{2,1,0:T(8,128)(2,1)S(1)} async-done(((bf16[32,128,128]{2,1,0:T(8,128)(2,1)}), bf16[32,128,128]{2,1,0:T(8,128)(2,1)S(1)}, u32[]{:S(2)}, u32[]{:S(2)}) %all-to-all-start.2) | async-done | bytes 1048608 | tf_op jit(solution)/shard_map/all_to_all | solution.py:539
  188.8 4.3 %all-to-all-start.3 = ((bf16[32,128,128]{2,1,0:T(8,128)(2,1)}), bf16[32,128,128]{2,1,0:T(8,128)(2,1)S(1)}, u32[]{:S(2)}, u32[]{:S(2)}) async-start(bf16[32,128,128]{2,1,0:T(8,128)(2,1)} %get-tuple-element.28.dkv_ref), calls=%async_computation.3 | async-start | bytes 2097152 | tf_op jit(solution)/shard_map/all_to_all | solution.py:539
  193.1 3.0 %collective-permute-start.4 = (bf16[2,128,1280]{2,1,0:T(8,128)(2,1)S(1)}, bf16[2,128,1280]{2,1,0:T(8,128)(2,1)S(1)}, u32[]{:S(2)}, u32[]{:S(2)}) collective-permute-start(bf16[2,128,1280]{2,1,0:T(8,128)(2,1)S(1)} %bitcast.36), channel_id=1, source_target_pairs={{0,1},{1,0},{2,3},{3,2},{4,5},{5,4},{6,7},{7,6},{8,9},{9,8},{10,11... | collective-permute-start | bytes 1966088 | tf_op jit(solution)/shard_map/ppermute | solution.py:535
  196.1 4.2 %shard_map.98 = (bf16[2,128,1280]{2,1,0:T(8,128)(2,1)}, bf16[2,128,1024]{2,1,0:T(8,128)(2,1)}) custom-call(s32[1]{0:T(128)} %bitcast.own_ref, bf16[16,2,128,128]{3,2,1,0:T(8,128)(2,1)} %bitcast.37, bf16[2,128,1280]{2,1,0:T(8,128)(2,1)} %bitcast.30, bf16[2,512,1280]{2,1,0:T(8,128)(2,1)} %pad_maximum_fusion.w_ref), custom_call_target="tpu_custom_call" | custom-call | flops 671088640 | bytes 6291456 | tf_op jit(solution)/shard_map/pallas_call | solution.py:341
  200.3 2.6 copy.33
  204.5 5.2 %shard_map.99.part_ref = f32[64,8,1280]{2,1,0:T(8,128)} custom-call(s32[1]{0:T(128)} %bitcast.own_ref, bf16[2,128,1024]{2,1,0:T(8,128)(2,1)} %get-tuple-element.29.att_ref, bf16[2,128,1024]{2,1,0:T(8,128)(2,1)} %copy-done.9, bf16[2,128,1280]{2,1,0:T(8,128)(2,1)} %bitcast.34, bf16[2,128,1280]{2,1,0:T(8,128)(2,1)} %copy-done.6), custom_call_target="tpu_custom_call" | custom-call | flops 1342177280 | bytes 6291456 | tf_op jit(solution)/shard_map/pallas_call | solution.py:374
  209.8 9.2 %all-to-all-start.4 = ((f32[128,16,128]{2,1,0:T(8,128)}), f32[128,16,128]{2,1,0:T(8,128)S(1)}, u32[]{:S(2)}, u32[]{:S(2)}) async-start(f32[128,16,128]{2,1,0:T(8,128)} %shard_map.97), calls=%async_computation.4 | async-start | bytes 2097152 | tf_op jit(solution)/shard_map/all_to_all | solution.py:539
  219.0 58.4 %shard_map.100 = (bf16[2,128,1280]{2,1,0:T(8,128)(2,1)}, f32[8,1280]{1,0:T(8,128)}) custom-call(f32[64,8,1280]{2,1,0:T(8,128)} %shard_map.99.part_ref, bf16[16,2,128,128]{3,2,1,0:T(8,128)(2,1)} %bitcast.38, bf16[16,2,128,128]{3,2,1,0:T(8,128)(2,1)} %bitcast.42, bf16[640,3072]{1,0:T(8,128)(2,1)} %mine_ref.1, ...), custom_call_target="tpu_custom_call" | custom-call | flops 34359738368 | bytes 16777216 | tf_op jit(solution)/shard_map/pallas_call | solution.py:518
  277.5 2.6 copy.34
  (60 shorter events, 7.2 us)
Async XLA Ops:
  7.2 17.2 %copy-start.4 = (bf16[512,1280]{1,0:T(8,128)(2,1)S(1)}, bf16[512,1280]{1,0:T(8,128)(2,1)}, u32[]{:S(2)}) copy-start(bf16[512,1280]{1,0:T(8,128)(2,1)} %param.11) | copy-start | bytes 3932164
  7.2 15.0 %copy-start.7 = (bf16[128,2,1280]{2,1,0:T(2,128)(2,1)S(1)}, bf16[128,2,1280]{2,1,0:T(2,128)(2,1)}, u32[]{:S(2)}) copy-start(bf16[128,2,1280]{2,1,0:T(2,128)(2,1)} %param.7) | copy-start | bytes 1966084
  7.2 15.9 %copy-start.12 = (f32[1280]{0:T(1024)S(1)}, f32[1280]{0:T(1024)}, u32[]{:S(2)}) copy-start(f32[1280]{0:T(1024)} %param.8) | copy-start | bytes 15364
  7.2 16.5 %copy-start.13 = (f32[1280]{0:T(1024)S(1)}, f32[1280]{0:T(1024)}, u32[]{:S(2)}) copy-start(f32[1280]{0:T(1024)} %param.9) | copy-start | bytes 15364
  7.2 23.4 %collective-permute-start.2 = (bf16[640,3072]{1,0:T(8,128)(2,1)}, bf16[640,3072]{1,0:T(8,128)(2,1)}, u32[]{:S(2)}, u32[]{:S(2)}) collective-permute-start(bf16[640,3072]{1,0:T(8,128)(2,1)} %mine_ref.1), channel_id=1, source_target_pairs={{0,1},{1,0},{2,3},{3,2},{4,5},{5,4},{6,7},{7,6},{8,9},{9,8},{10,11... | collective-permute-start | bytes 11796488 | tf_op jit(solution)/shard_map/ppermute | solution.py:535
  8.7 15.7 %collective-permute-start.1 = (bf16[512,1280]{1,0:T(8,128)(2,1)}, bf16[512,1280]{1,0:T(8,128)(2,1)S(1)}, u32[]{:S(2)}, u32[]{:S(2)}) collective-permute-start(bf16[512,1280]{1,0:T(8,128)(2,1)} %param.11), channel_id=1, source_target_pairs={{0,1},{1,0},{2,3},{3,2},{4,5},{5,4},{6,7},{7,6},{8,9},{9,8},{10,11... | collective-permute-start | bytes 3932168 | tf_op jit(solution)/shard_map/ppermute | solution.py:535
  13.1 17.5 %all-to-all-start = ((f32[32,8,128]{2,1,0:T(8,128)}), f32[32,8,128]{2,1,0:T(8,128)S(1)}, u32[]{:S(2)}, u32[]{:S(2)}) async-start(f32[32,8,128]{2,1,0:T(8,128)} %shard_map.93), calls=%async_computation | async-start | bytes 262144 | tf_op jit(solution)/shard_map/all_to_all | solution.py:539
  39.7 7.9 %copy-start = (bf16[128,2,1280]{2,0,1:T(8,128)(2,1)S(1)}, bf16[128,2,1280]{2,0,1:T(8,128)(2,1)}, u32[]{:S(2)}) copy-start(bf16[128,2,1280]{2,0,1:T(8,128)(2,1)} %copy.38) | copy-start | bytes 1966084
  39.7 39.9 %all-to-all-start.1 = ((bf16[32,256,128]{2,1,0:T(8,128)(2,1)}), bf16[32,256,128]{2,1,0:T(8,128)(2,1)S(1)}, u32[]{:S(2)}, u32[]{:S(2)}) async-start(bf16[32,256,128]{2,1,0:T(8,128)(2,1)} %bitcast.39), calls=%async_computation.1 | async-start | bytes 4194304 | tf_op jit(solution)/shard_map/all_to_all | solution.py:539
  47.6 126.4 %all-gather.2.cloned.1.call-start = ((), (), s32[]{:S(2)}) async-start(), calls=%async_computation.5 | async-start | bytes 11141120 | tf_op jit(solution)/shard_map/all_gather | solution.py:564
  47.7 31.0 %collective-permute-start = (bf16[128,1280]{1,0:T(8,128)(2,1)S(1)}, bf16[128,1280]{1,0:T(8,128)(2,1)S(1)}, u32[]{:S(2)}, u32[]{:S(2)}) collective-permute-start(bf16[128,1280]{1,0:T(8,128)(2,1)S(1)} %get-tuple-element.53), channel_id=1, source_target_pairs={{0,4},{4,0},{1,5},{5,1},{2,6},{6,2},{3,7},{7,3},{8,12},{12,8},{9,1... | collective-permute-start | bytes 983048 | tf_op jit(solution)/shard_map/ppermute | solution.py:535
  79.6 1.3 copy-start.3
  80.9 92.4 %copy-start.11 = (f32[8,1280]{1,0:T(8,128)S(1)}, f32[8,1280]{1,0:T(8,128)}, u32[]{:S(2)}) copy-start(f32[8,1280]{1,0:T(8,128)} %get-tuple-element.25.chan_ref) | copy-start | bytes 122884
  163.9 24.9 %all-to-all-start.2 = ((bf16[32,128,128]{2,1,0:T(8,128)(2,1)}), bf16[32,128,128]{2,1,0:T(8,128)(2,1)S(1)}, u32[]{:S(2)}, u32[]{:S(2)}) async-start(bf16[32,128,128]{2,1,0:T(8,128)(2,1)} %get-tuple-element.22.dqo_ref), calls=%async_computation.2 | async-start | bytes 2097152 | tf_op jit(solution)/shard_map/all_to_all | solution.py:539
  174.0 19.2 %copy-start.1 = (bf16[128,2,1280]{2,0,1:T(8,128)(2,1)S(1)}, bf16[128,2,1280]{2,0,1:T(8,128)(2,1)}, u32[]{:S(2)}) copy-start(bf16[128,2,1280]{2,0,1:T(8,128)(2,1)} %copy.37) | copy-start | bytes 1966084
  188.8 7.4 %copy-start.2 = (bf16[32,128,128]{2,1,0:T(8,128)(2,1)}, bf16[32,128,128]{2,1,0:T(8,128)(2,1)S(1)}, u32[]{:S(2)}) copy-start(bf16[32,128,128]{2,1,0:T(8,128)(2,1)S(1)} %all-to-all-done.2) | copy-start | bytes 3145732
  188.8 21.0 %all-to-all-start.3 = ((bf16[32,128,128]{2,1,0:T(8,128)(2,1)}), bf16[32,128,128]{2,1,0:T(8,128)(2,1)S(1)}, u32[]{:S(2)}, u32[]{:S(2)}) async-start(bf16[32,128,128]{2,1,0:T(8,128)(2,1)} %get-tuple-element.28.dkv_ref), calls=%async_computation.3 | async-start | bytes 2097152 | tf_op jit(solution)/shard_map/all_to_all | solution.py:539
  193.1 9.8 %collective-permute-start.4 = (bf16[2,128,1280]{2,1,0:T(8,128)(2,1)S(1)}, bf16[2,128,1280]{2,1,0:T(8,128)(2,1)S(1)}, u32[]{:S(2)}, u32[]{:S(2)}) collective-permute-start(bf16[2,128,1280]{2,1,0:T(8,128)(2,1)S(1)} %bitcast.36), channel_id=1, source_target_pairs={{0,1},{1,0},{2,3},{3,2},{4,5},{5,4},{6,7},{7,6},{8,9},{9,8},{10,11... | collective-permute-start | bytes 1966088 | tf_op jit(solution)/shard_map/ppermute | solution.py:535
  200.3 2.6 collective-permute-start.3
  202.9 0.8 copy-start.6
  203.8 0.8 copy-start.9
  209.8 9.3 %copy-start.5 = (bf16[32,128,128]{2,1,0:T(8,128)(2,1)}, bf16[32,128,128]{2,1,0:T(8,128)(2,1)S(1)}, u32[]{:S(2)}) copy-start(bf16[32,128,128]{2,1,0:T(8,128)(2,1)S(1)} %all-to-all-done.3) | copy-start | bytes 3145732
  209.8 70.3 %all-to-all-start.4 = ((f32[128,16,128]{2,1,0:T(8,128)}), f32[128,16,128]{2,1,0:T(8,128)S(1)}, u32[]{:S(2)}, u32[]{:S(2)}) async-start(f32[128,16,128]{2,1,0:T(8,128)} %shard_map.97), calls=%async_computation.4 | async-start | bytes 2097152 | tf_op jit(solution)/shard_map/all_to_all | solution.py:539
  277.5 4.0 %copy-start.10 = (f32[8,1280]{1,0:T(8,128)S(1)}, f32[8,1280]{1,0:T(8,128)}, u32[]{:S(2)}) copy-start(f32[8,1280]{1,0:T(8,128)} %get-tuple-element.63) | copy-start | bytes 122884
  (1 other events, 0.7 us)
Sparse Core Ops, SparseCore 0:
  79.8 84.9 all-gather.1

commit v4 on v3

--- a/solution.py
+++ b/solution.py
@@ -67,69 +67,117 @@
     return jnp.concatenate([means[0:2], lax.rsqrt(var + 1e-06), jnp.zeros((4, 128), F32)], axis=0)
 
 
-def project_kernel(count, own_ref, lat_ref, sums_ref, gain_ref, shift_ref, g_ref, *refs):
-    mine, other = refs[0:3], refs[3:6]
-    out_ref, chan_ref, normed_ref = refs[6:]
-    own = own_ref[0]
-    half = mine[0].shape[0]
-
-    @pl.when(pl.program_id(0) == 0)
-    def _():
-        table = members(lat_ref.shape[2])
-        chan = by_channel(moments(jnp.sum(sums_ref[...], axis=0), count), table)
-        chan_ref[...] = chan
-        for i in range(2):
-            centred = (lat_ref[i].astype(F32) - chan[i : i + 1]) * chan[2 + i : 3 + i]
-            normed_ref[i * 128 : (i + 1) * 128] = (centred * gain_ref[...] + shift_ref[...]).astype(BF16)
-
-    out_ref[:, :, 192:256] = g_ref[...]
+def project_kernel(
+    count, lat_ref, sums_ref, gain_ref, shift_ref, g_ref, mine_ref, other_ref,
+    chan_ref, out_ref, normed_ref, send_ref, send_sem, recv_sem, keep_sem,
+):
+    here = place()
+    own = here[4]
+    half = mine_ref.shape[0]
+    inner = HEADS * HEAD
+    line = (here[0] * 4 + here[1]) * 2 + here[2]
+    seqs = out_ref.shape[0]
+
+    def device(at):
+        return {"y": at // 8, "z": (at // 2) % 4, "xl": at % 2}
+
+    barrier = pltpu.get_barrier_semaphore()
+
+    @pl.loop(1, seqs)
+    def _(k):
+        to = lax.rem(line + k, seqs)
+        pl.semaphore_signal(barrier, inc=1, device_id=device(to), device_id_type=pl.DeviceIdType.MESH)
+
+    table = members(lat_ref.shape[2])
+    chan = by_channel(moments(jnp.sum(sums_ref[...], axis=0), count), table)
+    chan_ref[...] = chan
+    for i in range(2):
+        centred = (lat_ref[i].astype(F32) - chan[i : i + 1]) * chan[2 + i : 3 + i]
+        normed_ref[i * 128 : (i + 1) * 128] = (centred * gain_ref[...] + shift_ref[...]).astype(BF16)
     near = normed_ref[:, pl.ds(pl.multiple_of(own * half, 128), half)]
     far = normed_ref[:, pl.ds(pl.multiple_of((1 - own) * half, 128), half)]
-    query, key, value = [
-        jnp.dot(near, a[...], preferred_element_type=F32) + jnp.dot(far, b[...], preferred_element_type=F32)
-        for a, b in zip(mine, other)
-    ]
     low = lax.broadcasted_iota(jnp.int32, (128, 128), 1) < HEAD
-    for h in range(0, query.shape[1] // HEAD, 2):
-        for i in range(2):
-            rows, lanes = slice(i * 128, (i + 1) * 128), slice(h * HEAD, (h + 2) * HEAD)
-            q, k, v = query[rows, lanes], key[rows, lanes], value[rows, lanes]
-            k_roll, v_roll = pltpu.roll(k, HEAD, 1), pltpu.roll(v, HEAD, 1)
-            out_ref[h, i, :128] = jnp.where(low, k, v_roll).astype(BF16)
-            out_ref[h + 1, i, :128] = jnp.where(low, k_roll, v).astype(BF16)
-            first, second = q[:64], q[64:]
-            out_ref[h, i, 128:192] = jnp.where(low[:64], first, pltpu.roll(second, HEAD, 1)).astype(BF16)
-            out_ref[h + 1, i, 128:192] = jnp.where(low[:64], pltpu.roll(first, HEAD, 1), second).astype(BF16)
-
-
-def project(own, lat, sums, gain, shift, g, mine, other, count):
+
+    def copy(row, column):
+        at = row * 8 + column
+        return pltpu.make_async_remote_copy(
+            src_ref=send_ref.at[at], dst_ref=out_ref.at[line],
+            send_sem=send_sem.at[at], recv_sem=recv_sem.at[line],
+            device_id=device(at), device_id_type=pl.DeviceIdType.MESH,
+        )
+
+    def arrival(at):
+        return pltpu.make_async_remote_copy(
+            src_ref=send_ref.at[at], dst_ref=out_ref.at[at],
+            send_sem=send_sem.at[at], recv_sem=recv_sem.at[at],
+            device_id=device(at), device_id_type=pl.DeviceIdType.MESH,
+        )
+
+    def block_row(row):
+        lanes = [pl.ds(pl.multiple_of(p * inner + row * 256, 256), 256) for p in range(3)]
+        query, key, value = [
+            jnp.dot(near, mine_ref[:, at], preferred_element_type=F32)
+            + jnp.dot(far, other_ref[:, at], preferred_element_type=F32)
+            for at in lanes
+        ]
+        for h in range(0, 4, 2):
+            for i in range(2):
+                rows, part = slice(i * 128, (i + 1) * 128), slice(h * HEAD, (h + 2) * HEAD)
+                q, k, v = query[rows, part], key[rows, part], value[rows, part]
+                k_roll, v_roll = pltpu.roll(k, HEAD, 1), pltpu.roll(v, HEAD, 1)
+                first, second = q[:64], q[64:]
+                one, two = row * 8 + h * 2 + i, row * 8 + (h + 1) * 2 + i
+                send_ref[one, :128] = jnp.where(low, k, v_roll).astype(BF16)
+                send_ref[two, :128] = jnp.where(low, k_roll, v).astype(BF16)
+                send_ref[one, 128:192] = jnp.where(low[:64], first, pltpu.roll(second, HEAD, 1)).astype(BF16)
+                send_ref[two, 128:192] = jnp.where(low[:64], pltpu.roll(first, HEAD, 1), second).astype(BF16)
+                send_ref[one, 192:256] = g_ref[row * 4 + h, i]
+                send_ref[two, 192:256] = g_ref[row * 4 + h + 1, i]
+
+    pl.semaphore_wait(barrier, seqs - 1)
+    for j in range(4):
+        row = (here[0] + (j + 1)) % 4
+        block_row(row)
+        if j < 3:
+            @pl.loop(0, 8)
+            def _(k):
+                copy(row, (here[1] * 2 + here[2] + k) % 8).start()
+        else:
+            @pl.loop(1, 8)
+            def _(k):
+                copy(row, (here[1] * 2 + here[2] + k) % 8).start()
+
+    keep = pltpu.make_async_copy(send_ref.at[line], out_ref.at[line], keep_sem)
+    keep.start()
+
+    @pl.loop(1, seqs)
+    def _(k):
+        arrival(lax.rem(line + k, seqs)).wait()
+
+    keep.wait()
+
+
+def project(lat, sums, gain, shift, g, mine, other, count):
     channels = lat.shape[2]
-    cols, half = HEADS * HEAD // 256, mine.shape[0]
-
-    def weight(part):
-        return pl.BlockSpec((half, 256), lambda s, own: (0, part * cols + s))
-
-    def whole(*shape):
-        return pl.BlockSpec(shape, lambda s, own: (0,) * len(shape))
-
+    seqs = sums.shape[0]
+    dma = pltpu.SemaphoreType.DMA
+    whole = pl.BlockSpec(memory_space=pltpu.VMEM)
     return pl.pallas_call(
         functools.partial(project_kernel, count),
-        grid_spec=pltpu.PrefetchScalarGridSpec(
-            num_scalar_prefetch=1,
-            grid=(cols,),
-            in_specs=[whole(*lat.shape), whole(*sums.shape), whole(1, channels), whole(1, channels)]
-            + [pl.BlockSpec((4, 2, 64, 128), lambda s, own: (s, 0, 0, 0))]
-            + [weight(p) for p in range(3)] * 2,
-            out_specs=[pl.BlockSpec((4, 2, 256, 128), lambda s, own: (s, 0, 0, 0)), whole(8, channels)],
-            scratch_shapes=[pltpu.VMEM((256, channels), BF16)],
-        ),
+        in_specs=[whole] * 7,
+        out_specs=[whole, pl.BlockSpec(memory_space=pl.ANY)],
         out_shape=[
-            jax.ShapeDtypeStruct((HEADS, 2, 256, 128), BF16),
             jax.ShapeDtypeStruct((8, channels), F32),
-        ],
-        compiler_params=pltpu.CompilerParams(vmem_limit_bytes=VMEM),
-        cost_estimate=pl.CostEstimate(flops=2 * 256 * 1280 * 3072, bytes_accessed=12 << 20, transcendentals=0),
-    )(own, lat, sums, gain, shift, g, mine, mine, mine, other, other, other)
+            jax.ShapeDtypeStruct((seqs, 256, 128), BF16),
+        ],
+        scratch_shapes=[
+            pltpu.VMEM((256, channels), BF16),
+            pltpu.VMEM((seqs, 256, 128), BF16),
+            dma((seqs,)), dma((seqs,)), dma,
+        ],
+        compiler_params=pltpu.CompilerParams(vmem_limit_bytes=VMEM, collective_id=2, has_side_effects=True),
+        cost_estimate=pl.CostEstimate(flops=2 << 34, bytes_accessed=12 << 20, transcendentals=0),
+    )(lat, sums, gain, shift, g, mine, other)
 
 
 def attended_grad_kernel(own_ref, cot_ref, w_ref, out_ref):
@@ -261,7 +309,7 @@
     )(kvq)
 
 
-def in_weight_kernel(lat_ref, chan_ref, gain_ref, shift_ref, dqo_ref, dkv_ref, out_ref, acc_ref, turned_ref):
+def in_weight_kernel(lat_ref, chan_ref, gain_ref, shift_ref, dqo_ref, dkv_ref, out_ref, acc_ref, turned_ref, block_ref):
     step, last = pl.program_id(0), pl.num_programs(0) - 1
     sources, _, channels = lat_ref.shape
     rows = sources * 128
@@ -284,10 +332,11 @@
         low = lax.broadcasted_iota(jnp.int32, (5, 128), 1) < HEAD
         for d in range(channels // 10):
             at = d * 10
-            out_ref[d, 0:10] = turned_ref[at : at + 10, 128:256]
+            block_ref[0:10] = turned_ref[at : at + 10, 128:256]
             first, second = turned_ref[at : at + 5, 0:128], turned_ref[at + 5 : at + 10, 0:128]
-            out_ref[d, 10:15] = jnp.where(low, first, pltpu.roll(second, HEAD, 1))
-            out_ref[d, 15:16] = jnp.zeros((1, 128), F32)
+            block_ref[10:15] = jnp.where(low, first, pltpu.roll(second, HEAD, 1))
+            block_ref[15:16] = jnp.zeros((1, 128), F32)
+            out_ref[d] = block_ref[...].astype(BF16)
 
 
 def in_weight(lat, chan, gain, shift, dqo, dkv, here=4):
@@ -304,8 +353,10 @@
             pl.BlockSpec((here, 128, 128), lambda i: (i, 0, 0)),
         ],
         out_specs=pl.BlockSpec((channels // 10, 16, 128), lambda i: (0, 0, 0)),
-        out_shape=jax.ShapeDtypeStruct((channels // 10, 16, 128), F32),
-        scratch_shapes=[pltpu.VMEM((256, channels), F32), pltpu.VMEM((channels, 256), F32)],
+        out_shape=jax.ShapeDtypeStruct((channels // 10, 16, 128), BF16),
+        scratch_shapes=[
+            pltpu.VMEM((256, channels), F32), pltpu.VMEM((channels, 256), F32), pltpu.VMEM((16, 128), F32),
+        ],
         compiler_params=pltpu.CompilerParams(vmem_limit_bytes=VMEM),
         cost_estimate=pl.CostEstimate(flops=2 * 4096 * 1280 * 256, bytes_accessed=14 << 20, transcendentals=0),
     )(lat, chan, gain, shift, dqo, dkv)
@@ -363,7 +414,7 @@
     total = lax.dot_general(att, cot, (((0,), (0,)), ((), ())), preferred_element_type=F32)
     blocks = total.reshape(wide // 16, 2, 8, channels)
     own = own_ref[0]
-    out_ref[...] = jnp.where(own == 0, blocks[:, 0], blocks[:, 1])
+    out_ref[...] = jnp.where(own == 0, blocks[:, 0], blocks[:, 1]).astype(BF16)
 
 
 def out_weight(own, att, att_far, cot, cot_far):
@@ -379,7 +430,7 @@
             in_specs=[side, side, full, full],
             out_specs=pl.BlockSpec((tile // 16, 8, channels), lambda s, own: (s, 0, 0)),
         ),
-        out_shape=jax.ShapeDtypeStruct((wide // 16, 8, channels), F32),
+        out_shape=jax.ShapeDtypeStruct((wide // 16, 8, channels), BF16),
         compiler_params=pltpu.CompilerParams(vmem_limit_bytes=VMEM),
         cost_estimate=pl.CostEstimate(flops=4 * 256 * 1280 * 1024, bytes_accessed=6 << 20, transcendentals=0),
     )(own, att, att_far, cot, cot_far)
@@ -501,7 +552,10 @@
     def _(k):
         part_arrival(k).wait_recv()
 
-    weight_ref[...] = jnp.sum(got_ref[...], axis=0)
+    total = got_ref[0:8].astype(F32)
+    for k in range(8, lines, 8):
+        total = total + got_ref[k : k + 8].astype(F32)
+    weight_ref[...] = jnp.sum(total, axis=0)
 
     @pl.loop(1, lines)
     def _(k):
@@ -523,7 +577,7 @@
             pltpu.VMEM(lat.shape, F32),
             pltpu.VMEM((8, 128), F32),
             pltpu.VMEM((lines // 2, 8, 128), F32),
-            pltpu.VMEM(part.shape, F32),
+            pltpu.VMEM(part.shape, BF16),
             dma((lines,)), dma((lines,)), dma((lines // 2,)), dma((lines // 2,)),
         ],
         compiler_params=pltpu.CompilerParams(vmem_limit_bytes=VMEM, collective_id=1, has_side_effects=True),
@@ -558,8 +612,8 @@
     halves_out = jnp.stack([proj_out, other_out])
     cot_far = swapped(cot, "own")
     g = attended_grad(own, cot, halves_out)
-    kvqg_send, chan = project(own, lat, sums, gain, shift, g, proj_qkv, other_qkv, count)
-    kvqg = exchanged(kvqg_send.reshape(seq_count, 256, 128), SEQ)
+    pair_lat, sums = lax.optimization_barrier((pair_lat, sums))
+    chan, kvqg = project(lat, sums, gain, shift, g, proj_qkv, other_qkv, count)
     pair_lat, kvqg = lax.optimization_barrier((pair_lat, kvqg))
     image_lat = lax.all_gather(pair_lat, ("y", "z"), tiled=True)
 
@@ -580,7 +634,7 @@
         out_part, dqo_tok, dkv_tok, proj_qkv, other_qkv, lat, cot, chan, gain, count
     )
 
-    summed = jnp.sum(in_blocks.reshape(HEADS, 8, 16, 128), axis=1)
+    summed = jnp.sum(in_blocks.reshape(HEADS, 8, 16, 128).astype(F32), axis=1)
     dq = summed[:, 10:15].reshape(HEADS, 5, 2, HEAD).transpose(2, 1, 0, 3).reshape(10, HEADS * HEAD)
     dk = summed[:, :10, :HEAD].transpose(1, 0, 2).reshape(10, HEADS * HEAD)
     dv = summed[:, :10, HEAD:].transpose(1, 0, 2).reshape(10, HEADS * HEAD)

time: 293 us -> 260 us (0.89)
  waiting for transfers between devices: 32.9 us -> 5.33 us
  starting transfers between devices: 45.9 us -> 33.8 us
  Pallas kernels: 178 us -> 187 us
    ppermute x5, waiting for transfers between devices: 29.7 us -> 0.01 us  [swapped(): return lax.ppermute(value, axis, [(0, 1), (1, 0)])]
    pallas_call x1, Pallas kernels: 8.39 us -> 37.8 us  [project(): pl.pallas_call(functools.partial(project_kernel, count), in_specs=[whole]...]
    pallas_call x1, Pallas kernels: 58.4 us -> 37.9 us  [tail(): pl.pallas_call(functools.partial(tail_kernel, count), out_shape=[jax.Shap...]
    all_to_all x5 -> x4, starting transfers between devices: 39.9 us -> 28.2 us  [exchanged(): return lax.all_to_all(value, axes, 0, 0, tiled=True)]
    unnamed x33 -> x29, local copies, waits for them, and re-layouts: 12.3 us -> 10.6 us
  transfers between devices with their start and end apart: 11 -> 10, of which waited for: 2 -> 2; matrix products, arithmetic and copies ran while one was open for 4% -> 6% of each run, Pallas kernels for 59% -> 58%
where the time goes in v4:
time: 260 us; the launch traced here: 259 us
  Pallas kernels  187 us (72%)
  starting transfers between devices  33.8 us (13%)
  between operations  14.3 us (6%)
  local copies, waits for them, and re-layouts  12.4 us (5%)
  other arithmetic  6.15 us (2%)
  waiting for transfers between devices  5.33 us (2%)
    pallas_call x1, Pallas kernels, attention(): pl.pallas_call(functools.partial(attention_kernel, ck), grid=(sources //...  83 us
    pallas_call x1, Pallas kernels, tail(): pl.pallas_call(functools.partial(tail_kernel, count), out_shape=[jax.Shap...  37.9 us
    pallas_call x1, Pallas kernels, project(): pl.pallas_call(functools.partial(project_kernel, count), in_specs=[whole]...  37.8 us
    all_to_all x4, starting transfers between devices, exchanged(): return lax.all_to_all(value, axes, 0, 0, tiled=True)  28.2 us
    pallas_call x1, Pallas kernels, in_weight(): pl.pallas_call(in_weight_kernel, grid=(sources // here,), in_specs=[pl.Bl...  12 us
    unnamed x29, local copies, waits for them, and re-layouts  10.6 us
    ppermute x5, starting transfers between devices, swapped(): return lax.ppermute(value, axis, [(0, 1), (1, 0)])  5.58 us
    all_to_all x4, waiting for transfers between devices, exchanged(): return lax.all_to_all(value, axes, 0, 0, tiled=True)  5.3 us
  transfers between devices with their start and end apart: 10, of which 2 were waited for; matrix products, arithmetic and copies ran while one was open for 6% of the time, Pallas kernels for 58%

profile of v4, /device:TPU:1, one launch (start us, length us, event | category | flops | bytes accessed | tf_op | source)
XLA Modules:
  0.0 258.7 jit_solution(7958015232150331348)
XLA Ops:
  7.2 1.5 collective-permute-start.2
  8.7 1.2 copy.38
  9.9 0.9 broadcast_select_fusion
  10.8 1.3 collective-permute-start
  12.1 2.3 shard_map.93
  14.5 8.1 %all-to-all-start = ((f32[32,8,128]{2,1,0:T(8,128)}), f32[32,8,128]{2,1,0:T(8,128)S(1)}, u32[]{:S(2)}, u32[]{:S(2)}) async-start(f32[32,8,128]{2,1,0:T(8,128)} %shard_map.93), calls=%async_computation | async-start | bytes 262144 | tf_op jit(solution)/shard_map/all_to_all | solution.py:593
  22.6 2.0 copy.37
  25.8 2.2 maximum_select_fusion
  28.0 2.1 all-to-all-done.sums_ref
  30.1 1.7 pad_maximum_fusion.w_ref
  31.8 4.6 %shard_map.94.g_ref = bf16[16,2,64,128]{3,2,1,0:T(8,128)(2,1)} custom-call(s32[1]{0:T(128)} %bitcast.own_ref, bf16[2,128,1280]{2,1,0:T(8,128)(2,1)} %bitcast.35, bf16[2,512,1280]{2,1,0:T(8,128)(2,1)} %pad_maximum_fusion.w_ref), custom_call_target="tpu_custom_call" | custom-call | flops 671088640 | bytes 4194304 | tf_op jit(solution)/shard_map/pallas_call | solution.py:199
  36.5 37.8 %shard_map.95 = (f32[8,1280]{1,0:T(8,128)}, bf16[32,256,128]{2,1,0:T(8,128)(2,1)}) custom-call(bf16[2,128,1280]{2,1,0:T(8,128)(2,1)} %bitcast.30, f32[32,8,128]{2,1,0:T(8,128)} %copy-done.5, f32[1,1280]{1,0:T(1,128)} %reshape.41.gain_ref, f32[1,1280]{1,0:T(1,128)} %reshape.42.shift_ref, bf16[16,2,64,128]{3,2,1,0:T(8,128)(2,1)} %shard_map.94.g_ref, ...), custom_call_target="tpu_custom_call" | custom-call | flops 34359738368 | bytes 12582912 | tf_op jit(solution)/shard_map/pallas_call | solution.py:165
  74.3 83.0 %shard_map.96 = (bf16[32,128,128]{2,1,0:T(8,128)(2,1)}, bf16[32,128,128]{2,1,0:T(8,128)(2,1)}) custom-call(bf16[32,256,128]{2,1,0:T(8,128)(2,1)} %get-tuple-element.25.kvq_ref), custom_call_target="tpu_custom_call" | custom-call | flops 51539607552 | bytes 4194304 | tf_op jit(solution)/shard_map/pallas_call | solution.py:287
  157.3 6.2 %all-to-all-start.1 = ((bf16[32,128,128]{2,1,0:T(8,128)(2,1)}), bf16[32,128,128]{2,1,0:T(8,128)(2,1)S(1)}, u32[]{:S(2)}, u32[]{:S(2)}) async-start(bf16[32,128,128]{2,1,0:T(8,128)(2,1)} %get-tuple-element.26.dqo_ref), calls=%async_computation.1 | async-start | bytes 2097152 | tf_op jit(solution)/shard_map/all_to_all | solution.py:593
  164.1 12.0 %shard_map.97 = bf16[128,16,128]{2,1,0:T(8,128)(2,1)} custom-call(bf16[32,128,1280]{2,1,0:T(8,128)(2,1)} %all-gather.2.cloned.1.call-done.lat_ref, f32[2,1280]{1,0:T(2,128)} %broadcast_select_fusion.1.chan_ref, f32[1,1280]{1,0:T(1,128)} %reshape.41.gain_ref, f32[1,1280]{1,0:T(1,128)} %reshape.42.shift_ref, bf16[32,128,128]{2,1,0:T(8,128)(2,1)} %get-tuple-element.26.dqo_ref, ...), custom_call_target="tpu_custom_call" | custom-call | flops 2684354560 | bytes 14680064 | tf_op jit(solution)/shard_map/pallas_call | solution.py:344
  176.1 3.2 %all-to-all-done.1 = bf16[32,128,128]{2,1,0:T(8,128)(2,1)S(1)} async-done(((bf16[32,128,128]{2,1,0:T(8,128)(2,1)}), bf16[32,128,128]{2,1,0:T(8,128)(2,1)S(1)}, u32[]{:S(2)}, u32[]{:S(2)}) %all-to-all-start.1) | async-done | bytes 1048608 | tf_op jit(solution)/shard_map/all_to_all | solution.py:593
  179.3 4.4 %all-to-all-start.2 = ((bf16[32,128,128]{2,1,0:T(8,128)(2,1)}), bf16[32,128,128]{2,1,0:T(8,128)(2,1)S(1)}, u32[]{:S(2)}, u32[]{:S(2)}) async-start(bf16[32,128,128]{2,1,0:T(8,128)(2,1)} %get-tuple-element.32.dkv_ref), calls=%async_computation.2 | async-start | bytes 2097152 | tf_op jit(solution)/shard_map/all_to_all | solution.py:593
  183.7 2.7 %collective-permute-start.4 = (bf16[2,128,1280]{2,1,0:T(8,128)(2,1)S(1)}, bf16[2,128,1280]{2,1,0:T(8,128)(2,1)S(1)}, u32[]{:S(2)}, u32[]{:S(2)}) collective-permute-start(bf16[2,128,1280]{2,1,0:T(8,128)(2,1)S(1)} %bitcast.38), channel_id=1, source_target_pairs={{0,1},{1,0},{2,3},{3,2},{4,5},{5,4},{6,7},{7,6},{8,9},{9,8},{10,11... | collective-permute-start | bytes 1966088 | tf_op jit(solution)/shard_map/ppermute | solution.py:589
  186.4 4.2 %shard_map.98 = (bf16[2,128,1280]{2,1,0:T(8,128)(2,1)}, bf16[2,128,1024]{2,1,0:T(8,128)(2,1)}) custom-call(s32[1]{0:T(128)} %bitcast.own_ref, bf16[16,2,128,128]{3,2,1,0:T(8,128)(2,1)} %bitcast.33, bf16[2,128,1280]{2,1,0:T(8,128)(2,1)} %bitcast.31, bf16[2,512,1280]{2,1,0:T(8,128)(2,1)} %pad_maximum_fusion.w_ref), custom_call_target="tpu_custom_call" | custom-call | flops 671088640 | bytes 6291456 | tf_op jit(solution)/shard_map/pallas_call | solution.py:392
  190.6 2.6 %copy.33 = bf16[128,2,1280]{2,1,0:T(2,128)(2,1)} copy(bf16[128,2,1280]{2,0,1:T(8,128)(2,1)} %bitcast.43) | data formatting | bytes 1310720
  194.8 5.0 %shard_map.99.part_ref = bf16[64,8,1280]{2,1,0:T(8,128)(2,1)} custom-call(s32[1]{0:T(128)} %bitcast.own_ref, bf16[2,128,1024]{2,1,0:T(8,128)(2,1)} %get-tuple-element.33.att_ref, bf16[2,128,1024]{2,1,0:T(8,128)(2,1)} %copy-done.11, bf16[2,128,1280]{2,1,0:T(8,128)(2,1)} %bitcast.36, bf16[2,128,1280]{2,1,0:T(8,128)(2,1)} %copy-done.10), custom_call_target="tpu_custom_call" | custom-call | flops 1342177280 | bytes 6291456 | tf_op jit(solution)/shard_map/pallas_call | solution.py:425
  199.8 9.5 %all-to-all-start.3 = ((bf16[128,16,128]{2,1,0:T(8,128)(2,1)}), bf16[128,16,128]{2,1,0:T(8,128)(2,1)S(1)}, u32[]{:S(2)}, u32[]{:S(2)}) async-start(bf16[128,16,128]{2,1,0:T(8,128)(2,1)} %shard_map.97), calls=%async_computation.3 | async-start | bytes 1048576 | tf_op jit(solution)/shard_map/all_to_all | solution.py:593
  209.4 37.9 %shard_map.100 = (bf16[2,128,1280]{2,1,0:T(8,128)(2,1)}, f32[8,1280]{1,0:T(8,128)}) custom-call(bf16[64,8,1280]{2,1,0:T(8,128)(2,1)} %shard_map.99.part_ref, bf16[16,2,128,128]{3,2,1,0:T(8,128)(2,1)} %bitcast.34, bf16[16,2,128,128]{3,2,1,0:T(8,128)(2,1)} %bitcast.41, bf16[640,3072]{1,0:T(8,128)(2,1)} %mine_ref.3, ...), custom_call_target="tpu_custom_call" | custom-call | flops 34359738368 | bytes 16777216 | tf_op jit(solution)/shard_map/pallas_call | solution.py:572
  247.3 2.6 %copy.34 = bf16[128,2,1280]{2,1,0:T(2,128)(2,1)} copy(bf16[128,2,1280]{2,0,1:T(8,128)(2,1)} %bitcast.42) | data formatting | bytes 1310720
  (54 shorter events, 5.6 us)
Async XLA Ops:
  7.2 17.4 %copy-start.8 = (f32[1280]{0:T(1024)S(1)}, f32[1280]{0:T(1024)}, u32[]{:S(2)}) copy-start(f32[1280]{0:T(1024)} %param.8) | copy-start | bytes 15364
  7.2 18.0 %copy-start.9 = (f32[1280]{0:T(1024)S(1)}, f32[1280]{0:T(1024)}, u32[]{:S(2)}) copy-start(f32[1280]{0:T(1024)} %param.9) | copy-start | bytes 15364
  7.2 29.3 %collective-permute-start.2 = (bf16[640,3072]{1,0:T(8,128)(2,1)}, bf16[640,3072]{1,0:T(8,128)(2,1)}, u32[]{:S(2)}, u32[]{:S(2)}) collective-permute-start(bf16[640,3072]{1,0:T(8,128)(2,1)} %mine_ref.3), channel_id=1, source_target_pairs={{0,1},{1,0},{2,3},{3,2},{4,5},{5,4},{6,7},{7,6},{8,9},{9,8},{10,11... | collective-permute-start | bytes 11796488 | tf_op jit(solution)/shard_map/ppermute | solution.py:589
  8.6 21.5 %collective-permute-start.1 = (bf16[512,1280]{1,0:T(8,128)(2,1)}, bf16[512,1280]{1,0:T(8,128)(2,1)S(1)}, u32[]{:S(2)}, u32[]{:S(2)}) collective-permute-start(bf16[512,1280]{1,0:T(8,128)(2,1)} %param.11), channel_id=1, source_target_pairs={{0,1},{1,0},{2,3},{3,2},{4,5},{5,4},{6,7},{7,6},{8,9},{9,8},{10,11... | collective-permute-start | bytes 3932168 | tf_op jit(solution)/shard_map/ppermute | solution.py:589
  9.9 2.2 copy-start
  9.9 20.2 %copy-start.3 = (bf16[512,1280]{1,0:T(8,128)(2,1)S(1)}, bf16[512,1280]{1,0:T(8,128)(2,1)}, u32[]{:S(2)}) copy-start(bf16[512,1280]{1,0:T(8,128)(2,1)} %param.11) | copy-start | bytes 3932164
  10.8 15.0 %collective-permute-start = (bf16[128,1280]{1,0:T(8,128)(2,1)}, bf16[128,1280]{1,0:T(8,128)(2,1)}, u32[]{:S(2)}, u32[]{:S(2)}) collective-permute-start(bf16[128,1280]{1,0:T(8,128)(2,1)} %get-tuple-element.57), channel_id=1, source_target_pairs={{0,4},{4,0},{1,5},{5,1},{2,6},{6,2},{3,7},{7,3},{8,12},{12,8},{9,1... | collective-permute-start | bytes 983048 | tf_op jit(solution)/shard_map/ppermute | solution.py:589
  14.5 15.7 %all-to-all-start = ((f32[32,8,128]{2,1,0:T(8,128)}), f32[32,8,128]{2,1,0:T(8,128)S(1)}, u32[]{:S(2)}, u32[]{:S(2)}) async-start(f32[32,8,128]{2,1,0:T(8,128)} %shard_map.93), calls=%async_computation | async-start | bytes 262144 | tf_op jit(solution)/shard_map/all_to_all | solution.py:593
  22.5 141.6 %all-gather.2.cloned.1.call-start = ((), (), s32[]{:S(2)}) async-start(), calls=%async_computation.4 | async-start | bytes 11141120 | tf_op jit(solution)/shard_map/all_gather | solution.py:618
  30.1 1.7 copy-start.5
  74.3 89.2 %copy-start.7 = (f32[8,1280]{1,0:T(8,128)S(1)}, f32[8,1280]{1,0:T(8,128)}, u32[]{:S(2)}) copy-start(f32[8,1280]{1,0:T(8,128)} %get-tuple-element.29.chan_ref) | copy-start | bytes 122884
  157.3 22.0 %all-to-all-start.1 = ((bf16[32,128,128]{2,1,0:T(8,128)(2,1)}), bf16[32,128,128]{2,1,0:T(8,128)(2,1)S(1)}, u32[]{:S(2)}, u32[]{:S(2)}) async-start(bf16[32,128,128]{2,1,0:T(8,128)(2,1)} %get-tuple-element.26.dqo_ref), calls=%async_computation.1 | async-start | bytes 2097152 | tf_op jit(solution)/shard_map/all_to_all | solution.py:593
  164.1 19.6 %copy-start.2 = (bf16[128,2,1280]{2,0,1:T(8,128)(2,1)S(1)}, bf16[128,2,1280]{2,0,1:T(8,128)(2,1)}, u32[]{:S(2)}) copy-start(bf16[128,2,1280]{2,0,1:T(8,128)(2,1)} %copy.37) | copy-start | bytes 1966084
  179.3 7.1 %copy-start.1 = (bf16[32,128,128]{2,1,0:T(8,128)(2,1)}, bf16[32,128,128]{2,1,0:T(8,128)(2,1)S(1)}, u32[]{:S(2)}) copy-start(bf16[32,128,128]{2,1,0:T(8,128)(2,1)S(1)} %all-to-all-done.1) | copy-start | bytes 3145732
  179.3 20.5 %all-to-all-start.2 = ((bf16[32,128,128]{2,1,0:T(8,128)(2,1)}), bf16[32,128,128]{2,1,0:T(8,128)(2,1)S(1)}, u32[]{:S(2)}, u32[]{:S(2)}) async-start(bf16[32,128,128]{2,1,0:T(8,128)(2,1)} %get-tuple-element.32.dkv_ref), calls=%async_computation.2 | async-start | bytes 2097152 | tf_op jit(solution)/shard_map/all_to_all | solution.py:593
  183.7 9.5 %collective-permute-start.4 = (bf16[2,128,1280]{2,1,0:T(8,128)(2,1)S(1)}, bf16[2,128,1280]{2,1,0:T(8,128)(2,1)S(1)}, u32[]{:S(2)}, u32[]{:S(2)}) collective-permute-start(bf16[2,128,1280]{2,1,0:T(8,128)(2,1)S(1)} %bitcast.38), channel_id=1, source_target_pairs={{0,1},{1,0},{2,3},{3,2},{4,5},{5,4},{6,7},{7,6},{8,9},{9,8},{10,11... | collective-permute-start | bytes 1966088 | tf_op jit(solution)/shard_map/ppermute | solution.py:589
  190.6 2.6 %collective-permute-start.3 = (bf16[2,128,1024]{2,1,0:T(8,128)(2,1)}, bf16[2,128,1024]{2,1,0:T(8,128)(2,1)S(1)}, u32[]{:S(2)}, u32[]{:S(2)}) collective-permute-start(bf16[2,128,1024]{2,1,0:T(8,128)(2,1)} %get-tuple-element.33.att_ref), channel_id=1, source_target_pairs={{0,1},{1,0},{2,3},{3,2},{4,5},{5,4},{6,7},{7,6},{8,9},{9,8},{10,11... | collective-permute-start | bytes 1572872 | tf_op jit(solution)/shard_map/ppermute | solution.py:589
  193.2 0.8 copy-start.10
  194.0 0.8 copy-start.11
  199.8 9.6 %copy-start.4 = (bf16[32,128,128]{2,1,0:T(8,128)(2,1)}, bf16[32,128,128]{2,1,0:T(8,128)(2,1)S(1)}, u32[]{:S(2)}) copy-start(bf16[32,128,128]{2,1,0:T(8,128)(2,1)S(1)} %all-to-all-done.2) | copy-start | bytes 3145732
  199.8 50.1 %all-to-all-start.3 = ((bf16[128,16,128]{2,1,0:T(8,128)(2,1)}), bf16[128,16,128]{2,1,0:T(8,128)(2,1)S(1)}, u32[]{:S(2)}, u32[]{:S(2)}) async-start(bf16[128,16,128]{2,1,0:T(8,128)(2,1)} %shard_map.97), calls=%async_computation.3 | async-start | bytes 1048576 | tf_op jit(solution)/shard_map/all_to_all | solution.py:593
  247.3 4.0 %copy-start.6 = (f32[8,1280]{1,0:T(8,128)S(1)}, f32[8,1280]{1,0:T(8,128)}, u32[]{:S(2)}) copy-start(f32[8,1280]{1,0:T(8,128)} %get-tuple-element.67) | copy-start | bytes 122884
Sparse Core Ops, SparseCore 0:
  74.4 80.7 all-gather.1

commit v5 on v4

--- a/solution.py
+++ b/solution.py
@@ -17,6 +17,10 @@
 ALL = ("y", "z", "xl", "rep", "own")
 F32, BF16 = jnp.float32, jnp.bfloat16
 VMEM = 60 << 20
+
+
+def place():
+    return tuple(lax.axis_index(axis) for axis in ALL)
 
 
 def members(channels):
@@ -216,21 +220,55 @@
     )(own, cot, halves)
 
 
-def attention_kernel(ck, kvq_ref, dqo_ref, dkv_ref, s_ref, x_ref, y_ref, acc_ref):
+def attention_kernel(
+    ck, kvq_ref, dqo_ref, dkv_ref, tok_ref, s_ref, x_ref, y_ref, acc_ref, send_ref, send_sem, recv_sem, keep_sem
+):
+    here_at = place()
+    line = (here_at[0] * 4 + here_at[1]) * 2 + here_at[2]
+
+    def device(at):
+        return {"y": at // 8, "z": (at // 2) % 4, "xl": at % 2}
+
+    def copy(at):
+        return pltpu.make_async_remote_copy(
+            src_ref=send_ref.at[at], dst_ref=tok_ref.at[line],
+            send_sem=send_sem.at[at], recv_sem=recv_sem.at[line],
+            device_id=device(at), device_id_type=pl.DeviceIdType.MESH,
+        )
+
+    def arrival(at):
+        return pltpu.make_async_remote_copy(
+            src_ref=send_ref.at[at], dst_ref=tok_ref.at[at],
+            send_sem=send_sem.at[at], recv_sem=recv_sem.at[at],
+            device_id=device(at), device_id_type=pl.DeviceIdType.MESH,
+        )
+
+    def keep():
+        return pltpu.make_async_copy(send_ref.at[line], tok_ref.at[line], keep_sem)
+
     step, last = pl.program_id(0), pl.num_programs(0) - 1
     sources, _, width = kvq_ref.shape
     keys = sources * 128
     here = dqo_ref.shape[0]
+    base = lax.rem(line // here * here + (step + 1) * here, sources)
     rows = here * 128
     half = rows // 2
 
     @pl.when(step == 0)
     def _():
         acc_ref[...] = jnp.zeros_like(acc_ref)
+        barrier = pltpu.get_barrier_semaphore()
+
+        @pl.loop(1, sources)
+        def _(k):
+            to = lax.rem(line + k, sources)
+            pl.semaphore_signal(barrier, inc=1, device_id=device(to), device_id_type=pl.DeviceIdType.MESH)
+
+        pl.semaphore_wait(barrier, sources - 1)
 
     low = lax.broadcasted_iota(jnp.int32, (half, width), 1) < HEAD
-    xq = kvq_ref[pl.ds(step * here, here), 128:192, :].reshape(half, width).astype(F32) * SCALE
-    xg = kvq_ref[pl.ds(step * here, here), 192:256, :].reshape(half, width).astype(F32)
+    xq = kvq_ref[pl.ds(base, here), 128:192, :].reshape(half, width).astype(F32) * SCALE
+    xg = kvq_ref[pl.ds(base, here), 192:256, :].reshape(half, width).astype(F32)
     zero = jnp.zeros_like(xq)
     y_ref[0 * half : 1 * half] = jnp.where(low, xq, zero).astype(BF16)
     y_ref[1 * half : 2 * half] = jnp.where(low, pltpu.roll(xq, HEAD, 1), zero).astype(BF16)
@@ -275,15 +313,38 @@
         for a in range(here):
             at = h * half + a * 64
             dqo_ref[a, h * 64 : (h + 1) * 64, :] = res[at : at + 64]
+            send_ref[base + a, h * 64 : (h + 1) * 64, :] = res[at : at + 64]
+
+    for a in range(here):
+        @pl.when(base + a != line)
+        def _():
+            copy(base + a).start()
+
+        @pl.when(base + a == line)
+        def _():
+            keep().start()
 
     @pl.when(step == last)
     def _():
         dkv_ref[...] = acc_ref[...].reshape(sources, 128, width).astype(BF16)
 
+        @pl.loop(1, sources)
+        def _(k):
+            arrival(lax.rem(line + k, sources)).wait()
+
+        keep().wait()
+
 
 def attention(kvq, here=2, ck=1024):
     sources = kvq.shape[0]
     keys, rows = sources * 128, here * 128
+    dma = pltpu.SemaphoreType.DMA
+
+    def block(i):
+        here_at = place()
+        line = (here_at[0] * 4 + here_at[1]) * 2 + here_at[2]
+        return lax.rem(line // here + i + 1, sources // here), 0, 0
+
     return pl.pallas_call(
         functools.partial(attention_kernel, ck),
         grid=(sources // here,),
@@ -291,10 +352,12 @@
             pl.BlockSpec((sources, 256, 128), lambda i: (0, 0, 0), pipeline_mode=pl.Buffered(1)),
         ],
         out_specs=[
-            pl.BlockSpec((here, 128, 128), lambda i: (i, 0, 0)),
+            pl.BlockSpec((here, 128, 128), block),
             pl.BlockSpec((sources, 128, 128), lambda i: (0, 0, 0)),
+            pl.BlockSpec(memory_space=pl.ANY),
         ],
         out_shape=[
+            jax.ShapeDtypeStruct((sources, 128, 128), BF16),
             jax.ShapeDtypeStruct((sources, 128, 128), BF16),
             jax.ShapeDtypeStruct((sources, 128, 128), BF16),
         ],
@@ -303,8 +366,10 @@
             pltpu.VMEM((2 * rows, keys), BF16),
             pltpu.VMEM((2 * rows, 128), BF16),
             pltpu.VMEM((keys, 128), F32),
-        ],
-        compiler_params=pltpu.CompilerParams(vmem_limit_bytes=VMEM),
+            pltpu.VMEM((sources, 128, 128), BF16),
+            dma((sources,)), dma((sources,)), dma,
+        ],
+        compiler_params=pltpu.CompilerParams(vmem_limit_bytes=VMEM, collective_id=3, has_side_effects=True),
         cost_estimate=pl.CostEstimate(flops=48 * keys * keys * HEAD, bytes_accessed=4 << 20, transcendentals=keys * keys),
     )(kvq)
 
@@ -434,10 +499,6 @@
         compiler_params=pltpu.CompilerParams(vmem_limit_bytes=VMEM),
         cost_estimate=pl.CostEstimate(flops=4 * 256 * 1280 * 1024, bytes_accessed=6 << 20, transcendentals=0),
     )(own, att, att_far, cot, cot_far)
-
-
-def place():
-    return tuple(lax.axis_index(axis) for axis in ALL)
 
 
 def shifted(here, k, sign):
@@ -617,13 +678,12 @@
     pair_lat, kvqg = lax.optimization_barrier((pair_lat, kvqg))
     image_lat = lax.all_gather(pair_lat, ("y", "z"), tiled=True)
 
-    dqo, dkv = attention(kvqg)
-
-    dqo_tok = exchanged(dqo, SEQ)
+    dqo, dkv, dqo_tok = attention(kvqg)
+
+    dkv_tok = exchanged(dkv, SEQ)
     chan_image = jnp.where(image == 0, chan[0:4:2], chan[1:4:2])
     in_part = in_weight(image_lat, chan_image, gain, shift, dqo, dkv)
-    dqo_tok, dkv, in_part = lax.optimization_barrier((dqo_tok, dkv, in_part))
-    dkv_tok = exchanged(dkv, SEQ)
+    dqo_tok, in_part = lax.optimization_barrier((dqo_tok, in_part))
     dqo_tok = dqo_tok.reshape(HEADS, images, 128, 128)
     mixed, att = mix(own, dqo_tok, lat, halves_out)
     out_part = out_weight(own, att, swapped(att, "own"), cot, cot_far)

time: 260 us -> 262 us (level)
  Pallas kernels: 187 us -> 196 us
  starting transfers between devices: 33.8 us -> 28.2 us
  waiting for transfers between devices: 5.33 us -> 2.14 us
    pallas_call x1, Pallas kernels: 83 us -> 92 us  [attention(): pl.pallas_call(functools.partial(attention_kernel, ck), grid=(sources //...]
    all_to_all x4 -> x3, starting transfers between devices: 28.2 us -> 22.3 us  [exchanged(): return lax.all_to_all(value, axes, 0, 0, tiled=True)]
    all_to_all x4 -> x3, waiting for transfers between devices: 5.3 us -> 2.11 us  [exchanged(): return lax.all_to_all(value, axes, 0, 0, tiled=True)]
    unnamed x29 -> x25, local copies, waits for them, and re-layouts: 10.6 us -> 10.6 us
  transfers between devices with their start and end apart: 10 -> 9, of which waited for: 2 -> 1; matrix products, arithmetic and copies ran while one was open for 6% -> 6% of each run, Pallas kernels for 58% -> 61%
where the time goes in v5:
time: 262 us; the launch traced here: 261 us
  Pallas kernels  196 us (75%)
  starting transfers between devices  28.2 us (11%)
  between operations  14.2 us (5%)
  local copies, waits for them, and re-layouts  14 us (5%)
  other arithmetic  6.15 us (2%)
    pallas_call x1, Pallas kernels, attention(): pl.pallas_call(functools.partial(attention_kernel, ck), grid=(sources //...  92 us
    pallas_call x1, Pallas kernels, tail(): pl.pallas_call(functools.partial(tail_kernel, count), out_shape=[jax.Shap...  37.9 us
    pallas_call x1, Pallas kernels, project(): pl.pallas_call(functools.partial(project_kernel, count), in_specs=[whole]...  37.9 us
    all_to_all x3, starting transfers between devices, exchanged(): return lax.all_to_all(value, axes, 0, 0, tiled=True)  22.3 us
    pallas_call x1, Pallas kernels, in_weight(): pl.pallas_call(in_weight_kernel, grid=(sources // here,), in_specs=[pl.Bl...  11.9 us
    unnamed x25, local copies, waits for them, and re-layouts  10.6 us
    ppermute x5, starting transfers between devices, swapped(): return lax.ppermute(value, axis, [(0, 1), (1, 0)])  5.84 us
  transfers between devices with their start and end apart: 9, of which 1 were waited for; matrix products, arithmetic and copies ran while one was open for 6% of the time, Pallas kernels for 61%

profile of v5, /device:TPU:1, one launch (start us, length us, event | category | flops | bytes accessed | tf_op | source)
XLA Modules:
  0.0 260.6 jit_solution(5962864544190986164)
XLA Ops:
  7.2 1.5 collective-permute-start.2
  8.7 1.2 copy.38
  9.9 0.9 broadcast_select_fusion
  10.8 1.3 collective-permute-start
  12.1 2.3 shard_map.93
  14.5 8.1 %all-to-all-start = ((f32[32,8,128]{2,1,0:T(8,128)}), f32[32,8,128]{2,1,0:T(8,128)S(1)}, u32[]{:S(2)}, u32[]{:S(2)}) async-start(f32[32,8,128]{2,1,0:T(8,128)} %shard_map.93), calls=%async_computation | async-start | bytes 262144 | tf_op jit(solution)/shard_map/all_to_all | solution.py:654
  23.8 2.0 copy.37
  25.8 2.2 maximum_select_fusion
  28.0 2.1 all-to-all-done.sums_ref
  30.1 1.7 pad_maximum_fusion.w_ref
  31.8 4.6 %shard_map.94.g_ref = bf16[16,2,64,128]{3,2,1,0:T(8,128)(2,1)} custom-call(s32[1]{0:T(128)} %bitcast.own_ref, bf16[2,128,1280]{2,1,0:T(8,128)(2,1)} %bitcast.33, bf16[2,512,1280]{2,1,0:T(8,128)(2,1)} %pad_maximum_fusion.w_ref), custom_call_target="tpu_custom_call" | custom-call | flops 671088640 | bytes 4194304 | tf_op jit(solution)/shard_map/pallas_call | solution.py:203
  36.5 37.9 %shard_map.95 = (f32[8,1280]{1,0:T(8,128)}, bf16[32,256,128]{2,1,0:T(8,128)(2,1)}) custom-call(bf16[2,128,1280]{2,1,0:T(8,128)(2,1)} %bitcast.30, f32[32,8,128]{2,1,0:T(8,128)} %copy-done.4, f32[1,1280]{1,0:T(1,128)} %reshape.41.gain_ref, f32[1,1280]{1,0:T(1,128)} %reshape.42.shift_ref, bf16[16,2,64,128]{3,2,1,0:T(8,128)(2,1)} %shard_map.94.g_ref, ...), custom_call_target="tpu_custom_call" | custom-call | flops 34359738368 | bytes 12582912 | tf_op jit(solution)/shard_map/pallas_call | solution.py:169
  74.4 1.8 collective-permute-start.4
  77.8 92.0 %shard_map.96 = (bf16[32,128,128]{2,1,0:T(8,128)(2,1)}, bf16[32,128,128]{2,1,0:T(8,128)(2,1)}, bf16[32,128,128]{2,1,0:T(8,128)(2,1)}) custom-call(bf16[32,256,128]{2,1,0:T(8,128)(2,1)} %get-tuple-element.25.kvq_ref), custom_call_target="tpu_custom_call" | custom-call | flops 51539607552 | bytes 4194304 | tf_op jit(solution)/shard_map/pallas_call | solution.py:348
  169.9 5.1 %all-to-all-start.1 = ((bf16[32,128,128]{2,1,0:T(8,128)(2,1)}), bf16[32,128,128]{2,1,0:T(8,128)(2,1)S(1)}, u32[]{:S(2)}, u32[]{:S(2)}) async-start(bf16[32,128,128]{2,1,0:T(8,128)(2,1)} %get-tuple-element.30.dkv_ref), calls=%async_computation.1 | async-start | bytes 2097152 | tf_op jit(solution)/shard_map/all_to_all | solution.py:654
  175.6 11.9 %shard_map.97 = bf16[128,16,128]{2,1,0:T(8,128)(2,1)} custom-call(bf16[32,128,1280]{2,1,0:T(8,128)(2,1)} %all-gather.2.cloned.1.call-done.lat_ref, f32[2,1280]{1,0:T(2,128)} %broadcast_select_fusion.1.chan_ref, f32[1,1280]{1,0:T(1,128)} %reshape.41.gain_ref, f32[1,1280]{1,0:T(1,128)} %reshape.42.shift_ref, bf16[32,128,128]{2,1,0:T(8,128)(2,1)} %get-tuple-element.29.dqo_ref, ...), custom_call_target="tpu_custom_call" | custom-call | flops 2684354560 | bytes 14680064 | tf_op jit(solution)/shard_map/pallas_call | solution.py:409
  187.5 4.2 %shard_map.98 = (bf16[2,128,1280]{2,1,0:T(8,128)(2,1)}, bf16[2,128,1024]{2,1,0:T(8,128)(2,1)}) custom-call(s32[1]{0:T(128)} %bitcast.own_ref, bf16[16,2,128,128]{3,2,1,0:T(8,128)(2,1)} %bitcast.39, bf16[2,128,1280]{2,1,0:T(8,128)(2,1)} %bitcast.31, bf16[2,512,1280]{2,1,0:T(8,128)(2,1)} %pad_maximum_fusion.w_ref), custom_call_target="tpu_custom_call" | custom-call | flops 671088640 | bytes 6291456 | tf_op jit(solution)/shard_map/pallas_call | solution.py:457
  191.7 1.1 collective-permute-start.3
  192.8 2.6 copy.33
  195.4 0.8 copy-done.8
  197.1 5.0 %shard_map.99.part_ref = bf16[64,8,1280]{2,1,0:T(8,128)(2,1)} custom-call(s32[1]{0:T(128)} %bitcast.own_ref, bf16[2,128,1024]{2,1,0:T(8,128)(2,1)} %get-tuple-element.33.att_ref, bf16[2,128,1024]{2,1,0:T(8,128)(2,1)} %copy-done.9, bf16[2,128,1280]{2,1,0:T(8,128)(2,1)} %bitcast.34, bf16[2,128,1280]{2,1,0:T(8,128)(2,1)} %copy-done.8), custom_call_target="tpu_custom_call" | custom-call | flops 1342177280 | bytes 6291456 | tf_op jit(solution)/shard_map/pallas_call | solution.py:490
  202.0 9.2 %all-to-all-start.2 = ((bf16[128,16,128]{2,1,0:T(8,128)(2,1)}), bf16[128,16,128]{2,1,0:T(8,128)(2,1)S(1)}, u32[]{:S(2)}, u32[]{:S(2)}) async-start(bf16[128,16,128]{2,1,0:T(8,128)(2,1)} %shard_map.97), calls=%async_computation.2 | async-start | bytes 1048576 | tf_op jit(solution)/shard_map/all_to_all | solution.py:654
  211.2 37.9 %shard_map.100 = (bf16[2,128,1280]{2,1,0:T(8,128)(2,1)}, f32[8,1280]{1,0:T(8,128)}) custom-call(bf16[64,8,1280]{2,1,0:T(8,128)(2,1)} %shard_map.99.part_ref, bf16[16,2,128,128]{3,2,1,0:T(8,128)(2,1)} %bitcast.40, bf16[16,2,128,128]{3,2,1,0:T(8,128)(2,1)} %bitcast.41, bf16[640,3072]{1,0:T(8,128)(2,1)} %mine_ref.3, ...), custom_call_target="tpu_custom_call" | custom-call | flops 34359738368 | bytes 16777216 | tf_op jit(solution)/shard_map/pallas_call | solution.py:633
  249.1 2.6 %copy.34 = bf16[128,2,1280]{2,1,0:T(2,128)(2,1)} copy(bf16[128,2,1280]{2,0,1:T(8,128)(2,1)} %bitcast.42) | data formatting | bytes 1310720
  (48 shorter events, 6.3 us)
Async XLA Ops:
  7.2 15.4 %copy-start.6 = (f32[1280]{0:T(1024)S(1)}, f32[1280]{0:T(1024)}, u32[]{:S(2)}) copy-start(f32[1280]{0:T(1024)} %param.8) | copy-start | bytes 15364
  7.2 16.0 %copy-start.7 = (f32[1280]{0:T(1024)S(1)}, f32[1280]{0:T(1024)}, u32[]{:S(2)}) copy-start(f32[1280]{0:T(1024)} %param.9) | copy-start | bytes 15364
  7.2 29.3 %collective-permute-start.2 = (bf16[640,3072]{1,0:T(8,128)(2,1)}, bf16[640,3072]{1,0:T(8,128)(2,1)}, u32[]{:S(2)}, u32[]{:S(2)}) collective-permute-start(bf16[640,3072]{1,0:T(8,128)(2,1)} %mine_ref.3), channel_id=1, source_target_pairs={{0,1},{1,0},{2,3},{3,2},{4,5},{5,4},{6,7},{7,6},{8,9},{9,8},{10,11... | collective-permute-start | bytes 11796488 | tf_op jit(solution)/shard_map/ppermute | solution.py:650
  8.6 21.5 %collective-permute-start.1 = (bf16[512,1280]{1,0:T(8,128)(2,1)}, bf16[512,1280]{1,0:T(8,128)(2,1)S(1)}, u32[]{:S(2)}, u32[]{:S(2)}) collective-permute-start(bf16[512,1280]{1,0:T(8,128)(2,1)} %param.11), channel_id=1, source_target_pairs={{0,1},{1,0},{2,3},{3,2},{4,5},{5,4},{6,7},{7,6},{8,9},{9,8},{10,11... | collective-permute-start | bytes 3932168 | tf_op jit(solution)/shard_map/ppermute | solution.py:650
  9.9 2.2 copy-start
  9.9 20.2 %copy-start.2 = (bf16[512,1280]{1,0:T(8,128)(2,1)S(1)}, bf16[512,1280]{1,0:T(8,128)(2,1)}, u32[]{:S(2)}) copy-start(bf16[512,1280]{1,0:T(8,128)(2,1)} %param.11) | copy-start | bytes 3932164
  10.8 15.0 %collective-permute-start = (bf16[128,1280]{1,0:T(8,128)(2,1)}, bf16[128,1280]{1,0:T(8,128)(2,1)}, u32[]{:S(2)}, u32[]{:S(2)}) collective-permute-start(bf16[128,1280]{1,0:T(8,128)(2,1)} %get-tuple-element.57), channel_id=1, source_target_pairs={{0,4},{4,0},{1,5},{5,1},{2,6},{6,2},{3,7},{7,3},{8,12},{12,8},{9,1... | collective-permute-start | bytes 983048 | tf_op jit(solution)/shard_map/ppermute | solution.py:650
  14.5 15.7 %all-to-all-start = ((f32[32,8,128]{2,1,0:T(8,128)}), f32[32,8,128]{2,1,0:T(8,128)S(1)}, u32[]{:S(2)}, u32[]{:S(2)}) async-start(f32[32,8,128]{2,1,0:T(8,128)} %shard_map.93), calls=%async_computation | async-start | bytes 262144 | tf_op jit(solution)/shard_map/all_to_all | solution.py:654
  22.5 153.1 %all-gather.2.cloned.1.call-start = ((), (), s32[]{:S(2)}) async-start(), calls=%async_computation.3 | async-start | bytes 11141120 | tf_op jit(solution)/shard_map/all_gather | solution.py:679
  30.1 1.7 copy-start.4
  36.5 37.9 %copy-start.1 = (bf16[128,2,1280]{2,0,1:T(8,128)(2,1)S(1)}, bf16[128,2,1280]{2,0,1:T(8,128)(2,1)}, u32[]{:S(2)}) copy-start(bf16[128,2,1280]{2,0,1:T(8,128)(2,1)} %copy.37) | copy-start | bytes 1966084
  74.4 121.0 %collective-permute-start.4 = (bf16[2,128,1280]{2,1,0:T(8,128)(2,1)S(1)}, bf16[2,128,1280]{2,1,0:T(8,128)(2,1)S(1)}, u32[]{:S(2)}, u32[]{:S(2)}) collective-permute-start(bf16[2,128,1280]{2,1,0:T(8,128)(2,1)S(1)} %bitcast.36), channel_id=1, source_target_pairs={{0,1},{1,0},{2,3},{3,2},{4,5},{5,4},{6,7},{7,6},{8,9},{9,8},{10,11... | collective-permute-start | bytes 1966088 | tf_op jit(solution)/shard_map/ppermute | solution.py:650
  169.9 32.2 %all-to-all-start.1 = ((bf16[32,128,128]{2,1,0:T(8,128)(2,1)}), bf16[32,128,128]{2,1,0:T(8,128)(2,1)S(1)}, u32[]{:S(2)}, u32[]{:S(2)}) async-start(bf16[32,128,128]{2,1,0:T(8,128)(2,1)} %get-tuple-element.30.dkv_ref), calls=%async_computation.1 | async-start | bytes 2097152 | tf_op jit(solution)/shard_map/all_to_all | solution.py:654
  191.7 3.7 %collective-permute-start.3 = (bf16[2,128,1024]{2,1,0:T(8,128)(2,1)}, bf16[2,128,1024]{2,1,0:T(8,128)(2,1)S(1)}, u32[]{:S(2)}, u32[]{:S(2)}) collective-permute-start(bf16[2,128,1024]{2,1,0:T(8,128)(2,1)} %get-tuple-element.33.att_ref), channel_id=1, source_target_pairs={{0,1},{1,0},{2,3},{3,2},{4,5},{5,4},{6,7},{7,6},{8,9},{9,8},{10,11... | collective-permute-start | bytes 1572872 | tf_op jit(solution)/shard_map/ppermute | solution.py:650
  195.4 0.8 copy-start.8
  196.3 0.8 copy-start.9
  202.0 9.2 %copy-start.3 = (bf16[32,128,128]{2,1,0:T(8,128)(2,1)}, bf16[32,128,128]{2,1,0:T(8,128)(2,1)S(1)}, u32[]{:S(2)}) copy-start(bf16[32,128,128]{2,1,0:T(8,128)(2,1)S(1)} %all-to-all-done.1) | copy-start | bytes 3145732
  202.0 49.7 %all-to-all-start.2 = ((bf16[128,16,128]{2,1,0:T(8,128)(2,1)}), bf16[128,16,128]{2,1,0:T(8,128)(2,1)S(1)}, u32[]{:S(2)}, u32[]{:S(2)}) async-start(bf16[128,16,128]{2,1,0:T(8,128)(2,1)} %shard_map.97), calls=%async_computation.2 | async-start | bytes 1048576 | tf_op jit(solution)/shard_map/all_to_all | solution.py:654
  249.1 4.0 %copy-start.5 = (f32[8,1280]{1,0:T(8,128)S(1)}, f32[8,1280]{1,0:T(8,128)}, u32[]{:S(2)}) copy-start(f32[8,1280]{1,0:T(8,128)} %get-tuple-element.67) | copy-start | bytes 122884
Sparse Core Ops, SparseCore 0:
  74.5 93.5 all-gather.1

commit v6 on v5

--- a/solution.py
+++ b/solution.py
@@ -13,7 +13,6 @@
 GROUPS = 32
 SCALE = HEAD ** (-0.5)
 SEQ = ("y", "z", "xl")
-LINE = ("y", "z", "xl", "rep")
 ALL = ("y", "z", "xl", "rep", "own")
 F32, BF16 = jnp.float32, jnp.bfloat16
 VMEM = 60 << 20
@@ -433,140 +432,104 @@
     return jnp.where(low, first.astype(F32), pltpu.roll(second.astype(F32), HEAD, 1)).astype(BF16)
 
 
-def mixed_kernel(own_ref, dqo_ref, lat_ref, w_ref, mixed_ref, att_ref):
-    half = w_ref.shape[1]
+def shifted(here, k, sign):
+    dy, dz, dx = k // 8, (k // 2) % 4, k % 2
+    y = (here[0] + (dy if sign > 0 else 4 - dy)) % 4
+    z = (here[1] + (dz if sign > 0 else 4 - dz)) % 4
+    x = (here[2] + dx) % 2
+    return {"y": y, "z": z, "xl": x}, (y * 4 + z) * 2 + x
+
+
+def tail_kernel(
+    count, dqo_ref, dkv_ref, mine_ref, other_ref, halves_ref, lat_ref, cot_ref, cot_far_ref, chan_ref, gain_ref,
+    out_ref, weight_ref, mixed_ref, rows_ref, grad_ref, near_ref, far_ref, got_ref, part_ref, att_ref, att_far_ref,
+    give_ref, take_ref, part_send, part_recv, sums_send, sums_recv, att_send, att_recv, give_send, give_recv,
+):
+    here = place()
+    own = here[4]
+    seqs = far_ref.shape[0]
+    line = (here[0] * 4 + here[1]) * 2 + here[2]
+    mesh_id = pl.DeviceIdType.MESH
+
+    barrier = pltpu.get_barrier_semaphore()
+
+    @pl.loop(1, seqs)
+    def _(k):
+        pl.semaphore_signal(barrier, inc=1, device_id=shifted(here, k, 1)[0], device_id_type=mesh_id)
+
+    pl.semaphore_signal(barrier, inc=1, device_id={"own": 1 - own}, device_id_type=mesh_id)
+    pl.semaphore_signal(barrier, inc=1, device_id={"rep": 1 - here[3]}, device_id_type=mesh_id)
+    pl.semaphore_wait(barrier, seqs + 1)
+
+    def pair(at):
+        return pl.ds(at * 2, 2)
+
+    def part_copy(k):
+        target, there = shifted(here, k, 1)
+        return pltpu.make_async_remote_copy(
+            src_ref=part_ref.at[pair(there)], dst_ref=got_ref.at[pair(line)],
+            send_sem=part_send.at[k], recv_sem=part_recv.at[k],
+            device_id=target, device_id_type=mesh_id,
+        )
+
+    def part_arrival(k):
+        source, there = shifted(here, k, -1)
+        return pltpu.make_async_remote_copy(
+            src_ref=part_ref.at[pair(there)], dst_ref=got_ref.at[pair(there)],
+            send_sem=part_send.at[k], recv_sem=part_recv.at[k],
+            device_id=source, device_id_type=mesh_id,
+        )
+
+    def sums_copy(k):
+        target, _ = shifted(here, k, 1)
+        return pltpu.make_async_remote_copy(
+            src_ref=near_ref, dst_ref=far_ref.at[line],
+            send_sem=sums_send.at[k], recv_sem=sums_recv.at[k],
+            device_id=target, device_id_type=mesh_id,
+        )
+
+    def sums_arrival(k):
+        source, there = shifted(here, k, -1)
+        return pltpu.make_async_remote_copy(
+            src_ref=near_ref, dst_ref=far_ref.at[there],
+            send_sem=sums_send.at[k], recv_sem=sums_recv.at[k],
+            device_id=source, device_id_type=mesh_id,
+        )
+
+    inner, half = HEADS * HEAD, mine_ref.shape[0]
     low = lax.broadcasted_iota(jnp.int32, (128, 128), 1) < HEAD
     for h in range(0, HEADS, 2):
         for i in range(2):
-            att_ref[i, :, h * HEAD : (h + 2) * HEAD] = paired(dqo_ref[h, i], dqo_ref[h + 1, i], low, True)
-    own = own_ref[0]
+            att_ref[i * 128 : (i + 1) * 128, h * HEAD : (h + 2) * HEAD] = paired(dqo_ref[h, i], dqo_ref[h + 1, i], low, True)
+    swap = pltpu.make_async_remote_copy(
+        src_ref=att_ref, dst_ref=att_far_ref, send_sem=att_send, recv_sem=att_recv,
+        device_id={"own": 1 - own}, device_id_type=pl.DeviceIdType.MESH,
+    )
+    swap.start()
+    wide = halves_ref.shape[1]
+    near = att_ref[:, pl.ds(pl.multiple_of(own * wide, 128), wide)]
+    far = att_ref[:, pl.ds(pl.multiple_of((1 - own) * wide, 128), wide)]
+    total = jnp.dot(near, halves_ref[0], preferred_element_type=F32)
+    total = total + jnp.dot(far, halves_ref[1], preferred_element_type=F32)
     for i in range(2):
-        near = att_ref[i, :, pl.ds(pl.multiple_of(own * half, 128), half)]
-        far = att_ref[i, :, pl.ds(pl.multiple_of((1 - own) * half, 128), half)]
-        total = jnp.dot(near, w_ref[0], preferred_element_type=F32)
-        total = total + jnp.dot(far, w_ref[1], preferred_element_type=F32)
-        mixed_ref[i] = (lat_ref[i].astype(F32) + total).astype(BF16)
-
-
-def mix(own, dqo, lat, halves):
-    channels = lat.shape[2]
-
-    def whole(*shape):
-        return pl.BlockSpec(shape, lambda s, own: (0,) * len(shape))
-
-    return pl.pallas_call(
-        mixed_kernel,
-        grid_spec=pltpu.PrefetchScalarGridSpec(
-            num_scalar_prefetch=1,
-            grid=(1,),
-            in_specs=[whole(*dqo.shape), whole(*lat.shape), whole(*halves.shape)],
-            out_specs=[whole(*lat.shape), whole(2, 128, HEADS * HEAD)],
-        ),
-        out_shape=[
-            jax.ShapeDtypeStruct(lat.shape, BF16),
-            jax.ShapeDtypeStruct((2, 128, HEADS * HEAD), BF16),
-        ],
-        compiler_params=pltpu.CompilerParams(vmem_limit_bytes=VMEM),
-        cost_estimate=pl.CostEstimate(flops=2 * 256 * 1280 * 1024, bytes_accessed=6 << 20, transcendentals=0),
-    )(own, dqo, lat, halves)
-
-
-def out_weight_kernel(own_ref, att_ref, att_far_ref, cot_ref, cot_far_ref, out_ref):
+        mixed_ref[i] = (lat_ref[i].astype(F32) + total[i * 128 : (i + 1) * 128]).astype(BF16)
+    swap.wait()
     channels = cot_ref.shape[2]
-    wide = att_ref.shape[2]
-    att = jnp.concatenate([att_ref[...].reshape(256, wide), att_far_ref[...].reshape(256, wide)], axis=0)
-    cot = jnp.concatenate([cot_ref[...].reshape(256, channels), cot_far_ref[...].reshape(256, channels)], axis=0)
-    total = lax.dot_general(att, cot, (((0,), (0,)), ((), ())), preferred_element_type=F32)
-    blocks = total.reshape(wide // 16, 2, 8, channels)
-    own = own_ref[0]
-    out_ref[...] = jnp.where(own == 0, blocks[:, 0], blocks[:, 1]).astype(BF16)
-
-
-def out_weight(own, att, att_far, cot, cot_far):
-    channels, wide = cot.shape[2], att.shape[2]
-    tile = 256
-    side = pl.BlockSpec((2, 128, tile), lambda s, own: (0, 0, s))
-    full = pl.BlockSpec(cot.shape, lambda s, own: (0, 0, 0))
-    return pl.pallas_call(
-        out_weight_kernel,
-        grid_spec=pltpu.PrefetchScalarGridSpec(
-            num_scalar_prefetch=1,
-            grid=(wide // tile,),
-            in_specs=[side, side, full, full],
-            out_specs=pl.BlockSpec((tile // 16, 8, channels), lambda s, own: (s, 0, 0)),
-        ),
-        out_shape=jax.ShapeDtypeStruct((wide // 16, 8, channels), BF16),
-        compiler_params=pltpu.CompilerParams(vmem_limit_bytes=VMEM),
-        cost_estimate=pl.CostEstimate(flops=4 * 256 * 1280 * 1024, bytes_accessed=6 << 20, transcendentals=0),
-    )(own, att, att_far, cot, cot_far)
-
-
-def shifted(here, k, sign):
-    dy, dz, dx, dr = k // 16, (k // 4) % 4, (k // 2) % 2, k % 2
-    y = (here[0] + (dy if sign > 0 else 4 - dy)) % 4
-    z = (here[1] + (dz if sign > 0 else 4 - dz)) % 4
-    x = (here[2] + dx) % 2
-    r = (here[3] + dr) % 2
-    return {"y": y, "z": z, "xl": x, "rep": r}, ((y * 4 + z) * 2 + x) * 2 + r
-
-
-def tail_kernel(
-    count, part_ref, dqo_ref, dkv_ref, mine_ref, other_ref, lat_ref, cot_ref, chan_ref, gain_ref,
-    out_ref, weight_ref, rows_ref, grad_ref, near_ref, far_ref, got_ref,
-    part_send, part_recv, sums_send, sums_recv,
-):
-    here = place()
-    own = here[4]
-    lines, seqs = part_ref.shape[0], far_ref.shape[0]
-    block = ((here[0] * 4 + here[1]) * 2 + here[2]) * 2 + here[3]
-    line = block // 2
-
-    barrier = pltpu.get_barrier_semaphore()
-
-    @pl.loop(1, lines)
-    def _(k):
-        pl.semaphore_signal(barrier, inc=1, device_id=shifted(here, k, 1)[0], device_id_type=pl.DeviceIdType.MESH)
-
-    pl.semaphore_wait(barrier, lines - 1)
-
-    def part_copy(k):
-        target, there = shifted(here, k, 1)
-        return pltpu.make_async_remote_copy(
-            src_ref=part_ref.at[there], dst_ref=got_ref.at[block],
-            send_sem=part_send.at[k], recv_sem=part_recv.at[k],
-            device_id=target, device_id_type=pl.DeviceIdType.MESH,
-        )
-
-    def part_arrival(k):
-        source, there = shifted(here, k, -1)
-        return pltpu.make_async_remote_copy(
-            src_ref=part_ref.at[there], dst_ref=got_ref.at[there],
-            send_sem=part_send.at[k], recv_sem=part_recv.at[k],
-            device_id=source, device_id_type=pl.DeviceIdType.MESH,
-        )
-
-    def sums_copy(k):
-        target, _ = shifted(here, 2 * k, 1)
-        return pltpu.make_async_remote_copy(
-            src_ref=near_ref, dst_ref=far_ref.at[line],
-            send_sem=sums_send.at[k], recv_sem=sums_recv.at[k],
-            device_id=target, device_id_type=pl.DeviceIdType.MESH,
-        )
-
-    def sums_arrival(k):
-        source, there = shifted(here, 2 * k, -1)
-        return pltpu.make_async_remote_copy(
-            src_ref=near_ref, dst_ref=far_ref.at[there // 2],
-            send_sem=sums_send.at[k], recv_sem=sums_recv.at[k],
-            device_id=source, device_id_type=pl.DeviceIdType.MESH,
-        )
-
-    @pl.loop(1, lines)
-    def _(k):
-        part_copy(k).start()
-
-    inner, half = HEADS * HEAD, mine_ref.shape[0]
-    low = lax.broadcasted_iota(jnp.int32, (128, 128), 1) < HEAD
+    cot, cot_far = cot_ref[...].reshape(256, channels), cot_far_ref[...].reshape(256, channels)
+    for j in range(4):
+        row = (here[0] + (j + 1)) % 4
+        at = pl.ds(pl.multiple_of(row * 256, 256), 256)
+        total = lax.dot_general(att_ref[:, at], cot, (((0,), (0,)), ((), ())), preferred_element_type=F32)
+        total = total + lax.dot_general(
+            att_far_ref[:, at], cot_far, (((0,), (0,)), ((), ())), preferred_element_type=F32
+        )
+        blocks = total.reshape(16, 2, 8, channels)
+        part_ref[pl.ds(row * 16, 16)] = jnp.where(own == 0, blocks[:, 0], blocks[:, 1]).astype(BF16)
+
+        @pl.loop(0 if j < 3 else 1, 8)
+        def _(k):
+            part_copy(((j + 1) % 4) * 8 + k).start()
+
     for h in range(0, HEADS, 2):
         for i in range(2):
             rows, at = slice(i * 128, (i + 1) * 128), h * HEAD
@@ -596,7 +559,7 @@
     def _(k):
         sums_copy(k).start()
 
-    got_ref[block] = part_ref[block]
+    got_ref[pair(line)] = part_ref[pair(line)]
 
     @pl.loop(1, seqs)
     def _(k):
@@ -609,16 +572,25 @@
         grad = inv * (grad_ref[i] - means[i : i + 1] - centred * means[2 + i : 3 + i])
         out_ref[i] = (cot_ref[i].astype(F32) + grad).astype(BF16)
 
-    @pl.loop(1, lines)
+    @pl.loop(1, seqs)
     def _(k):
         part_arrival(k).wait_recv()
 
     total = got_ref[0:8].astype(F32)
-    for k in range(8, lines, 8):
+    for k in range(8, 2 * seqs, 8):
         total = total + got_ref[k : k + 8].astype(F32)
-    weight_ref[...] = jnp.sum(total, axis=0)
-
-    @pl.loop(1, lines)
+    pairs = jnp.sum(total.reshape(4, 2, 8, channels), axis=0)
+    upper = here[3] == 1
+    give_ref[...] = jnp.where(upper, pairs[0], pairs[1])
+    give = pltpu.make_async_remote_copy(
+        src_ref=give_ref, dst_ref=take_ref, send_sem=give_send, recv_sem=give_recv,
+        device_id={"rep": 1 - here[3]}, device_id_type=mesh_id,
+    )
+    give.start()
+    give.wait()
+    weight_ref[...] = jnp.where(upper, pairs[1], pairs[0]) + take_ref[...]
+
+    @pl.loop(1, seqs)
     def _(k):
         part_copy(k).wait_send()
 
@@ -627,23 +599,33 @@
         sums_copy(k).wait_send()
 
 
-def tail(part, dqo, dkv, mine, other, lat, cot, chan, gain, count):
-    lines, channels = part.shape[0], part.shape[2]
+def tail(dqo, dkv, mine, other, halves, lat, cot, cot_far, chan, gain, count):
+    channels, wide = lat.shape[2], HEADS * HEAD
+    seqs = wide // 32
     dma = pltpu.SemaphoreType.DMA
     return pl.pallas_call(
         functools.partial(tail_kernel, count),
-        out_shape=[jax.ShapeDtypeStruct(lat.shape, BF16), jax.ShapeDtypeStruct((8, channels), F32)],
+        out_shape=[
+            jax.ShapeDtypeStruct(lat.shape, BF16),
+            jax.ShapeDtypeStruct((8, channels), F32),
+            jax.ShapeDtypeStruct(lat.shape, BF16),
+        ],
         scratch_shapes=[
             pltpu.VMEM((256, 3 * HEADS * HEAD), BF16),
             pltpu.VMEM(lat.shape, F32),
             pltpu.VMEM((8, 128), F32),
-            pltpu.VMEM((lines // 2, 8, 128), F32),
-            pltpu.VMEM(part.shape, BF16),
-            dma((lines,)), dma((lines,)), dma((lines // 2,)), dma((lines // 2,)),
+            pltpu.VMEM((seqs, 8, 128), F32),
+            pltpu.VMEM((2 * seqs, 8, channels), BF16),
+            pltpu.VMEM((2 * seqs, 8, channels), BF16),
+            pltpu.VMEM((256, wide), BF16),
+            pltpu.VMEM((256, wide), BF16),
+            pltpu.VMEM((8, channels), F32),
+            pltpu.VMEM((8, channels), F32),
+            dma((seqs,)), dma((seqs,)), dma((seqs,)), dma((seqs,)), dma, dma, dma, dma,
         ],
         compiler_params=pltpu.CompilerParams(vmem_limit_bytes=VMEM, collective_id=1, has_side_effects=True),
         cost_estimate=pl.CostEstimate(flops=2 << 34, bytes_accessed=16 << 20, transcendentals=0),
-    )(part, dqo, dkv, mine, other, lat, cot, chan, gain)
+    )(dqo, dkv, mine, other, halves, lat, cot, cot_far, chan, gain)
 
 
 def swapped(value, axis):
@@ -673,7 +655,7 @@
     halves_out = jnp.stack([proj_out, other_out])
     cot_far = swapped(cot, "own")
     g = attended_grad(own, cot, halves_out)
-    pair_lat, sums = lax.optimization_barrier((pair_lat, sums))
+    pair_lat, g = lax.optimization_barrier((pair_lat, g))
     chan, kvqg = project(lat, sums, gain, shift, g, proj_qkv, other_qkv, count)
     pair_lat, kvqg = lax.optimization_barrier((pair_lat, kvqg))
     image_lat = lax.all_gather(pair_lat, ("y", "z"), tiled=True)
@@ -685,13 +667,11 @@
     in_part = in_weight(image_lat, chan_image, gain, shift, dqo, dkv)
     dqo_tok, in_part = lax.optimization_barrier((dqo_tok, in_part))
     dqo_tok = dqo_tok.reshape(HEADS, images, 128, 128)
-    mixed, att = mix(own, dqo_tok, lat, halves_out)
-    out_part = out_weight(own, att, swapped(att, "own"), cot, cot_far)
-    dkv_tok, out_part, in_part = lax.optimization_barrier((dkv_tok, out_part, in_part))
+    dkv_tok, in_part = lax.optimization_barrier((dkv_tok, in_part))
     in_blocks = exchanged(in_part, ALL)
     dkv_tok = dkv_tok.reshape(HEADS, images, 128, 128)
-    grad_latent, grad_out = tail(
-        out_part, dqo_tok, dkv_tok, proj_qkv, other_qkv, lat, cot, chan, gain, count
+    grad_latent, grad_out, mixed = tail(
+        dqo_tok, dkv_tok, proj_qkv, other_qkv, halves_out, lat, cot, cot_far, chan, gain, count
     )
 
     summed = jnp.sum(in_blocks.reshape(HEADS, 8, 16, 128).astype(F32), axis=1)

time: 262 us -> 256 us (0.977)
    pallas_call x2 -> x0, Pallas kernels: 9.17 us -> none  [the longest x1 4.98 us: out_weight(): pl.pallas_call(out_weight_kernel, grid_spec=pltpu.PrefetchScalarGridSpec(...]
    pallas_call x1, Pallas kernels: 37.9 us -> 43.2 us  [tail(): pl.pallas_call(functools.partial(tail_kernel, count), out_shape=[jax.Shap...]
    ppermute x5 -> x4, starting transfers between devices: 5.84 us -> 5.84 us  [swapped(): return lax.ppermute(value, axis, [(0, 1), (1, 0)])]
  transfers between devices with their start and end apart: 9 -> 8, of which waited for: 1 -> 0; matrix products, arithmetic and copies ran while one was open for 6% -> 6% of each run, Pallas kernels for 61% -> 61%
where the time goes in v6:
time: 256 us; the launch traced here: 255 us
  Pallas kernels  195 us (76%)
  starting transfers between devices  27 us (11%)
  between operations  14.2 us (6%)
  local copies, waits for them, and re-layouts  12.3 us (5%)
  other arithmetic  6.17 us (2%)
    pallas_call x1, Pallas kernels, attention(): pl.pallas_call(functools.partial(attention_kernel, ck), grid=(sources //...  92.9 us
    pallas_call x1, Pallas kernels, tail(): pl.pallas_call(functools.partial(tail_kernel, count), out_shape=[jax.Shap...  43.2 us
    pallas_call x1, Pallas kernels, project(): pl.pallas_call(functools.partial(project_kernel, count), in_specs=[whole]...  40 us
    all_to_all x3, starting transfers between devices, exchanged(): return lax.all_to_all(value, axes, 0, 0, tiled=True)  21.1 us
    pallas_call x1, Pallas kernels, in_weight(): pl.pallas_call(in_weight_kernel, grid=(sources // here,), in_specs=[pl.Bl...  11.9 us
    unnamed x25, local copies, waits for them, and re-layouts  10.5 us
    ppermute x4, starting transfers between devices, swapped(): return lax.ppermute(value, axis, [(0, 1), (1, 0)])  5.84 us
  transfers between devices with their start and end apart: 8, of which 0 were waited for; matrix products, arithmetic and copies ran while one was open for 6% of the time, Pallas kernels for 61%

profile of v6, /device:TPU:1, one launch (start us, length us, event | category | flops | bytes accessed | tf_op | source)
XLA Modules:
  0.0 254.8 jit_solution(2812949313193316997)
XLA Ops:
  7.2 1.5 collective-permute-start.2
  8.7 1.2 copy.38
  9.9 0.9 broadcast_select_fusion
  10.8 1.3 collective-permute-start
  12.1 2.3 shard_map.94
  14.5 8.1 %all-to-all-start = ((f32[32,8,128]{2,1,0:T(8,128)}), f32[32,8,128]{2,1,0:T(8,128)S(1)}, u32[]{:S(2)}, u32[]{:S(2)}) async-start(f32[32,8,128]{2,1,0:T(8,128)} %shard_map.94), calls=%async_computation | async-start | bytes 262144 | tf_op jit(solution)/shard_map/all_to_all | solution.py:636
  22.6 2.0 copy.37
  25.8 2.2 maximum_select_fusion
  28.0 1.7 pad_maximum_fusion.w_ref.halves_ref
  29.7 4.6 %shard_map.93.g_ref = bf16[16,2,64,128]{3,2,1,0:T(8,128)(2,1)} custom-call(s32[1]{0:T(128)} %bitcast.3.own_ref, bf16[2,128,1280]{2,1,0:T(8,128)(2,1)} %bitcast.32, bf16[2,512,1280]{2,1,0:T(8,128)(2,1)} %pad_maximum_fusion.w_ref.halves_ref), custom_call_target="tpu_custom_call" | custom-call | flops 671088640 | bytes 4194304 | tf_op jit(solution)/shard_map/pallas_call | solution.py:202
  34.3 0.6 copy-done.4
  35.0 40.0 %shard_map.95 = (f32[8,1280]{1,0:T(8,128)}, bf16[32,256,128]{2,1,0:T(8,128)(2,1)}) custom-call(bf16[2,128,1280]{2,1,0:T(8,128)(2,1)} %bitcast.30, f32[32,8,128]{2,1,0:T(8,128)} %copy-done.4, f32[1,1280]{1,0:T(1,128)} %reshape.41.gain_ref, f32[1,1280]{1,0:T(1,128)} %reshape.42.shift_ref, bf16[16,2,64,128]{3,2,1,0:T(8,128)(2,1)} %shard_map.93.g_ref, ...), custom_call_target="tpu_custom_call" | custom-call | flops 34359738368 | bytes 12582912 | tf_op jit(solution)/shard_map/pallas_call | solution.py:168
  75.1 92.9 %shard_map.96 = (bf16[32,128,128]{2,1,0:T(8,128)(2,1)}, bf16[32,128,128]{2,1,0:T(8,128)(2,1)}, bf16[32,128,128]{2,1,0:T(8,128)(2,1)}) custom-call(bf16[32,256,128]{2,1,0:T(8,128)(2,1)} %get-tuple-element.23.kvq_ref), custom_call_target="tpu_custom_call" | custom-call | flops 51539607552 | bytes 4194304 | tf_op jit(solution)/shard_map/pallas_call | solution.py:347
  167.9 3.9 %all-to-all-start.1 = ((bf16[32,128,128]{2,1,0:T(8,128)(2,1)}), bf16[32,128,128]{2,1,0:T(8,128)(2,1)S(1)}, u32[]{:S(2)}, u32[]{:S(2)}) async-start(bf16[32,128,128]{2,1,0:T(8,128)(2,1)} %get-tuple-element.28.dkv_ref), calls=%async_computation.1 | async-start | bytes 2097152 | tf_op jit(solution)/shard_map/all_to_all | solution.py:636
  171.9 3.0 %collective-permute-start.3 = (bf16[2,128,1280]{2,1,0:T(8,128)(2,1)S(1)}, bf16[2,128,1280]{2,1,0:T(8,128)(2,1)S(1)}, u32[]{:S(2)}, u32[]{:S(2)}) collective-permute-start(bf16[2,128,1280]{2,1,0:T(8,128)(2,1)S(1)} %bitcast.34), channel_id=1, source_target_pairs={{0,1},{1,0},{2,3},{3,2},{4,5},{5,4},{6,7},{7,6},{8,9},{9,8},{10,11... | collective-permute-start | bytes 1966088 | tf_op jit(solution)/shard_map/ppermute | solution.py:632
  174.9 0.6 broadcast_select_fusion.1.chan_ref
  175.5 11.9 %shard_map.97 = bf16[128,16,128]{2,1,0:T(8,128)(2,1)} custom-call(bf16[32,128,1280]{2,1,0:T(8,128)(2,1)} %all-gather.2.cloned.1.call-done.lat_ref, f32[2,1280]{1,0:T(2,128)} %broadcast_select_fusion.1.chan_ref, f32[1,1280]{1,0:T(1,128)} %reshape.41.gain_ref, f32[1,1280]{1,0:T(1,128)} %reshape.42.shift_ref, bf16[32,128,128]{2,1,0:T(8,128)(2,1)} %get-tuple-element.27.dqo_ref, ...), custom_call_target="tpu_custom_call" | custom-call | flops 2684354560 | bytes 14680064 | tf_op jit(solution)/shard_map/pallas_call | solution.py:408
  187.5 9.1 %all-to-all-start.2 = ((bf16[128,16,128]{2,1,0:T(8,128)(2,1)}), bf16[128,16,128]{2,1,0:T(8,128)(2,1)S(1)}, u32[]{:S(2)}, u32[]{:S(2)}) async-start(bf16[128,16,128]{2,1,0:T(8,128)(2,1)} %shard_map.97), calls=%async_computation.2 | async-start | bytes 1048576 | tf_op jit(solution)/shard_map/all_to_all | solution.py:636
  196.6 0.8 copy-done.9
  197.5 43.2 %shard_map.98 = (bf16[2,128,1280]{2,1,0:T(8,128)(2,1)}, f32[8,1280]{1,0:T(8,128)}, bf16[2,128,1280]{2,1,0:T(8,128)(2,1)}) custom-call(bf16[16,2,128,128]{3,2,1,0:T(8,128)(2,1)} %bitcast.41, bf16[16,2,128,128]{3,2,1,0:T(8,128)(2,1)} %bitcast.37, bf16[640,3072]{1,0:T(8,128)(2,1)} %mine_ref.3, bf16[640,3072]{1,0:T(8,128)(2,1)} %collective-permute-done.2.other_ref, ...), custom_call_target="tpu_custom_call" | custom-call | flops 34359738368 | bytes 16777216 | tf_op jit(solution)/shard_map/pallas_call | solution.py:606
  240.7 2.6 %copy.33 = bf16[128,2,1280]{2,1,0:T(2,128)(2,1)} copy(bf16[128,2,1280]{2,0,1:T(8,128)(2,1)} %bitcast.39) | data formatting | bytes 1310720
  243.3 2.6 %copy.34 = bf16[128,2,1280]{2,1,0:T(2,128)(2,1)} copy(bf16[128,2,1280]{2,0,1:T(8,128)(2,1)} %bitcast.38) | data formatting | bytes 1310720
  246.6 0.7 pad_maximum_fusion.1
  247.3 0.6 copy.40
  (44 shorter events, 2.1 us)
Async XLA Ops:
  7.2 17.4 %copy-start.7 = (f32[1280]{0:T(1024)S(1)}, f32[1280]{0:T(1024)}, u32[]{:S(2)}) copy-start(f32[1280]{0:T(1024)} %param.8) | copy-start | bytes 15364
  7.2 18.0 %copy-start.8 = (f32[1280]{0:T(1024)S(1)}, f32[1280]{0:T(1024)}, u32[]{:S(2)}) copy-start(f32[1280]{0:T(1024)} %param.9) | copy-start | bytes 15364
  7.2 27.1 %collective-permute-start.2 = (bf16[640,3072]{1,0:T(8,128)(2,1)}, bf16[640,3072]{1,0:T(8,128)(2,1)}, u32[]{:S(2)}, u32[]{:S(2)}) collective-permute-start(bf16[640,3072]{1,0:T(8,128)(2,1)} %mine_ref.3), channel_id=1, source_target_pairs={{0,1},{1,0},{2,3},{3,2},{4,5},{5,4},{6,7},{7,6},{8,9},{9,8},{10,11... | collective-permute-start | bytes 11796488 | tf_op jit(solution)/shard_map/ppermute | solution.py:632
  8.6 19.4 %collective-permute-start.1 = (bf16[512,1280]{1,0:T(8,128)(2,1)}, bf16[512,1280]{1,0:T(8,128)(2,1)S(1)}, u32[]{:S(2)}, u32[]{:S(2)}) collective-permute-start(bf16[512,1280]{1,0:T(8,128)(2,1)} %param.11), channel_id=1, source_target_pairs={{0,1},{1,0},{2,3},{3,2},{4,5},{5,4},{6,7},{7,6},{8,9},{9,8},{10,11... | collective-permute-start | bytes 3932168 | tf_op jit(solution)/shard_map/ppermute | solution.py:632
  9.9 2.2 copy-start
  9.9 18.1 %copy-start.2 = (bf16[512,1280]{1,0:T(8,128)(2,1)S(1)}, bf16[512,1280]{1,0:T(8,128)(2,1)}, u32[]{:S(2)}) copy-start(bf16[512,1280]{1,0:T(8,128)(2,1)} %param.11) | copy-start | bytes 3932164
  10.8 15.0 %collective-permute-start = (bf16[128,1280]{1,0:T(8,128)(2,1)}, bf16[128,1280]{1,0:T(8,128)(2,1)}, u32[]{:S(2)}, u32[]{:S(2)}) collective-permute-start(bf16[128,1280]{1,0:T(8,128)(2,1)} %get-tuple-element.53), channel_id=1, source_target_pairs={{0,4},{4,0},{1,5},{5,1},{2,6},{6,2},{3,7},{7,3},{8,12},{12,8},{9,1... | collective-permute-start | bytes 983048 | tf_op jit(solution)/shard_map/ppermute | solution.py:632
  14.5 19.9 %all-to-all-start = ((f32[32,8,128]{2,1,0:T(8,128)}), f32[32,8,128]{2,1,0:T(8,128)S(1)}, u32[]{:S(2)}, u32[]{:S(2)}) async-start(f32[32,8,128]{2,1,0:T(8,128)} %shard_map.94), calls=%async_computation | async-start | bytes 262144 | tf_op jit(solution)/shard_map/all_to_all | solution.py:636
  22.5 153.0 %all-gather.2.cloned.1.call-start = ((), (), s32[]{:S(2)}) async-start(), calls=%async_computation.3 | async-start | bytes 11141120 | tf_op jit(solution)/shard_map/all_gather | solution.py:661
  34.3 0.7 copy-start.4
  75.0 96.8 %copy-start.1 = (bf16[128,2,1280]{2,0,1:T(8,128)(2,1)S(1)}, bf16[128,2,1280]{2,0,1:T(8,128)(2,1)}, u32[]{:S(2)}) copy-start(bf16[128,2,1280]{2,0,1:T(8,128)(2,1)} %copy.37) | copy-start | bytes 1966084
  75.0 99.8 %copy-start.6 = (f32[8,1280]{1,0:T(8,128)S(1)}, f32[8,1280]{1,0:T(8,128)}, u32[]{:S(2)}) copy-start(f32[8,1280]{1,0:T(8,128)} %get-tuple-element.26.chan_ref) | copy-start | bytes 122884
  167.9 19.5 %all-to-all-start.1 = ((bf16[32,128,128]{2,1,0:T(8,128)(2,1)}), bf16[32,128,128]{2,1,0:T(8,128)(2,1)S(1)}, u32[]{:S(2)}, u32[]{:S(2)}) async-start(bf16[32,128,128]{2,1,0:T(8,128)(2,1)} %get-tuple-element.28.dkv_ref), calls=%async_computation.1 | async-start | bytes 2097152 | tf_op jit(solution)/shard_map/all_to_all | solution.py:636
  171.9 24.7 %collective-permute-start.3 = (bf16[2,128,1280]{2,1,0:T(8,128)(2,1)S(1)}, bf16[2,128,1280]{2,1,0:T(8,128)(2,1)S(1)}, u32[]{:S(2)}, u32[]{:S(2)}) collective-permute-start(bf16[2,128,1280]{2,1,0:T(8,128)(2,1)S(1)} %bitcast.34), channel_id=1, source_target_pairs={{0,1},{1,0},{2,3},{3,2},{4,5},{5,4},{6,7},{7,6},{8,9},{9,8},{10,11... | collective-permute-start | bytes 1966088 | tf_op jit(solution)/shard_map/ppermute | solution.py:632
  187.5 9.2 %copy-start.3 = (bf16[32,128,128]{2,1,0:T(8,128)(2,1)}, bf16[32,128,128]{2,1,0:T(8,128)(2,1)S(1)}, u32[]{:S(2)}) copy-start(bf16[32,128,128]{2,1,0:T(8,128)(2,1)S(1)} %all-to-all-done.1) | copy-start | bytes 3145732
  187.5 58.5 %all-to-all-start.2 = ((bf16[128,16,128]{2,1,0:T(8,128)(2,1)}), bf16[128,16,128]{2,1,0:T(8,128)(2,1)S(1)}, u32[]{:S(2)}, u32[]{:S(2)}) async-start(bf16[128,16,128]{2,1,0:T(8,128)(2,1)} %shard_map.97), calls=%async_computation.2 | async-start | bytes 1048576 | tf_op jit(solution)/shard_map/all_to_all | solution.py:636
  196.6 0.8 copy-start.9
  240.7 6.6 %copy-start.5 = (f32[8,1280]{1,0:T(8,128)S(1)}, f32[8,1280]{1,0:T(8,128)}, u32[]{:S(2)}) copy-start(f32[8,1280]{1,0:T(8,128)} %get-tuple-element.63) | copy-start | bytes 122884
Sparse Core Ops, SparseCore 0:
  75.2 92.1 all-gather.1

commit v7 on v6

--- a/solution.py
+++ b/solution.py
@@ -46,22 +46,6 @@
 def four_rows(rows):
     width = rows[0].shape[1]
     return jnp.concatenate([*rows, jnp.zeros((4, width), F32)], axis=0)
-
-
-def stats_kernel(lat_ref, out_ref):
-    values = [lat_ref[i].astype(F32) for i in range(2)]
-    rows = [jnp.sum(v, axis=0, keepdims=True) for v in values]
-    rows += [jnp.sum(v * v, axis=0, keepdims=True) for v in values]
-    out_ref[...] = jnp.broadcast_to(by_group(four_rows(rows), members(lat_ref.shape[2]))[None], out_ref.shape)
-
-
-def stats(lat, copies):
-    return pl.pallas_call(
-        stats_kernel,
-        out_shape=jax.ShapeDtypeStruct((copies, 8, 128), F32),
-        compiler_params=pltpu.CompilerParams(vmem_limit_bytes=VMEM),
-        cost_estimate=pl.CostEstimate(flops=1 << 20, bytes_accessed=lat.size * 2, transcendentals=0),
-    )(lat)
 
 
 def moments(sums, count):
@@ -92,7 +76,7 @@
         pl.semaphore_signal(barrier, inc=1, device_id=device(to), device_id_type=pl.DeviceIdType.MESH)
 
     table = members(lat_ref.shape[2])
-    chan = by_channel(moments(jnp.sum(sums_ref[...], axis=0), count), table)
+    chan = by_channel(moments(sums_ref[...], count), table)
     chan_ref[...] = chan
     for i in range(2):
         centred = (lat_ref[i].astype(F32) - chan[i : i + 1]) * chan[2 + i : 3 + i]
@@ -137,10 +121,11 @@
                 send_ref[one, 192:256] = g_ref[row * 4 + h, i]
                 send_ref[two, 192:256] = g_ref[row * 4 + h + 1, i]
 
-    pl.semaphore_wait(barrier, seqs - 1)
     for j in range(4):
         row = (here[0] + (j + 1)) % 4
         block_row(row)
+        if j == 0:
+            pl.semaphore_wait(barrier, seqs - 1)
         if j < 3:
             @pl.loop(0, 8)
             def _(k):
@@ -162,7 +147,7 @@
 
 def project(lat, sums, gain, shift, g, mine, other, count):
     channels = lat.shape[2]
-    seqs = sums.shape[0]
+    seqs = g.shape[0] * 2
     dma = pltpu.SemaphoreType.DMA
     whole = pl.BlockSpec(memory_space=pltpu.VMEM)
     return pl.pallas_call(
@@ -183,40 +168,84 @@
     )(lat, sums, gain, shift, g, mine, other)
 
 
-def attended_grad_kernel(own_ref, cot_ref, w_ref, out_ref):
-    rows = cot_ref[...].reshape(256, cot_ref.shape[2])
-    grad = lax.dot_general(rows, w_ref[...], (((1,), (1,)), ((), ())), preferred_element_type=F32)
+def first_kernel(
+    lat_ref, cot_ref, mine_ref, other_ref, sums_ref, g_ref, near_ref, far_ref, sums_send, sums_recv
+):
+    here = place()
+    own = here[4]
+    seqs, channels = far_ref.shape[0], lat_ref.shape[2]
+    line = (here[0] * 4 + here[1]) * 2 + here[2]
+    mesh_id = pl.DeviceIdType.MESH
+    barrier = pltpu.get_barrier_semaphore()
+
+    @pl.loop(1, seqs)
+    def _(k):
+        pl.semaphore_signal(barrier, inc=1, device_id=shifted(here, k, 1)[0], device_id_type=mesh_id)
+
+    values = [lat_ref[i].astype(F32) for i in range(2)]
+    rows = [jnp.sum(v, axis=0, keepdims=True) for v in values]
+    rows += [jnp.sum(v * v, axis=0, keepdims=True) for v in values]
+    sums = by_group(four_rows(rows), members(channels))
+    near_ref[...] = sums
+    far_ref[line] = sums
+
+    def sums_copy(k):
+        target, _ = shifted(here, k, 1)
+        return pltpu.make_async_remote_copy(
+            src_ref=near_ref, dst_ref=far_ref.at[line],
+            send_sem=sums_send.at[k], recv_sem=sums_recv.at[k],
+            device_id=target, device_id_type=mesh_id,
+        )
+
+    def sums_arrival(k):
+        source, there = shifted(here, k, -1)
+        return pltpu.make_async_remote_copy(
+            src_ref=near_ref, dst_ref=far_ref.at[there],
+            send_sem=sums_send.at[k], recv_sem=sums_recv.at[k],
+            device_id=source, device_id_type=mesh_id,
+        )
+
+    pl.semaphore_wait(barrier, seqs - 1)
+
+    @pl.loop(1, seqs)
+    def _(k):
+        sums_copy(k).start()
+
+    cot = cot_ref[...].reshape(256, channels)
     low = lax.broadcasted_iota(jnp.int32, (64, 128), 1) < HEAD
-    for h in range(0, grad.shape[1] // HEAD, 2):
-        for i in range(2):
-            first = grad[i * 128 : i * 128 + 64, h * HEAD : (h + 2) * HEAD]
-            second = grad[i * 128 + 64 : (i + 1) * 128, h * HEAD : (h + 2) * HEAD]
-            out_ref[h, i] = jnp.where(low, first, pltpu.roll(second, HEAD, 1)).astype(BF16)
-            out_ref[h + 1, i] = jnp.where(low, pltpu.roll(first, HEAD, 1), second).astype(BF16)
-
-
-def attended_grad(own, cot, halves):
-    channels = cot.shape[2]
-    per = halves.shape[1] // 256
-
+    half = mine_ref.shape[0] // HEAD
+    for side, w_ref in ((own, mine_ref), (1 - own, other_ref)):
+        grad = lax.dot_general(cot, w_ref[...], (((1,), (1,)), ((), ())), preferred_element_type=F32)
+        for h in range(0, half, 2):
+            for i in range(2):
+                upper = grad[i * 128 : i * 128 + 64, h * HEAD : (h + 2) * HEAD]
+                lower = grad[i * 128 + 64 : (i + 1) * 128, h * HEAD : (h + 2) * HEAD]
+                g_ref[side * half + h, i] = jnp.where(low, upper, pltpu.roll(lower, HEAD, 1)).astype(BF16)
+                g_ref[side * half + h + 1, i] = jnp.where(low, pltpu.roll(upper, HEAD, 1), lower).astype(BF16)
+
+    @pl.loop(1, seqs)
+    def _(k):
+        sums_arrival(k).wait()
+
+    sums_ref[...] = jnp.sum(far_ref[...], axis=0)
+
+
+def first(lat, cot, mine, other):
+    dma = pltpu.SemaphoreType.DMA
     return pl.pallas_call(
-        attended_grad_kernel,
-        grid_spec=pltpu.PrefetchScalarGridSpec(
-            num_scalar_prefetch=1,
-            grid=(2 * per,),
-            in_specs=[
-                pl.BlockSpec(cot.shape, lambda s, own: (0, 0, 0)),
-                pl.BlockSpec((None, 256, channels), lambda s, own: (s // per, s % per, 0)),
-            ],
-            out_specs=pl.BlockSpec(
-                (4, 2, 64, 128),
-                lambda s, own: ((s // per + own[0] - 2 * own[0] * (s // per)) * per + s % per, 0, 0, 0),
-            ),
-        ),
-        out_shape=jax.ShapeDtypeStruct((HEADS, 2, 64, 128), BF16),
-        compiler_params=pltpu.CompilerParams(vmem_limit_bytes=VMEM),
-        cost_estimate=pl.CostEstimate(flops=2 * 256 * 1280 * 1024, bytes_accessed=4 << 20, transcendentals=0),
-    )(own, cot, halves)
+        first_kernel,
+        out_shape=[
+            jax.ShapeDtypeStruct((8, 128), F32),
+            jax.ShapeDtypeStruct((HEADS, 2, 64, 128), BF16),
+        ],
+        scratch_shapes=[
+            pltpu.VMEM((8, 128), F32),
+            pltpu.VMEM((2 * HEADS, 8, 128), F32),
+            dma((2 * HEADS,)), dma((2 * HEADS,)),
+        ],
+        compiler_params=pltpu.CompilerParams(vmem_limit_bytes=VMEM, collective_id=4, has_side_effects=True),
+        cost_estimate=pl.CostEstimate(flops=2 << 32, bytes_accessed=6 << 20, transcendentals=0),
+    )(lat, cot, mine, other)
 
 
 def attention_kernel(
@@ -262,8 +291,6 @@
         def _(k):
             to = lax.rem(line + k, sources)
             pl.semaphore_signal(barrier, inc=1, device_id=device(to), device_id_type=pl.DeviceIdType.MESH)
-
-        pl.semaphore_wait(barrier, sources - 1)
 
     low = lax.broadcasted_iota(jnp.int32, (half, width), 1) < HEAD
     xq = kvq_ref[pl.ds(base, here), 128:192, :].reshape(half, width).astype(F32) * SCALE
@@ -314,6 +341,10 @@
             dqo_ref[a, h * 64 : (h + 1) * 64, :] = res[at : at + 64]
             send_ref[base + a, h * 64 : (h + 1) * 64, :] = res[at : at + 64]
 
+    @pl.when(step == 0)
+    def _():
+        pl.semaphore_wait(pltpu.get_barrier_semaphore(), sources - 1)
+
     for a in range(here):
         @pl.when(base + a != line)
         def _():
@@ -640,21 +671,20 @@
     local_len, images, channels = latent.shape
     seq_count = lax.axis_size(SEQ)
     count = local_len * seq_count * (channels // GROUPS)
-    own = lax.axis_index("own").reshape(1)
     gain, shift = norm_gain.reshape(1, channels), norm_shift.reshape(1, channels)
 
     other_out = swapped(proj_out, "own")
     other_qkv = swapped(proj_qkv, "own")
     lat = latent.transpose(1, 0, 2)
-    sums = exchanged(stats(lat, seq_count), SEQ)
     cot = cotangent.transpose(1, 0, 2)
     image = lax.axis_index("xl")
     near = jnp.where(image == 0, lat[0], lat[1])
     far = swapped(jnp.where(image == 0, lat[1], lat[0]), "xl")
-    pair_lat = jnp.where(image == 0, jnp.stack([near, far]), jnp.stack([far, near]))
     halves_out = jnp.stack([proj_out, other_out])
     cot_far = swapped(cot, "own")
-    g = attended_grad(own, cot, halves_out)
+    sums, g = first(lat, cot, proj_out, other_out)
+    far, sums = lax.optimization_barrier((far, sums))
+    pair_lat = jnp.where(image == 0, jnp.stack([near, far]), jnp.stack([far, near]))
     pair_lat, g = lax.optimization_barrier((pair_lat, g))
     chan, kvqg = project(lat, sums, gain, shift, g, proj_qkv, other_qkv, count)
     pair_lat, kvqg = lax.optimization_barrier((pair_lat, kvqg))

time: 256 us -> 251 us (0.980)
  starting transfers between devices: 27 us -> 17.9 us
  waiting for transfers between devices: 0.06 us -> 6.03 us
    all_to_all x3 -> x2, starting transfers between devices: 21.1 us -> 12.8 us  [exchanged(): return lax.all_to_all(value, axes, 0, 0, tiled=True)]
    pallas_call x2 -> x1, Pallas kernels: 6.97 us -> 15.2 us  [first(): pl.pallas_call(first_kernel, out_shape=[jax.ShapeDtypeStruct((8, 128), F3...]
    ppermute x4, waiting for transfers between devices: 0.01 us -> 3.67 us  [swapped(): return lax.ppermute(value, axis, [(0, 1), (1, 0)])]
    pallas_call x1, Pallas kernels: 92.9 us -> 89.6 us  [attention(): pl.pallas_call(functools.partial(attention_kernel, ck), grid=(sources //...]
    pallas_call x1, Pallas kernels: 40 us -> 36.8 us  [project(): pl.pallas_call(functools.partial(project_kernel, count), in_specs=[whole]...]
  transfers between devices with their start and end apart: 8 -> 7, of which waited for: 0 -> 2; matrix products, arithmetic and copies ran while one was open for 6% -> 5% of each run, Pallas kernels for 61% -> 64%
where the time goes in v7:
time: 251 us; the launch traced here: 250 us
  Pallas kernels  197 us (78%)
  starting transfers between devices  17.9 us (7%)
  between operations  14.3 us (6%)
  local copies, waits for them, and re-layouts  10.8 us (4%)
  waiting for transfers between devices  6.03 us (2%)
  other arithmetic  4.06 us (2%)
    pallas_call x1, Pallas kernels, attention(): pl.pallas_call(functools.partial(attention_kernel, ck), grid=(sources //...  89.6 us
    pallas_call x1, Pallas kernels, tail(): pl.pallas_call(functools.partial(tail_kernel, count), out_shape=[jax.Shap...  43.3 us
    pallas_call x1, Pallas kernels, project(): pl.pallas_call(functools.partial(project_kernel, count), in_specs=[whole]...  36.8 us
    pallas_call x1, Pallas kernels, first(): pl.pallas_call(first_kernel, out_shape=[jax.ShapeDtypeStruct((8, 128), F3...  15.2 us
    all_to_all x2, starting transfers between devices, exchanged(): return lax.all_to_all(value, axes, 0, 0, tiled=True)  12.8 us
    pallas_call x1, Pallas kernels, in_weight(): pl.pallas_call(in_weight_kernel, grid=(sources // here,), in_specs=[pl.Bl...  11.9 us
    unnamed x25, local copies, waits for them, and re-layouts  8.98 us
    ppermute x4, starting transfers between devices, swapped(): return lax.ppermute(value, axis, [(0, 1), (1, 0)])  5.08 us
  transfers between devices with their start and end apart: 7, of which 2 were waited for; matrix products, arithmetic and copies ran while one was open for 5% of the time, Pallas kernels for 64%

profile of v7, /device:TPU:1, one launch (start us, length us, event | category | flops | bytes accessed | tf_op | source)
XLA Modules:
  0.0 249.9 jit_solution(2451100254272486484)
XLA Ops:
  7.2 1.5 collective-permute-start.2
  8.8 1.2 copy.38
  10.0 1.4 collective-permute-start
  11.4 0.9 copy.37
  12.3 0.6 reshape.37.gain_ref
  12.9 0.6 reshape.38.shift_ref
  13.5 3.7 %collective-permute-done.1.other_ref = bf16[512,1280]{1,0:T(8,128)(2,1)S(1)} collective-permute-done((bf16[512,1280]{1,0:T(8,128)(2,1)}, bf16[512,1280]{1,0:T(8,128)(2,1)S(1)}, u32[]{:S(2)}, u32[]{:S(2)}) %collective-permute-start.1) | collective-permute-done | bytes 1310752 | tf_op jit(solution)/shard_map/ppermute | solution.py:663
  17.2 1.1 copy-done.2
  18.3 15.2 %shard_map.93 = (f32[8,128]{1,0:T(8,128)}, bf16[16,2,64,128]{3,2,1,0:T(8,128)(2,1)}) custom-call(bf16[2,128,1280]{2,1,0:T(8,128)(2,1)} %bitcast.28, bf16[2,128,1280]{2,1,0:T(8,128)(2,1)} %bitcast.33, bf16[512,1280]{1,0:T(8,128)(2,1)} %mine_ref.3, bf16[512,1280]{1,0:T(8,128)(2,1)} %copy-done.2), custom_call_target="tpu_custom_call" | custom-call | flops 8589934592 | bytes 6291456 | tf_op jit(solution)/shard_map/pallas_call | solution.py:235
  33.5 0.9 maximum_select_fusion
  34.4 36.8 %shard_map.94 = (f32[8,1280]{1,0:T(8,128)}, bf16[32,256,128]{2,1,0:T(8,128)(2,1)}) custom-call(bf16[2,128,1280]{2,1,0:T(8,128)(2,1)} %bitcast.29, f32[8,128]{1,0:T(8,128)} %get-tuple-element.28.sums_ref, f32[1,1280]{1,0:T(1,128)} %reshape.37.gain_ref, f32[1,1280]{1,0:T(1,128)} %reshape.38.shift_ref, bf16[16,2,64,128]{3,2,1,0:T(8,128)(2,1)} %get-tuple-element.29.g_ref, ...), custom_call_target="tpu_custom_call" | custom-call | flops 34359738368 | bytes 12582912 | tf_op jit(solution)/shard_map/pallas_call | solution.py:153
  71.3 2.1 collective-permute-start.3
  73.4 89.6 %shard_map.95 = (bf16[32,128,128]{2,1,0:T(8,128)(2,1)}, bf16[32,128,128]{2,1,0:T(8,128)(2,1)}, bf16[32,128,128]{2,1,0:T(8,128)(2,1)}) custom-call(bf16[32,256,128]{2,1,0:T(8,128)(2,1)} %get-tuple-element.31.kvq_ref), custom_call_target="tpu_custom_call" | custom-call | flops 51539607552 | bytes 4194304 | tf_op jit(solution)/shard_map/pallas_call | solution.py:378
  163.0 5.4 %all-to-all-start = ((bf16[32,128,128]{2,1,0:T(8,128)(2,1)}), bf16[32,128,128]{2,1,0:T(8,128)(2,1)}, u32[]{:S(2)}, u32[]{:S(2)}) async-start(bf16[32,128,128]{2,1,0:T(8,128)(2,1)} %get-tuple-element.36.dkv_ref), calls=%async_computation | async-start | bytes 2097152 | tf_op jit(solution)/shard_map/all_to_all | solution.py:667
  168.4 1.7 pad_maximum_fusion.halves_ref
  170.2 0.6 broadcast_select_fusion.1.chan_ref
  170.8 11.9 %shard_map.96 = bf16[128,16,128]{2,1,0:T(8,128)(2,1)} custom-call(bf16[32,128,1280]{2,1,0:T(8,128)(2,1)} %all-gather.2.cloned.1.call-done.lat_ref, f32[2,1280]{1,0:T(2,128)} %broadcast_select_fusion.1.chan_ref, f32[1,1280]{1,0:T(1,128)} %reshape.37.gain_ref, f32[1,1280]{1,0:T(1,128)} %reshape.38.shift_ref, bf16[32,128,128]{2,1,0:T(8,128)(2,1)} %get-tuple-element.35.dqo_ref, ...), custom_call_target="tpu_custom_call" | custom-call | flops 2684354560 | bytes 14680064 | tf_op jit(solution)/shard_map/pallas_call | solution.py:439
  182.7 2.3 all-to-all-done
  185.1 7.4 %all-to-all-start.1 = ((bf16[128,16,128]{2,1,0:T(8,128)(2,1)}), bf16[128,16,128]{2,1,0:T(8,128)(2,1)S(1)}, u32[]{:S(2)}, u32[]{:S(2)}) async-start(bf16[128,16,128]{2,1,0:T(8,128)(2,1)} %shard_map.96), calls=%async_computation.1 | async-start | bytes 1048576 | tf_op jit(solution)/shard_map/all_to_all | solution.py:667
  192.5 43.3 %shard_map.97 = (bf16[2,128,1280]{2,1,0:T(8,128)(2,1)}, f32[8,1280]{1,0:T(8,128)}, bf16[2,128,1280]{2,1,0:T(8,128)(2,1)}) custom-call(bf16[16,2,128,128]{3,2,1,0:T(8,128)(2,1)} %bitcast.40, bf16[16,2,128,128]{3,2,1,0:T(8,128)(2,1)} %bitcast.5.dkv_ref, bf16[640,3072]{1,0:T(8,128)(2,1)} %mine_ref.5, bf16[640,3072]{1,0:T(8,128)(2,1)} %collective-permute-done.2.other_ref, ...), custom_call_target="tpu_custom_call" | custom-call | flops 34359738368 | bytes 16777216 | tf_op jit(solution)/shard_map/pallas_call | solution.py:637
  235.9 2.6 %copy.33 = bf16[128,2,1280]{2,1,0:T(2,128)(2,1)} copy(bf16[128,2,1280]{2,0,1:T(8,128)(2,1)} %bitcast.37) | data formatting | bytes 1310720
  238.5 2.6 %copy.34 = bf16[128,2,1280]{2,1,0:T(2,128)(2,1)} copy(bf16[128,2,1280]{2,0,1:T(8,128)(2,1)} %bitcast.36) | data formatting | bytes 1310720
  241.7 0.7 pad_maximum_fusion.1
  242.4 0.6 copy.40
  (41 shorter events, 0.9 us)
Async XLA Ops:
  7.2 4.3 %copy-start.4 = (bf16[128,2,1280]{2,1,0:T(2,128)(2,1)S(1)}, bf16[128,2,1280]{2,1,0:T(2,128)(2,1)}, u32[]{:S(2)}) copy-start(bf16[128,2,1280]{2,1,0:T(2,128)(2,1)} %param.7) | copy-start | bytes 1966084
  7.2 5.2 %copy-start.8 = (f32[1280]{0:T(1024)S(1)}, f32[1280]{0:T(1024)}, u32[]{:S(2)}) copy-start(f32[1280]{0:T(1024)} %param.8) | copy-start | bytes 15364
  7.2 5.8 %copy-start.9 = (f32[1280]{0:T(1024)S(1)}, f32[1280]{0:T(1024)}, u32[]{:S(2)}) copy-start(f32[1280]{0:T(1024)} %param.9) | copy-start | bytes 15364
  7.2 163.6 %all-gather.2.cloned.1.call-start = ((), (), s32[]{:S(2)}) async-start(), calls=%async_computation.2 | async-start | bytes 11141120 | tf_op jit(solution)/shard_map/all_gather | solution.py:691
  7.2 27.2 %collective-permute-start.2 = (bf16[640,3072]{1,0:T(8,128)(2,1)}, bf16[640,3072]{1,0:T(8,128)(2,1)}, u32[]{:S(2)}, u32[]{:S(2)}) collective-permute-start(bf16[640,3072]{1,0:T(8,128)(2,1)} %mine_ref.5), channel_id=1, source_target_pairs={{0,1},{1,0},{2,3},{3,2},{4,5},{5,4},{6,7},{7,6},{8,9},{9,8},{10,11... | collective-permute-start | bytes 11796488 | tf_op jit(solution)/shard_map/ppermute | solution.py:663
  8.7 8.5 %collective-permute-start.1 = (bf16[512,1280]{1,0:T(8,128)(2,1)}, bf16[512,1280]{1,0:T(8,128)(2,1)S(1)}, u32[]{:S(2)}, u32[]{:S(2)}) collective-permute-start(bf16[512,1280]{1,0:T(8,128)(2,1)} %mine_ref.3), channel_id=1, source_target_pairs={{0,1},{1,0},{2,3},{3,2},{4,5},{5,4},{6,7},{7,6},{8,9},{9,8},{10,11... | collective-permute-start | bytes 3932168 | tf_op jit(solution)/shard_map/ppermute | solution.py:663
  10.0 7.2 %copy-start = (bf16[128,2,1280]{2,0,1:T(8,128)(2,1)}, bf16[128,2,1280]{2,0,1:T(8,128)(2,1)S(1)}, u32[]{:S(2)}) copy-start(bf16[128,2,1280]{2,0,1:T(8,128)(2,1)S(1)} %copy.38) | copy-start | bytes 1966084
  10.0 23.4 %collective-permute-start = (bf16[128,1280]{1,0:T(8,128)(2,1)S(1)}, bf16[128,1280]{1,0:T(8,128)(2,1)S(1)}, u32[]{:S(2)}, u32[]{:S(2)}) collective-permute-start(bf16[128,1280]{1,0:T(8,128)(2,1)S(1)} %get-tuple-element.61), channel_id=1, source_target_pairs={{0,4},{4,0},{1,5},{5,1},{2,6},{6,2},{3,7},{7,3},{8,12},{12,8},{9,1... | collective-permute-start | bytes 983048 | tf_op jit(solution)/shard_map/ppermute | solution.py:663
  17.2 1.1 copy-start.2
  34.4 36.9 %copy-start.5 = (bf16[128,2,1280]{2,0,1:T(8,128)(2,1)S(1)}, bf16[128,2,1280]{2,0,1:T(8,128)(2,1)}, u32[]{:S(2)}) copy-start(bf16[128,2,1280]{2,0,1:T(8,128)(2,1)} %copy.37) | copy-start | bytes 1966084
  71.3 121.2 %collective-permute-start.3 = (bf16[2,128,1280]{2,1,0:T(8,128)(2,1)S(1)}, bf16[2,128,1280]{2,1,0:T(8,128)(2,1)}, u32[]{:S(2)}, u32[]{:S(2)}) collective-permute-start(bf16[2,128,1280]{2,1,0:T(8,128)(2,1)S(1)} %bitcast.35), channel_id=1, source_target_pairs={{0,1},{1,0},{2,3},{3,2},{4,5},{5,4},{6,7},{7,6},{8,9},{9,8},{10,11... | collective-permute-start | bytes 1966088 | tf_op jit(solution)/shard_map/ppermute | solution.py:663
  73.4 95.0 %copy-start.3 = (bf16[512,1280]{1,0:T(8,128)(2,1)S(1)}, bf16[512,1280]{1,0:T(8,128)(2,1)}, u32[]{:S(2)}) copy-start(bf16[512,1280]{1,0:T(8,128)(2,1)} %copy-done.2) | copy-start | bytes 3932164
  163.0 5.4 %copy-start.1 = (bf16[512,1280]{1,0:T(8,128)(2,1)S(1)}, bf16[512,1280]{1,0:T(8,128)(2,1)}, u32[]{:S(2)}) copy-start(bf16[512,1280]{1,0:T(8,128)(2,1)} %mine_ref.3) | copy-start | bytes 3932164
  163.0 22.0 %all-to-all-start = ((bf16[32,128,128]{2,1,0:T(8,128)(2,1)}), bf16[32,128,128]{2,1,0:T(8,128)(2,1)}, u32[]{:S(2)}, u32[]{:S(2)}) async-start(bf16[32,128,128]{2,1,0:T(8,128)(2,1)} %get-tuple-element.36.dkv_ref), calls=%async_computation | async-start | bytes 2097152 | tf_op jit(solution)/shard_map/all_to_all | solution.py:667
  168.4 1.7 copy-start.7
  185.1 56.0 %all-to-all-start.1 = ((bf16[128,16,128]{2,1,0:T(8,128)(2,1)}), bf16[128,16,128]{2,1,0:T(8,128)(2,1)S(1)}, u32[]{:S(2)}, u32[]{:S(2)}) async-start(bf16[128,16,128]{2,1,0:T(8,128)(2,1)} %shard_map.96), calls=%async_computation.1 | async-start | bytes 1048576 | tf_op jit(solution)/shard_map/all_to_all | solution.py:667
  235.9 6.6 %copy-start.6 = (f32[8,1280]{1,0:T(8,128)S(1)}, f32[8,1280]{1,0:T(8,128)}, u32[]{:S(2)}) copy-start(f32[8,1280]{1,0:T(8,128)} %get-tuple-element.71) | copy-start | bytes 122884
Sparse Core Ops, SparseCore 0:
  71.4 92.7 all-gather.1

commit v8 on v7

--- a/solution.py
+++ b/solution.py
@@ -547,7 +547,7 @@
     swap.wait()
     channels = cot_ref.shape[2]
     cot, cot_far = cot_ref[...].reshape(256, channels), cot_far_ref[...].reshape(256, channels)
-    for j in range(4):
+    def tile(j):
         row = (here[0] + (j + 1)) % 4
         at = pl.ds(pl.multiple_of(row * 256, 256), 256)
         total = lax.dot_general(att_ref[:, at], cot, (((0,), (0,)), ((), ())), preferred_element_type=F32)
@@ -561,6 +561,8 @@
         def _(k):
             part_copy(((j + 1) % 4) * 8 + k).start()
 
+    tile(0)
+    tile(1)
     for h in range(0, HEADS, 2):
         for i in range(2):
             rows, at = slice(i * 128, (i + 1) * 128), h * HEAD
@@ -590,6 +592,8 @@
     def _(k):
         sums_copy(k).start()
 
+    tile(2)
+    tile(3)
     got_ref[pair(line)] = part_ref[pair(line)]
 
     @pl.loop(1, seqs)

time: 251 us -> 251 us (level)
  no operation moved by 1% of the time
where the time goes in v8:
time: 251 us
  Pallas kernels  197 us (78%)
  starting transfers between devices  17.9 us (7%)
  between operations  14.3 us (6%)
  local copies, waits for them, and re-layouts  10.8 us (4%)
  waiting for transfers between devices  6.03 us (2%)
  other arithmetic  4.06 us (2%)
    pallas_call x1, Pallas kernels, attention(): pl.pallas_call(functools.partial(attention_kernel, ck), grid=(sources //...  89.6 us
    pallas_call x1, Pallas kernels, tail(): pl.pallas_call(functools.partial(tail_kernel, count), out_shape=[jax.Shap...  43.9 us
    pallas_call x1, Pallas kernels, project(): pl.pallas_call(functools.partial(project_kernel, count), in_specs=[whole]...  36.8 us
    pallas_call x1, Pallas kernels, first(): pl.pallas_call(first_kernel, out_shape=[jax.ShapeDtypeStruct((8, 128), F3...  15.2 us
    all_to_all x2, starting transfers between devices, exchanged(): return lax.all_to_all(value, axes, 0, 0, tiled=True)  12.8 us
    pallas_call x1, Pallas kernels, in_weight(): pl.pallas_call(in_weight_kernel, grid=(sources // here,), in_specs=[pl.Bl...  11.9 us
    unnamed x25, local copies, waits for them, and re-layouts  8.98 us
    ppermute x4, starting transfers between devices, swapped(): return lax.ppermute(value, axis, [(0, 1), (1, 0)])  5.08 us
  transfers between devices with their start and end apart: 7, of which 2 were waited for; matrix products, arithmetic and copies ran while one was open for 5% of the time, Pallas kernels for 64%

profile of v8, /device:TPU:1, one launch (start us, length us, event | category | flops | bytes accessed | tf_op | source)
XLA Modules:
  0.0 250.5 jit_solution(11710669627493864725)
XLA Ops:
  7.2 1.5 collective-permute-start.2
  8.8 1.2 copy.38
  10.0 1.4 collective-permute-start
  11.4 0.9 copy.37
  12.3 0.6 reshape.37.gain_ref
  12.9 0.6 reshape.38.shift_ref
  13.5 3.7 %collective-permute-done.1.other_ref = bf16[512,1280]{1,0:T(8,128)(2,1)S(1)} collective-permute-done((bf16[512,1280]{1,0:T(8,128)(2,1)}, bf16[512,1280]{1,0:T(8,128)(2,1)S(1)}, u32[]{:S(2)}, u32[]{:S(2)}) %collective-permute-start.1) | collective-permute-done | bytes 1310752 | tf_op jit(solution)/shard_map/ppermute | solution.py:667
  17.2 1.1 copy-done.2
  18.3 15.2 %shard_map.93 = (f32[8,128]{1,0:T(8,128)}, bf16[16,2,64,128]{3,2,1,0:T(8,128)(2,1)}) custom-call(bf16[2,128,1280]{2,1,0:T(8,128)(2,1)} %bitcast.28, bf16[2,128,1280]{2,1,0:T(8,128)(2,1)} %bitcast.33, bf16[512,1280]{1,0:T(8,128)(2,1)} %mine_ref.3, bf16[512,1280]{1,0:T(8,128)(2,1)} %copy-done.2), custom_call_target="tpu_custom_call" | custom-call | flops 8589934592 | bytes 6291456 | tf_op jit(solution)/shard_map/pallas_call | solution.py:235
  33.5 0.9 maximum_select_fusion
  34.4 36.8 %shard_map.94 = (f32[8,1280]{1,0:T(8,128)}, bf16[32,256,128]{2,1,0:T(8,128)(2,1)}) custom-call(bf16[2,128,1280]{2,1,0:T(8,128)(2,1)} %bitcast.29, f32[8,128]{1,0:T(8,128)} %get-tuple-element.28.sums_ref, f32[1,1280]{1,0:T(1,128)} %reshape.37.gain_ref, f32[1,1280]{1,0:T(1,128)} %reshape.38.shift_ref, bf16[16,2,64,128]{3,2,1,0:T(8,128)(2,1)} %get-tuple-element.29.g_ref, ...), custom_call_target="tpu_custom_call" | custom-call | flops 34359738368 | bytes 12582912 | tf_op jit(solution)/shard_map/pallas_call | solution.py:153
  71.3 2.1 collective-permute-start.3
  73.4 89.6 %shard_map.95 = (bf16[32,128,128]{2,1,0:T(8,128)(2,1)}, bf16[32,128,128]{2,1,0:T(8,128)(2,1)}, bf16[32,128,128]{2,1,0:T(8,128)(2,1)}) custom-call(bf16[32,256,128]{2,1,0:T(8,128)(2,1)} %get-tuple-element.31.kvq_ref), custom_call_target="tpu_custom_call" | custom-call | flops 51539607552 | bytes 4194304 | tf_op jit(solution)/shard_map/pallas_call | solution.py:378
  163.0 5.4 %all-to-all-start = ((bf16[32,128,128]{2,1,0:T(8,128)(2,1)}), bf16[32,128,128]{2,1,0:T(8,128)(2,1)}, u32[]{:S(2)}, u32[]{:S(2)}) async-start(bf16[32,128,128]{2,1,0:T(8,128)(2,1)} %get-tuple-element.36.dkv_ref), calls=%async_computation | async-start | bytes 2097152 | tf_op jit(solution)/shard_map/all_to_all | solution.py:671
  168.4 1.7 pad_maximum_fusion.halves_ref
  170.2 0.6 broadcast_select_fusion.1.chan_ref
  170.8 11.9 %shard_map.96 = bf16[128,16,128]{2,1,0:T(8,128)(2,1)} custom-call(bf16[32,128,1280]{2,1,0:T(8,128)(2,1)} %all-gather.2.cloned.1.call-done.lat_ref, f32[2,1280]{1,0:T(2,128)} %broadcast_select_fusion.1.chan_ref, f32[1,1280]{1,0:T(1,128)} %reshape.37.gain_ref, f32[1,1280]{1,0:T(1,128)} %reshape.38.shift_ref, bf16[32,128,128]{2,1,0:T(8,128)(2,1)} %get-tuple-element.35.dqo_ref, ...), custom_call_target="tpu_custom_call" | custom-call | flops 2684354560 | bytes 14680064 | tf_op jit(solution)/shard_map/pallas_call | solution.py:439
  182.7 2.3 all-to-all-done
  185.1 7.4 %all-to-all-start.1 = ((bf16[128,16,128]{2,1,0:T(8,128)(2,1)}), bf16[128,16,128]{2,1,0:T(8,128)(2,1)S(1)}, u32[]{:S(2)}, u32[]{:S(2)}) async-start(bf16[128,16,128]{2,1,0:T(8,128)(2,1)} %shard_map.96), calls=%async_computation.1 | async-start | bytes 1048576 | tf_op jit(solution)/shard_map/all_to_all | solution.py:671
  192.5 43.9 %shard_map.97 = (bf16[2,128,1280]{2,1,0:T(8,128)(2,1)}, f32[8,1280]{1,0:T(8,128)}, bf16[2,128,1280]{2,1,0:T(8,128)(2,1)}) custom-call(bf16[16,2,128,128]{3,2,1,0:T(8,128)(2,1)} %bitcast.40, bf16[16,2,128,128]{3,2,1,0:T(8,128)(2,1)} %bitcast.5.dkv_ref, bf16[640,3072]{1,0:T(8,128)(2,1)} %mine_ref.5, bf16[640,3072]{1,0:T(8,128)(2,1)} %collective-permute-done.2.other_ref, ...), custom_call_target="tpu_custom_call" | custom-call | flops 34359738368 | bytes 16777216 | tf_op jit(solution)/shard_map/pallas_call | solution.py:641
  236.5 2.6 %copy.33 = bf16[128,2,1280]{2,1,0:T(2,128)(2,1)} copy(bf16[128,2,1280]{2,0,1:T(8,128)(2,1)} %bitcast.37) | data formatting | bytes 1310720
  239.1 2.6 %copy.34 = bf16[128,2,1280]{2,1,0:T(2,128)(2,1)} copy(bf16[128,2,1280]{2,0,1:T(8,128)(2,1)} %bitcast.36) | data formatting | bytes 1310720
  242.4 0.7 pad_maximum_fusion.1
  243.1 0.6 copy.40
  (41 shorter events, 0.9 us)
Async XLA Ops:
  7.2 4.3 %copy-start.4 = (bf16[128,2,1280]{2,1,0:T(2,128)(2,1)S(1)}, bf16[128,2,1280]{2,1,0:T(2,128)(2,1)}, u32[]{:S(2)}) copy-start(bf16[128,2,1280]{2,1,0:T(2,128)(2,1)} %param.7) | copy-start | bytes 1966084
  7.2 5.2 %copy-start.8 = (f32[1280]{0:T(1024)S(1)}, f32[1280]{0:T(1024)}, u32[]{:S(2)}) copy-start(f32[1280]{0:T(1024)} %param.8) | copy-start | bytes 15364
  7.2 5.8 %copy-start.9 = (f32[1280]{0:T(1024)S(1)}, f32[1280]{0:T(1024)}, u32[]{:S(2)}) copy-start(f32[1280]{0:T(1024)} %param.9) | copy-start | bytes 15364
  7.2 163.6 %all-gather.2.cloned.1.call-start = ((), (), s32[]{:S(2)}) async-start(), calls=%async_computation.2 | async-start | bytes 11141120 | tf_op jit(solution)/shard_map/all_gather | solution.py:695
  7.2 27.2 %collective-permute-start.2 = (bf16[640,3072]{1,0:T(8,128)(2,1)}, bf16[640,3072]{1,0:T(8,128)(2,1)}, u32[]{:S(2)}, u32[]{:S(2)}) collective-permute-start(bf16[640,3072]{1,0:T(8,128)(2,1)} %mine_ref.5), channel_id=1, source_target_pairs={{0,1},{1,0},{2,3},{3,2},{4,5},{5,4},{6,7},{7,6},{8,9},{9,8},{10,11... | collective-permute-start | bytes 11796488 | tf_op jit(solution)/shard_map/ppermute | solution.py:667
  8.7 8.5 %collective-permute-start.1 = (bf16[512,1280]{1,0:T(8,128)(2,1)}, bf16[512,1280]{1,0:T(8,128)(2,1)S(1)}, u32[]{:S(2)}, u32[]{:S(2)}) collective-permute-start(bf16[512,1280]{1,0:T(8,128)(2,1)} %mine_ref.3), channel_id=1, source_target_pairs={{0,1},{1,0},{2,3},{3,2},{4,5},{5,4},{6,7},{7,6},{8,9},{9,8},{10,11... | collective-permute-start | bytes 3932168 | tf_op jit(solution)/shard_map/ppermute | solution.py:667
  10.0 7.2 %copy-start = (bf16[128,2,1280]{2,0,1:T(8,128)(2,1)}, bf16[128,2,1280]{2,0,1:T(8,128)(2,1)S(1)}, u32[]{:S(2)}) copy-start(bf16[128,2,1280]{2,0,1:T(8,128)(2,1)S(1)} %copy.38) | copy-start | bytes 1966084
  10.0 23.4 %collective-permute-start = (bf16[128,1280]{1,0:T(8,128)(2,1)S(1)}, bf16[128,1280]{1,0:T(8,128)(2,1)S(1)}, u32[]{:S(2)}, u32[]{:S(2)}) collective-permute-start(bf16[128,1280]{1,0:T(8,128)(2,1)S(1)} %get-tuple-element.61), channel_id=1, source_target_pairs={{0,4},{4,0},{1,5},{5,1},{2,6},{6,2},{3,7},{7,3},{8,12},{12,8},{9,1... | collective-permute-start | bytes 983048 | tf_op jit(solution)/shard_map/ppermute | solution.py:667
  17.2 1.1 copy-start.2
  34.4 36.9 %copy-start.5 = (bf16[128,2,1280]{2,0,1:T(8,128)(2,1)S(1)}, bf16[128,2,1280]{2,0,1:T(8,128)(2,1)}, u32[]{:S(2)}) copy-start(bf16[128,2,1280]{2,0,1:T(8,128)(2,1)} %copy.37) | copy-start | bytes 1966084
  71.3 121.2 %collective-permute-start.3 = (bf16[2,128,1280]{2,1,0:T(8,128)(2,1)S(1)}, bf16[2,128,1280]{2,1,0:T(8,128)(2,1)}, u32[]{:S(2)}, u32[]{:S(2)}) collective-permute-start(bf16[2,128,1280]{2,1,0:T(8,128)(2,1)S(1)} %bitcast.35), channel_id=1, source_target_pairs={{0,1},{1,0},{2,3},{3,2},{4,5},{5,4},{6,7},{7,6},{8,9},{9,8},{10,11... | collective-permute-start | bytes 1966088 | tf_op jit(solution)/shard_map/ppermute | solution.py:667
  73.4 95.0 %copy-start.3 = (bf16[512,1280]{1,0:T(8,128)(2,1)S(1)}, bf16[512,1280]{1,0:T(8,128)(2,1)}, u32[]{:S(2)}) copy-start(bf16[512,1280]{1,0:T(8,128)(2,1)} %copy-done.2) | copy-start | bytes 3932164
  163.0 5.4 %copy-start.1 = (bf16[512,1280]{1,0:T(8,128)(2,1)S(1)}, bf16[512,1280]{1,0:T(8,128)(2,1)}, u32[]{:S(2)}) copy-start(bf16[512,1280]{1,0:T(8,128)(2,1)} %mine_ref.3) | copy-start | bytes 3932164
  163.0 22.0 %all-to-all-start = ((bf16[32,128,128]{2,1,0:T(8,128)(2,1)}), bf16[32,128,128]{2,1,0:T(8,128)(2,1)}, u32[]{:S(2)}, u32[]{:S(2)}) async-start(bf16[32,128,128]{2,1,0:T(8,128)(2,1)} %get-tuple-element.36.dkv_ref), calls=%async_computation | async-start | bytes 2097152 | tf_op jit(solution)/shard_map/all_to_all | solution.py:671
  168.4 1.7 copy-start.7
  185.1 56.6 %all-to-all-start.1 = ((bf16[128,16,128]{2,1,0:T(8,128)(2,1)}), bf16[128,16,128]{2,1,0:T(8,128)(2,1)S(1)}, u32[]{:S(2)}, u32[]{:S(2)}) async-start(bf16[128,16,128]{2,1,0:T(8,128)(2,1)} %shard_map.96), calls=%async_computation.1 | async-start | bytes 1048576 | tf_op jit(solution)/shard_map/all_to_all | solution.py:671
  236.5 6.6 %copy-start.6 = (f32[8,1280]{1,0:T(8,128)S(1)}, f32[8,1280]{1,0:T(8,128)}, u32[]{:S(2)}) copy-start(f32[8,1280]{1,0:T(8,128)} %get-tuple-element.71) | copy-start | bytes 122884
Sparse Core Ops, SparseCore 0:
  71.4 92.7 all-gather.1
